TPU v7x, 512 devices: a whole 4x8x8 slice. The times are simulated.
512 devices in a mesh: chain: 8 (over y), rows: 32 (over x, z), clip: 2 (over core).
Axes of the slice: x: 4, y: 8, z: 8, core: 2. Of those that a mesh axis runs over, the one named last changes fastest.
Arguments:
- video: bfloat16 [2, 16, 64, 48, 384], P('clip', 'chain', 'rows'), may hold values from -6 to 6
- cotangent: bfloat16 [2, 32, 128, 96, 192], P('clip', 'chain', 'rows'), may hold values from -6 to 6
- w_time: bfloat16 [3, 384, 768], replicated, may hold values from -0.1875 to 0.1875
- w_space: bfloat16 [3, 3, 384, 192], replicated, may hold values from -0.109375 to 0.109375
Outputs:
- grad_video: bfloat16 [2, 16, 64, 48, 384], P('clip', 'chain', 'rows')
- grad_time: bfloat16 [1152, 768], P('rows')
- grad_space: bfloat16 [3456, 192], P('rows')
All inputs are finite; a program needn't handle non-finite values.
Results may differ from a plain program's by a relative error of at most 0.025.
Values may be sent and summed in bfloat16 or wider, within the bound.
No kernel may reach another device: no remote copies, remote signals or barrier semaphores. Data moves between devices by JAX's collectives and lax.ppermute only.
A program may use at most 64 MiB of HBM per device.

v0:
```python
import math

import jax
import jax.numpy as jnp
from jax import lax
from jax.sharding import PartitionSpec as P


def shifted_2(value, axis, steps):
    count = lax.axis_size(axis)
    leading, last = (max(0, -steps), min(count, count - steps))
    return lax.ppermute(value, axis, [(source, source + steps) for source in range(leading, last)])


def extended_2(block, sides, width):
    for axis, dim in sides:
        count = lax.axis_size(axis)
        forward = [(i, i + 1) for i in range(count - 1)]
        backward = [(target, source) for source, target in forward]
        low = lax.ppermute(
            lax.slice_in_dim(block, block.shape[dim] - width, None, axis=dim), axis, forward
        )
        high = lax.ppermute(lax.slice_in_dim(block, 0, width, axis=dim), axis, backward)
        block = jnp.concatenate([low, block, high], axis=dim)
    return block


def time_conv(extended, w_time, frames):
    channels = extended.shape[-1]
    summed_taps = jnp.zeros(
        (frames * extended.shape[1] * extended.shape[2], w_time.shape[2]), jnp.float32
    )
    for tap_t in range(3):
        summed_taps = summed_taps + jnp.dot(
            extended[tap_t : tap_t + frames].reshape(-1, channels),
            w_time[tap_t],
            preferred_element_type=jnp.float32,
        )
    return summed_taps.astype(jnp.bfloat16).reshape(
        frames, extended.shape[1], extended.shape[2], w_time.shape[2]
    )


def backward_block(hidden, own_input, padded_cot, w_time, w_space):
    frames, rows_ext, columns, doubled = hidden.shape
    band_rows = rows_ext - 2
    channels = doubled // 2
    half_ch = w_space.shape[3]
    upsampled = (
        hidden.reshape(frames, rows_ext, columns, 2, channels)
        .transpose(0, 3, 1, 2, 4)
        .reshape(2 * frames, rows_ext, columns, channels)
    )
    upsampled = jnp.repeat(jnp.repeat(upsampled, 2, axis=1), 2, axis=2)[:, 1 : 2 * band_rows + 3]
    upsampled = jnp.pad(upsampled, ((0, 0), (0, 0), (1, 1), (0, 0)))
    cot_core = padded_cot[:, 1 : 2 * band_rows + 1, 1 : 2 * columns + 1].reshape(-1, half_ch)
    space_terms = []
    grad_up = jnp.zeros((8 * frames * band_rows * columns, channels), jnp.float32)
    for tap_r in range(3):
        for tap_c in range(3):
            window = upsampled[
                :, tap_r : tap_r + 2 * band_rows, tap_c : tap_c + 2 * columns
            ].reshape(-1, channels)
            space_terms.append(jnp.dot(window.T, cot_core, preferred_element_type=jnp.float32))
            shifted = padded_cot[
                :, 2 - tap_r : 2 - tap_r + 2 * band_rows, 2 - tap_c : 2 - tap_c + 2 * columns
            ].reshape(-1, half_ch)
            grad_up = grad_up + jnp.dot(
                shifted, w_space[tap_r, tap_c].T, preferred_element_type=jnp.float32
            )
    part_space = jnp.stack(space_terms).reshape(9 * channels, half_ch)
    summed = grad_up.reshape(2 * frames, band_rows, 2, columns, 2, channels).sum(axis=(2, 4))
    grad_hidden = (
        summed.reshape(frames, 2, band_rows, columns, channels)
        .transpose(0, 2, 3, 1, 4)
        .reshape(frames * band_rows * columns, 2 * channels)
        .astype(jnp.bfloat16)
    )
    time_terms = []
    for tap_t in range(3):
        time_terms.append(
            jnp.dot(
                own_input[tap_t : tap_t + frames].reshape(-1, channels).T,
                grad_hidden,
                preferred_element_type=jnp.float32,
            )
        )
    part_time = jnp.stack(time_terms).reshape(3 * channels, 2 * channels)
    grad_ext = jnp.zeros((frames + 2, band_rows, columns, channels), jnp.float32)
    for tap_t in range(3):
        grad_ext = grad_ext.at[tap_t : tap_t + frames].add(
            jnp.dot(grad_hidden, w_time[tap_t].T, preferred_element_type=jnp.float32).reshape(
                frames, band_rows, columns, channels
            )
        )
    return (part_time, part_space, grad_ext)


def local(video, cotangent, w_time, w_space):
    own_video = video[0]
    frames, band_rows, columns, channels = own_video.shape
    carried = shifted_2(own_video, "chain", 1)
    extended = jnp.concatenate([carried, own_video], 0)
    hidden = extended_2(time_conv(extended, w_time, frames), (("rows", 1),), 1)
    cot_rimmed = extended_2(cotangent[0], (("rows", 1),), 1)
    padded_cot = jnp.pad(cot_rimmed, ((0, 0), (0, 0), (1, 1), (0, 0)))
    part_time, part_space, grad_ext = backward_block(hidden, extended, padded_cot, w_time, w_space)
    returned = shifted_2(grad_ext[:2], "chain", -1)
    grad_video = grad_ext[2:].at[frames - 2 :].add(returned).astype(jnp.bfloat16)[None]
    band_time, band_space = (
        lax.psum_scatter(
            part_time.astype(jnp.bfloat16), "rows", scatter_dimension=0, tiled=True
        ).astype(jnp.float32),
        lax.psum_scatter(
            part_space.astype(jnp.bfloat16), "rows", scatter_dimension=0, tiled=True
        ).astype(jnp.float32),
    )
    total_time, total_space = lax.psum((band_time, band_space), ("chain", "clip"))
    voxels = (
        lax.axis_size("clip")
        * 2
        * frames
        * lax.axis_size("chain")
        * 2
        * band_rows
        * lax.axis_size("rows")
        * 2
        * columns
    )
    grad_scale = 1.0 / math.sqrt(voxels)
    return (
        grad_video,
        (total_time * grad_scale).astype(jnp.bfloat16),
        (total_space * grad_scale).astype(jnp.bfloat16),
    )


def solution(mesh):
    placed = (
        P("clip", "chain", "rows", None, None),
        P("clip", "chain", "rows", None, None),
        P(),
        P(),
    )
    return jax.shard_map(
        local,
        mesh=mesh,
        in_specs=placed,
        out_specs=(P("clip", "chain", "rows", None, None), P("rows", None), P("rows", None)),
        check_vma=False,
    )
```

profile of v0, /device:TPU:1, one launch (start us, length us, event | category | flops | bytes accessed | tf_op | source)
XLA Modules:
  0.0 323.5 jit_solution(4748114858809368487)
XLA Ops:
  7.2 1.1 fusion.169
  8.3 1.3 collective-permute-start.1
  9.6 5.5 %collective-permute-start = (bf16[4,1,96,192]{3,2,1,0:T(8,128)(2,1)S(1)}, bf16[4,1,96,192]{3,2,1,0:T(8,128)(2,1)S(1)}, u32[]{:S(2)}, u32[]{:S(2)}) collective-permute-start(bf16[4,1,96,192]{3,2,1,0:T(8,128)(2,1)S(1)} %get-tuple-element.82), channel_id=1, source_target_pairs={{0,2},{2,4},{4,6},{6,8},{8,10},{10,12},{12,14},{14,16},{16,18},{18... | collective-permute-start | bytes 442376 | tf_op jit(solution)/shard_map/ppermute | solution.py:20
  15.1 3.9 %collective-permute-start.3 = (bf16[2,2,48,384]{3,2,1,0:T(8,128)(2,1)}, bf16[2,2,48,384]{3,2,1,0:T(8,128)(2,1)}, u32[]{:S(2)}, u32[]{:S(2)}) collective-permute-start(bf16[2,2,48,384]{3,2,1,0:T(8,128)(2,1)} %bitcast.293), channel_id=1, source_target_pairs={{0,64},{64,128},{128,192},{192,256},{256,320},{320,384},{384,448},... | collective-permute-start | bytes 442376 | tf_op jit(solution)/shard_map/ppermute | solution.py:12
  19.0 2.3 fusion.121
  21.3 0.5 fusion.8
  21.8 1.0 fusion.168
  22.8 0.3 copy-done.7
  23.2 0.6 fusion.132
  23.7 0.6 fusion.141
  24.5 0.6 convolution_add_fusion.6
  25.1 0.6 convolution_add_fusion.5
  25.7 0.6 convolution_add_fusion.4
  26.3 0.6 convolution_add_fusion.3
  26.8 0.6 convolution_add_fusion.2
  27.4 0.6 convolution_add_fusion.1
  28.0 1.9 fusion.2
  29.9 3.0 reshape.239
  32.9 2.0 reduce_sum.9
  35.2 1.6 fusion.11
  36.8 0.9 pad_maximum_fusion.5
  37.7 0.4 fusion.10
  38.1 0.3 fusion.123
  38.4 1.0 copy.74
  39.4 0.4 fusion.119
  39.9 0.4 fusion.26
  40.3 0.8 copy-done.3
  41.1 0.8 slice.289
  41.8 1.5 collective-permute-start.2
  43.3 1.3 fusion.9
  44.6 1.2 fusion.13
  45.9 1.3 collective-permute-start.5
  47.2 4.6 %collective-permute-start.4 = (bf16[2,1,48,768]{3,2,1,0:T(8,128)(2,1)S(1)}, bf16[2,1,48,768]{3,2,1,0:T(8,128)(2,1)S(1)}, u32[]{:S(2)}, u32[]{:S(2)}) collective-permute-start(bf16[2,1,48,768]{3,2,1,0:T(8,128)(2,1)S(1)} %get-tuple-element.86), channel_id=1, source_target_pairs={{0,2},{2,4},{4,6},{6,8},{8,10},{10,12},{12,14},{14,16},{16,18},{18... | collective-permute-start | bytes 442376 | tf_op jit(solution)/shard_map/ppermute | solution.py:20
  51.8 1.4 pad_maximum_fusion
  53.2 0.7 collective-permute-done.4
  54.2 3.0 broadcast_in_dim.12
  57.2 5.0 %reshape.245 = bf16[4,8,96,384]{3,2,1,0:T(8,128)(2,1)S(1)} reshape(bf16[4,8,48,2,384]{4,3,2,1,0:T(2,128)(2,1)} %broadcast_in_dim.12) | data formatting | bytes 4718592 | tf_op jit(solution)/shard_map/reshape | solution.py:54
  62.5 1.2 fusion.77
  63.7 1.2 fusion.115
  64.9 1.2 fusion.83
  66.1 1.2 fusion.89
  67.3 1.2 fusion.113
  68.5 1.2 fusion.95
  69.7 1.2 fusion.101
  70.9 1.2 fusion.111
  72.1 1.2 fusion.107
  73.4 3.8 %copy.51 = bf16[9,384,192]{2,1,0:T(8,128)(2,1)} copy(bf16[9,384,192]{1,2,0:T(8,128)(2,1)} %fusion.107) | data formatting | bytes 2654208 | tf_op jit(solution)/shard_map/stack | solution.py:71
  77.1 86.0 %fusion.167 = (bf16[40,768]{1,0:T(8,128)(2,1)S(1)}, bf16[112,192]{1,0:T(8,128)(2,1)S(1)}) fusion(bf16[1152,768]{1,0:T(8,128)(2,1)S(1)} %bitcast.271, bf16[3456,192]{1,0:T(8,128)(2,1)} %bitcast.272), kind=kCustom, calls=%all-reduce-scatter.2 | all-reduce-scatter fusion | flops 1671170 | bytes 3203072
  163.1 1.3 collective-permute-start.10
  164.4 1.3 collective-permute-start.11
  165.7 1.3 dynamic-slice.31
  167.7 1.3 collective-permute-start.8
  169.0 4.8 %collective-permute-start.7 = (bf16[40,768]{1,0:T(8,128)(2,1)S(1)}, bf16[40,768]{1,0:T(8,128)(2,1)S(1)}, u32[]{:S(2)}, u32[]{:S(2)}) collective-permute-start(bf16[40,768]{1,0:T(8,128)(2,1)S(1)} %get-tuple-element.72), channel_id=1, source_target_pairs={{0,4},{2,6},{4,8},{6,10},{8,12},{10,14},{12,16},{14,18},{16,20},{1... | collective-permute-start | bytes 184328
  173.8 1.9 collective-permute-start.6
  175.7 1.9 collective-permute-start.9
  177.6 0.5 concatenate.33
  178.1 0.7 dynamic-slice_convert_fusion.1
  178.8 0.7 concatenate.32
  179.5 0.7 dynamic-slice_convert_fusion
  180.2 2.2 fusion.116
  182.4 131.1 %all-reduce.11.cloned.1.call-done = (f32[36,768]{1,0:T(8,128)}, f32[108,192]{1,0:T(8,128)}) async-done(((f32[36,768]{1,0:T(8,128)}, f32[108,192]{1,0:T(8,128)}), (f32[36,768]{1,0:T(8,128)}, f32[108,192]{1,0:T(8,128)})) %all-reduce.11.cloned.1.call-update) | async-done | bytes 193552 | tf_op jit(solution)/shard_map/psum | solution.py:118
  313.5 1.5 multiply_convert_fusion
  315.0 0.9 multiply_convert_fusion.1
  315.9 0.7 copy.52
  (41 shorter events, 1.2 us)
Async XLA Ops:
  7.2 14.1 %copy-start = (bf16[1,4,4,96,192]{4,3,2,1,0:T(8,128)(2,1)S(1)}, bf16[1,4,4,96,192]{4,3,2,1,0:T(8,128)(2,1)}, u32[]{:S(2)}) copy-start(bf16[1,4,4,96,192]{4,3,2,1,0:T(8,128)(2,1)} %param.15) | copy-start | bytes 1769476
  7.2 306.3 %all-reduce.11.cloned.1.call-start = ((), (), s32[]{:S(2)}) async-start(), calls=%async_computation | async-start | bytes 475136 | tf_op jit(solution)/shard_map/psum | solution.py:118
  8.3 12.9 %collective-permute-start.1 = (bf16[4,1,96,192]{3,2,1,0:T(8,128)(2,1)S(1)}, bf16[4,1,96,192]{3,2,1,0:T(8,128)(2,1)S(1)}, u32[]{:S(2)}, u32[]{:S(2)}) collective-permute-start(bf16[4,1,96,192]{3,2,1,0:T(8,128)(2,1)S(1)} %get-tuple-element.83), channel_id=1, source_target_pairs={{2,0},{4,2},{6,4},{8,6},{10,8},{12,10},{14,12},{16,14},{18,16},{20... | collective-permute-start | bytes 442376 | tf_op jit(solution)/shard_map/ppermute | solution.py:23
  9.6 11.6 %collective-permute-start = (bf16[4,1,96,192]{3,2,1,0:T(8,128)(2,1)S(1)}, bf16[4,1,96,192]{3,2,1,0:T(8,128)(2,1)S(1)}, u32[]{:S(2)}, u32[]{:S(2)}) collective-permute-start(bf16[4,1,96,192]{3,2,1,0:T(8,128)(2,1)S(1)} %get-tuple-element.82), channel_id=1, source_target_pairs={{0,2},{2,4},{4,6},{6,8},{8,10},{10,12},{12,14},{14,16},{16,18},{18... | collective-permute-start | bytes 442376 | tf_op jit(solution)/shard_map/ppermute | solution.py:20
  15.1 21.7 %collective-permute-start.3 = (bf16[2,2,48,384]{3,2,1,0:T(8,128)(2,1)}, bf16[2,2,48,384]{3,2,1,0:T(8,128)(2,1)}, u32[]{:S(2)}, u32[]{:S(2)}) collective-permute-start(bf16[2,2,48,384]{3,2,1,0:T(8,128)(2,1)} %bitcast.293), channel_id=1, source_target_pairs={{0,64},{64,128},{128,192},{192,256},{256,320},{320,384},{384,448},... | collective-permute-start | bytes 442376 | tf_op jit(solution)/shard_map/ppermute | solution.py:12
  21.8 1.3 copy-start.7
  34.9 3.2 copy-start.5
  34.9 1.9 copy-start.8
  34.9 3.2 copy-start.2
  39.8 4.7 %copy-start.6 = (f32[192,768]{1,0:T(8,128)S(1)}, f32[192,768]{1,0:T(8,128)}, u32[]{:S(2)}) copy-start(f32[192,768]{1,0:T(8,128)} %fusion.121) | copy-start | bytes 1769476
  40.2 0.8 copy-start.3
  41.8 138.3 %collective-permute-start.2 = (f32[2,2,48,384]{3,2,1,0:T(8,128)}, f32[2,2,48,384]{3,2,1,0:T(8,128)}, u32[]{:S(2)}, u32[]{:S(2)}) collective-permute-start(f32[2,2,48,384]{3,2,1,0:T(8,128)} %slice.289), channel_id=1, source_target_pairs={{64,0},{128,64},{192,128},{256,192},{320,256},{384,320},{448,384},... | collective-permute-start | bytes 884744 | tf_op jit(solution)/shard_map/ppermute | solution.py:12
  45.9 7.3 %collective-permute-start.5 = (bf16[2,1,48,768]{3,2,1,0:T(8,128)(2,1)S(1)}, bf16[2,1,48,768]{3,2,1,0:T(8,128)(2,1)S(1)}, u32[]{:S(2)}, u32[]{:S(2)}) collective-permute-start(bf16[2,1,48,768]{3,2,1,0:T(8,128)(2,1)S(1)} %get-tuple-element.87), channel_id=1, source_target_pairs={{2,0},{4,2},{6,4},{8,6},{10,8},{12,10},{14,12},{16,14},{18,16},{20... | collective-permute-start | bytes 442376 | tf_op jit(solution)/shard_map/ppermute | solution.py:23
  47.2 6.7 %collective-permute-start.4 = (bf16[2,1,48,768]{3,2,1,0:T(8,128)(2,1)S(1)}, bf16[2,1,48,768]{3,2,1,0:T(8,128)(2,1)S(1)}, u32[]{:S(2)}, u32[]{:S(2)}) collective-permute-start(bf16[2,1,48,768]{3,2,1,0:T(8,128)(2,1)S(1)} %get-tuple-element.86), channel_id=1, source_target_pairs={{0,2},{2,4},{4,6},{6,8},{8,10},{10,12},{12,14},{14,16},{16,18},{18... | collective-permute-start | bytes 442376 | tf_op jit(solution)/shard_map/ppermute | solution.py:20
  73.4 3.8 %copy-start.1 = (bf16[3,384,768]{2,1,0:T(8,128)(2,1)S(1)}, bf16[3,384,768]{2,1,0:T(8,128)(2,1)}, u32[]{:S(2)}) copy-start(bf16[3,384,768]{2,1,0:T(8,128)(2,1)} %pad_maximum_fusion) | copy-start | bytes 5308420
  77.1 103.1 %copy-start.4 = (f32[4,2,48,384]{3,2,1,0:T(8,128)S(1)}, f32[4,2,48,384]{3,2,1,0:T(8,128)}, u32[]{:S(2)}) copy-start(f32[4,2,48,384]{3,2,1,0:T(8,128)} %copy-done.3) | copy-start | bytes 1769476
  163.1 12.6 %collective-permute-start.10 = (bf16[112,192]{1,0:T(8,128)(2,1)S(1)}, bf16[112,192]{1,0:T(8,128)(2,1)S(1)}, u32[]{:S(2)}, u32[]{:S(2)}) collective-permute-start(bf16[112,192]{1,0:T(8,128)(2,1)S(1)} %get-tuple-element.73), channel_id=1, source_target_pairs={{0,2},{2,4},{4,6},{6,8},{8,10},{10,12},{12,14},{14,16},{16,18},{18... | collective-permute-start | bytes 129032
  164.4 9.3 %collective-permute-start.11 = (bf16[12,192]{1,0:T(8,128)(2,1)S(1)}, bf16[12,192]{1,0:T(8,128)(2,1)S(1)}, u32[]{:S(2)}, u32[]{:S(2)}) collective-permute-start(bf16[12,192]{1,0:T(8,128)(2,1)S(1)} %slice.296), channel_id=1, source_target_pairs={{0,4},{2,6},{4,8},{6,10},{8,12},{10,14},{12,16},{14,18},{16,20},{1... | collective-permute-start | bytes 13832
  167.7 11.1 %collective-permute-start.8 = (bf16[40,768]{1,0:T(8,128)(2,1)S(1)}, bf16[40,768]{1,0:T(8,128)(2,1)S(1)}, u32[]{:S(2)}, u32[]{:S(2)}) collective-permute-start(bf16[40,768]{1,0:T(8,128)(2,1)S(1)} %get-tuple-element.72), channel_id=1, source_target_pairs={{0,6},{2,8},{4,10},{6,12},{8,14},{10,16},{12,18},{14,20},{16,22},{... | collective-permute-start | bytes 184328
  169.0 9.8 %collective-permute-start.7 = (bf16[40,768]{1,0:T(8,128)(2,1)S(1)}, bf16[40,768]{1,0:T(8,128)(2,1)S(1)}, u32[]{:S(2)}, u32[]{:S(2)}) collective-permute-start(bf16[40,768]{1,0:T(8,128)(2,1)S(1)} %get-tuple-element.72), channel_id=1, source_target_pairs={{0,4},{2,6},{4,8},{6,10},{8,12},{10,14},{12,16},{14,18},{16,20},{1... | collective-permute-start | bytes 184328
  173.8 5.0 %collective-permute-start.6 = (bf16[40,768]{1,0:T(8,128)(2,1)S(1)}, bf16[40,768]{1,0:T(8,128)(2,1)S(1)}, u32[]{:S(2)}, u32[]{:S(2)}) collective-permute-start(bf16[40,768]{1,0:T(8,128)(2,1)S(1)} %get-tuple-element.72), channel_id=1, source_target_pairs={{0,2},{2,4},{4,6},{6,8},{8,10},{10,12},{12,14},{14,16},{16,18},{18... | collective-permute-start | bytes 184328
  175.7 3.1 collective-permute-start.9
Sparse Core Ops, SparseCore 0:
  180.3 133.1 all-reduce.10
where the time goes:
time: 325 us; the launch traced here: 323 us
  waiting for transfers between devices  132 us (41%)
  blocking collectives  86 us (26%)
  starting transfers between devices  30.5 us (9%)
  matrix products  27.3 us (8%)
  local copies, waits for them, and re-layouts  23.7 us (7%)
  between operations  15.2 us (5%)
  other arithmetic  9.03 us (3%)
    psum x1, waiting for transfers between devices, local(): lax.psum((band_time, band_space), ('chain', 'clip'))  131 us
    unnamed x1, blocking collectives  86 us
    unnamed x6, starting transfers between devices  12.5 us
    dot_general x9, matrix products, backward_block(): jnp.dot(window.T, cot_core, preferred_element_type=jnp.float32)  10.9 us
    ppermute x2, starting transfers between devices, extended_2(): lax.ppermute(lax.slice_in_dim(block, block.shape[dim] - width, None, axis...  10.1 us
  transfers between devices with their start and end apart: 13, of which 2 were waited for; matrix products, arithmetic and copies ran while one was open for 42% of the time, Pallas kernels for 0%

commit v1 on v0

v1 whole, which is shorter than its diff:
```python
import math

import jax
import jax.numpy as jnp
from jax import lax
from jax.experimental import pallas as pl
from jax.experimental.pallas import tpu as pltpu
from jax.sharding import PartitionSpec as P

FRAMES, BAND, COLS, CH_IN, CH_OUT = 2, 2, 48, 384, 192
CELLS = BAND * COLS
N_X, N_Z = 4, 8
F32, BF16 = jnp.float32, jnp.bfloat16
LANES = 128
PIECE = 24
TIME_ROWS, SPACE_ROWS = 36, 108


def dot(a, b):
    return jnp.dot(a, b, preferred_element_type=F32)


def dot_t(a, b):
    return lax.dot_general(a, b, (((0,), (0,)), ((), ())), preferred_element_type=F32)


def block_kernel(cot, low, high, video, carried, w_time, w_space, packed, grad_hidden, ext, z, hid, time_acc, space_acc, line):
    ext[0 : FRAMES * CELLS] = carried[...]
    ext[FRAMES * CELLS :] = video[...]

    row = lax.broadcasted_iota(jnp.int32, (3 * COLS, 2 * COLS), 0)
    col = lax.broadcasted_iota(jnp.int32, (3 * COLS, 2 * COLS), 1)
    first = 2 * (row % COLS) + 1 - row // COLS
    pick = jnp.where((col == first) | (col == first + 1), 1.0, 0.0).astype(BF16)
    for s in range(2 * FRAMES):
        reach = [dot(pick, low[s])]
        for p in range(2 * BAND):
            reach.append(dot(pick, cot[s, p]))
        reach.append(dot(pick, high[s]))
        pairs = [(reach[i] + reach[i + 1]).astype(BF16) for i in range(2 * BAND + 1)]
        for p in range(BAND):
            for a in range(3):
                both = pairs[2 * p + 2 - a]
                for c in range(3):
                    start = s * CELLS + p * COLS
                    z[3 * a + c, start : start + COLS] = both[c * COLS : (c + 1) * COLS]

    grad = dot(z[0], w_space[0])
    for tap in range(1, 9):
        grad = grad + dot(z[tap], w_space[tap])
    for t in range(FRAMES):
        for j in range(2):
            s = 2 * t + j
            grad_hidden[t * CELLS : (t + 1) * CELLS, j * CH_IN : (j + 1) * CH_IN] = grad[
                s * CELLS : (s + 1) * CELLS
            ].astype(BF16)

    hidden = dot(ext[0 : FRAMES * CELLS], w_time[0])
    for k in range(1, 3):
        hidden = hidden + dot(ext[k * CELLS : (k + FRAMES) * CELLS], w_time[k])
    for t in range(FRAMES):
        for j in range(2):
            s = 2 * t + j
            hid[s * CELLS : (s + 1) * CELLS] = hidden[
                t * CELLS : (t + 1) * CELLS, j * CH_IN : (j + 1) * CH_IN
            ].astype(BF16)

    for k in range(3):
        time_acc[k * CH_IN : (k + 1) * CH_IN] = dot_t(ext[k * CELLS : (k + FRAMES) * CELLS], grad_hidden[...])
    hid_t = hid[...].T
    for tap in range(9):
        space_acc[tap * CH_IN : (tap + 1) * CH_IN] = dot(hid_t, z[tap])

    line[378:384] = jnp.zeros((6, LANES), F32)
    half = SPACE_ROWS // 2
    for r in range(N_X * N_Z):
        t0, s0 = r * TIME_ROWS, r * SPACE_ROWS
        for j in range(6):
            line[j * TIME_ROWS : (j + 1) * TIME_ROWS] = time_acc[t0 : t0 + TIME_ROWS, j * LANES : (j + 1) * LANES]
        line[216:324] = space_acc[s0 : s0 + SPACE_ROWS, 0:LANES]
        line[324:378] = jnp.concatenate(
            [space_acc[s0 : s0 + half, LANES:CH_OUT], space_acc[s0 + half : s0 + SPACE_ROWS, LANES:CH_OUT]], axis=1
        )
        for piece in range(16):
            packed[piece % 2, r // N_Z, piece // 2, r % N_Z] = line[piece * PIECE : (piece + 1) * PIECE].astype(BF16)


def block_terms(cot, low, high, video, carried, w_time, w_space):
    cells = FRAMES * CELLS
    return pl.pallas_call(
        block_kernel,
        name="block_terms",
        out_shape=(
            jax.ShapeDtypeStruct((2, N_X, 8, N_Z, PIECE, LANES), BF16),
            jax.ShapeDtypeStruct((cells, 2 * CH_IN), BF16),
        ),
        in_specs=[pl.BlockSpec(memory_space=pltpu.VMEM)] * 7,
        out_specs=(pl.BlockSpec(memory_space=pltpu.VMEM),) * 2,
        scratch_shapes=[
            pltpu.VMEM((2 * cells, CH_IN), BF16),
            pltpu.VMEM((9, 2 * cells, CH_OUT), BF16),
            pltpu.VMEM((2 * cells, CH_IN), BF16),
            pltpu.VMEM((3 * CH_IN, 2 * CH_IN), F32),
            pltpu.VMEM((9 * CH_IN, CH_OUT), F32),
            pltpu.VMEM((16 * PIECE, LANES), F32),
        ],
        compiler_params=pltpu.CompilerParams(vmem_limit_bytes=40 * 1024 * 1024),
    )(cot, low, high, video, carried, w_time, w_space)


def video_kernel(own, following, w_time, out):
    ahead = jnp.concatenate([own[...], following[...]], axis=0)
    total = None
    for k in range(3):
        term = lax.dot_general(
            ahead[(2 - k) * CELLS : (2 - k + FRAMES) * CELLS],
            w_time[k],
            (((1,), (1,)), ((), ())),
            preferred_element_type=F32,
        )
        total = term if total is None else total + term
    out[...] = total.astype(BF16)


def video_grad(own, following, w_time):
    return pl.pallas_call(
        video_kernel,
        name="video_grad",
        out_shape=jax.ShapeDtypeStruct((FRAMES * CELLS, CH_IN), BF16),
        in_specs=[pl.BlockSpec(memory_space=pltpu.VMEM)] * 3,
        out_specs=pl.BlockSpec(memory_space=pltpu.VMEM),
        compiler_params=pltpu.CompilerParams(vmem_limit_bytes=16 * 1024 * 1024),
    )(own, following, w_time)


def unpack(lines):
    time = lines[:216].reshape(6, TIME_ROWS, LANES).transpose(1, 0, 2).reshape(TIME_ROWS, 6 * LANES)
    rest = lines[324:378]
    space = jnp.concatenate([lines[216:324], jnp.concatenate([rest[:, :64], rest[:, 64:]], axis=0)], axis=1)
    return time, space


def along(axis, steps):
    count = lax.axis_size(axis)
    return [(i, i + steps) for i in range(count) if 0 <= i + steps < count]


def local(video, cotangent, w_time, w_space):
    cot = cotangent[0]
    own = video[0].reshape(FRAMES * CELLS, CH_IN)
    rows, chain = lax.axis_size("rows"), lax.axis_size("chain")
    low = lax.ppermute(cot[:, 2 * BAND - 1], "rows", along("rows", 1))
    high = lax.ppermute(cot[:, 0], "rows", along("rows", -1))
    carried = lax.ppermute(own, "chain", along("chain", 1))
    packed, grad_hidden = block_terms(
        cot, low, high, own, carried, w_time, w_space.transpose(0, 1, 3, 2).reshape(9, CH_OUT, CH_IN)
    )
    following = lax.ppermute(grad_hidden, "chain", along("chain", -1))

    share = packed.reshape(2, -1, LANES)
    share = lax.all_to_all(share, "clip", 0, 0, tiled=True)
    share = share.astype(F32).sum(0).astype(BF16)
    across_x = [[x * N_Z + z for x in range(N_X)] for z in range(N_Z)]
    share = lax.all_to_all(share.reshape(N_X, -1, LANES), "rows", 0, 0, tiled=True, axis_index_groups=across_x)
    share = share.astype(F32).sum(0).astype(BF16)
    across_cz = [[c * rows + x * N_Z + z for c in range(chain) for z in range(N_Z)] for x in range(N_X)]
    share = lax.all_to_all(
        share.reshape(chain * N_Z, PIECE, LANES), ("chain", "rows"), 0, 0, tiled=True, axis_index_groups=across_cz
    )
    voxels = 2 * chain * 2 * FRAMES * rows * 2 * BAND * 2 * COLS
    piece = (share.astype(F32).sum(0) * (1.0 / math.sqrt(voxels))).astype(BF16)
    pieces = jnp.broadcast_to(piece[None], (2 * chain, PIECE, LANES))
    pieces = lax.all_to_all(pieces, ("chain", "clip"), 0, 0, tiled=True)
    grad_time, grad_space = unpack(pieces.reshape(2 * chain * PIECE, LANES))
    grad_video = video_grad(grad_hidden, following, w_time).reshape(video.shape)
    return grad_video, grad_time, grad_space


def solution(mesh):
    placed = P("clip", "chain", "rows", None, None)
    return jax.shard_map(
        local,
        mesh=mesh,
        in_specs=(placed, placed, P(), P()),
        out_specs=(placed, P("rows", None), P("rows", None)),
        check_vma=False,
    )
```

time: 325 us -> 114 us (0.35)
  waiting for transfers between devices: 132 us -> 22.2 us
  blocking collectives: 86 us -> 40 us
  matrix products: 27.3 us -> 0 us
  local copies, waits for them, and re-layouts: 23.7 us -> 5.97 us
  between operations: 15.2 us -> 0.76 us
  Pallas kernels: 0 us -> 5.37 us
    psum x1 -> x0, waiting for transfers between devices: 131 us -> none  [local(): lax.psum((band_time, band_space), ('chain', 'clip'))]
    unnamed x1 -> x0, blocking collectives: 86 us -> none
    all_to_all x0 -> x2, blocking collectives: none -> 40 us  [the longest x1 29.3 us: local(): lax.all_to_all(share.reshape(N_X, -1, LANES), 'rows', 0, 0, tiled=True, a...]
    dot_general x27 -> x0, matrix products: 27.3 us -> none  [the longest x9 10.9 us: backward_block(): jnp.dot(window.T, cot_core, preferred_element_type=jnp.float32)]
    all_to_all x0 -> x2, starting transfers between devices: none -> 21.5 us  [the longest x1 12.9 us: local(): lax.all_to_all(share.reshape(chain * N_Z, PIECE, LANES), ('chain', 'rows'...]
    all_to_all x0 -> x2, waiting for transfers between devices: none -> 19.7 us  [the longest x1 12.6 us: local(): lax.all_to_all(share.reshape(chain * N_Z, PIECE, LANES), ('chain', 'rows'...]
    unnamed x6 -> x0, starting transfers between devices: 12.5 us -> none
    reshape x2 -> x1, local copies, waits for them, and re-layouts: 8.02 us -> 0.01 us  [unpack(): lines[:216].reshape(6, TIME_ROWS, LANES).transpose(1, 0, 2)]
  transfers between devices with their start and end apart: 13 -> 6, of which waited for: 2 -> 3; matrix products, arithmetic and copies ran while one was open for 42% -> 1% of each run, Pallas kernels for 0% -> 1%
where the time goes in v1:
time: 114 us; the launch traced here: 113 us
  blocking collectives  40 us (35%)
  starting transfers between devices  32.2 us (28%)
  waiting for transfers between devices  22.2 us (19%)
  other arithmetic  6.7 us (6%)
  local copies, waits for them, and re-layouts  5.97 us (5%)
  Pallas kernels  5.37 us (5%)
    all_to_all x1, blocking collectives, local(): lax.all_to_all(share.reshape(N_X, -1, LANES), 'rows', 0, 0, tiled=True, a...  29.3 us
    all_to_all x1, starting transfers between devices, local(): lax.all_to_all(share.reshape(chain * N_Z, PIECE, LANES), ('chain', 'rows'...  12.9 us
    all_to_all x1, waiting for transfers between devices, local(): lax.all_to_all(share.reshape(chain * N_Z, PIECE, LANES), ('chain', 'rows'...  12.6 us
    all_to_all x1, blocking collectives, local(): share = lax.all_to_all(share, 'clip', 0, 0, tiled=True)  10.7 us
    all_to_all x1, starting transfers between devices, local(): pieces = lax.all_to_all(pieces, ('chain', 'clip'), 0, 0, tiled=True)  8.6 us
    all_to_all x1, waiting for transfers between devices, local(): pieces = lax.all_to_all(pieces, ('chain', 'clip'), 0, 0, tiled=True)  7.08 us
    reduce_sum x2, other arithmetic, local(): share = share.astype(F32).sum(0).astype(BF16)  6.59 us
    unnamed x12, local copies, waits for them, and re-layouts  5.17 us
  transfers between devices with their start and end apart: 6, of which 3 were waited for; matrix products, arithmetic and copies ran while one was open for 1% of the time, Pallas kernels for 1%

profile of v1, /device:TPU:1, one launch (start us, length us, event | category | flops | bytes accessed | tf_op | source)
XLA Modules:
  0.0 113.2 jit_solution(1055641874504088397)
XLA Ops:
  0.6 0.0 copy-start.3
  0.6 0.0 copy-start
  0.6 1.3 %copy.21 = bf16[1,4,4,96,192]{4,3,1,2,0:T(8,128)(2,1)S(1)} copy(bf16[1,4,4,96,192]{4,3,2,1,0:T(8,128)(2,1)} %param.5) | data formatting | bytes 1179648 | tf_op args[1]
  2.0 4.8 %collective-permute-start = (bf16[4,96,192]{2,1,0:T(8,128)(2,1)S(1)}, bf16[4,96,192]{2,1,0:T(8,128)(2,1)S(1)}, u32[]{:S(2)}, u32[]{:S(2)}) collective-permute-start(bf16[4,96,192]{2,1,0:T(8,128)(2,1)S(1)} %get-tuple-element.14), channel_id=1, source_target_pairs={{0,2},{2,4},{4,6},{6,8},{8,10},{10,12},{12,14},{14,16},{16,18},{18... | collective-permute-start | bytes 442376 | tf_op jit(solution)/shard_map/ppermute | solution.py:152
  6.9 1.3 %collective-permute-start.1 = (bf16[4,96,192]{2,1,0:T(8,128)(2,1)S(1)}, bf16[4,96,192]{2,1,0:T(8,128)(2,1)S(1)}, u32[]{:S(2)}, u32[]{:S(2)}) collective-permute-start(bf16[4,96,192]{2,1,0:T(8,128)(2,1)S(1)} %get-tuple-element.13), channel_id=1, source_target_pairs={{2,0},{4,2},{6,4},{8,6},{10,8},{12,10},{14,12},{16,14},{18,16},{20... | collective-permute-start | bytes 442376 | tf_op jit(solution)/shard_map/ppermute | solution.py:153
  8.2 0.0 copy-done.3
  8.2 3.2 %collective-permute-start.2 = (bf16[192,384]{1,0:T(8,128)(2,1)S(1)}, bf16[192,384]{1,0:T(8,128)(2,1)S(1)}, u32[]{:S(2)}, u32[]{:S(2)}) collective-permute-start(bf16[192,384]{1,0:T(8,128)(2,1)S(1)} %bitcast.24), channel_id=1, source_target_pairs={{0,64},{64,128},{128,192},{192,256},{256,320},{320,384},{384,448},... | collective-permute-start | bytes 442376 | tf_op jit(solution)/shard_map/ppermute | solution.py:154
  11.4 0.0 collective-permute-done.low
  11.4 2.5 %collective-permute-done.1.high = bf16[4,96,192]{2,1,0:T(8,128)(2,1)S(1)} collective-permute-done((bf16[4,96,192]{2,1,0:T(8,128)(2,1)S(1)}, bf16[4,96,192]{2,1,0:T(8,128)(2,1)S(1)}, u32[]{:S(2)}, u32[]{:S(2)}) %collective-permute-start.1) | collective-permute-done | bytes 147488 | tf_op jit(solution)/shard_map/ppermute | solution.py:153
  13.9 0.0 collective-permute-done.2.carried
  13.9 0.0 copy-done
  13.9 0.0 copy-start.1
  13.9 1.1 copy-done.1
  15.0 0.0 copy-start.2
  15.0 1.3 %copy-done.2 = bf16[3,3,384,192]{2,3,1,0:T(8,128)(2,1)S(1)} copy-done((bf16[3,3,384,192]{2,3,1,0:T(8,128)(2,1)S(1)}, bf16[3,3,384,192]{2,3,1,0:T(8,128)(2,1)}, u32[]{:S(2)}) %copy-start.2) | copy-done | bytes 1327128
  16.4 4.0 %block_terms.1 = (bf16[2,4,8,8,24,128]{5,4,3,2,1,0:T(8,128)(2,1)S(1)}, bf16[192,768]{1,0:T(8,128)(2,1)S(1)}) custom-call(bf16[4,4,96,192]{3,2,1,0:T(8,128)(2,1)S(1)} %bitcast.21, bf16[4,96,192]{2,1,0:T(8,128)(2,1)S(1)} %collective-permute-done.low, bf16[4,96,192]{2,1,0:T(8,128)(2,1)S(1)} %collective-permute-done.1.high, bf16[192,384]{1,0:T(8,128)(2,1)S(1)} %bitcast.25, ...), custom_call_target="tpu_custom_call" | custom-call | tf_op jit(solution)/shard_map/block_terms/pallas_call | solution.py:90
  20.3 10.7 %all_to_all.20 = bf16[2,6144,128]{2,1,0:T(8,128)(2,1)} all-to-all(bf16[2,6144,128]{2,1,0:T(8,128)(2,1)S(1)} %bitcast.22), channel_id=1, replica_groups=mesh['chain'=8,'rows'=32,'clip'=2] {'clip'}, dimensions={0} | all-to-all | bytes 6291456 | tf_op jit(solution)/shard_map/all_to_all | solution.py:161
  31.0 4.1 %reduce_sum.33 = bf16[6144,128]{1,0:T(8,128)(2,1)} reduce(bf16[2,6144,128]{2,1,0:T(8,128)(2,1)} %all_to_all.20, bf16[]{:T(256)} %constant.4.clone.1), dimensions={0}, to_apply=%region_0.0 | reduce | flops 786432 | bytes 4718594 | tf_op jit(solution)/shard_map/reduce_sum | solution.py:162
  35.1 29.3 %all_to_all.21 = bf16[4,1536,128]{2,1,0:T(8,128)(2,1)} all-to-all(bf16[4,1536,128]{2,1,0:T(8,128)(2,1)} %bitcast.26), channel_id=1, replica_groups={{0,16,32,48},{2,18,34,50},{4,20,36,52},{6,22,38,54},{8,24,40,56},{10,26..., dimensions={0} | all-to-all | bytes 3145728 | tf_op jit(solution)/shard_map/all_to_all | solution.py:164
  64.4 2.5 %reduce_sum.34 = bf16[1536,128]{1,0:T(8,128)(2,1)} reduce(bf16[4,1536,128]{2,1,0:T(8,128)(2,1)} %all_to_all.21, bf16[]{:T(256)} %constant.4.clone.1), dimensions={0}, to_apply=%region_1.0 | reduce | flops 589824 | bytes 1966082 | tf_op jit(solution)/shard_map/reduce_sum | solution.py:165
  66.9 12.9 %all-to-all-start.2 = ((bf16[64,24,128]{2,1,0:T(8,128)(2,1)}), bf16[64,24,128]{2,1,0:T(8,128)(2,1)S(1)}, u32[]{:S(2)}, u32[]{:S(2)}) async-start(bf16[64,24,128]{2,1,0:T(8,128)(2,1)} %bitcast.10), calls=%async_computation.2 | async-start | bytes 786432 | tf_op jit(solution)/shard_map/all_to_all | solution.py:167
  79.9 1.3 %collective-permute-start.3 = (bf16[192,768]{1,0:T(8,128)(2,1)S(1)}, bf16[192,768]{1,0:T(8,128)(2,1)S(1)}, u32[]{:S(2)}, u32[]{:S(2)}) collective-permute-start(bf16[192,768]{1,0:T(8,128)(2,1)S(1)} %get-tuple-element.5.own), channel_id=1, source_target_pairs={{64,0},{128,64},{192,128},{256,192},{320,256},{384,320},{448,384},... | collective-permute-start | bytes 884744 | tf_op jit(solution)/shard_map/ppermute | solution.py:158
  81.2 12.6 %all-to-all-done.2 = bf16[64,24,128]{2,1,0:T(8,128)(2,1)S(1)} async-done(((bf16[64,24,128]{2,1,0:T(8,128)(2,1)}), bf16[64,24,128]{2,1,0:T(8,128)(2,1)S(1)}, u32[]{:S(2)}, u32[]{:S(2)}) %all-to-all-start.2) | async-done | bytes 393248 | tf_op jit(solution)/shard_map/all_to_all | solution.py:167
  93.8 0.1 convert_reduce_fusion
  93.9 0.7 broadcast_in_dim.2
  94.5 8.6 %all-to-all-start.3 = ((bf16[16,24,128]{2,1,0:T(8,128)(2,1)}), bf16[16,24,128]{2,1,0:T(8,128)(2,1)S(1)}, u32[]{:S(2)}, u32[]{:S(2)}) async-start(bf16[16,24,128]{2,1,0:T(8,128)(2,1)} %broadcast_in_dim.2), calls=%async_computation.3 | async-start | bytes 196608 | tf_op jit(solution)/shard_map/all_to_all | solution.py:173
  103.1 0.0 collective-permute-done.3.following
  103.1 1.4 %video_grad.1 = bf16[192,384]{1,0:T(8,128)(2,1)} custom-call(bf16[192,768]{1,0:T(8,128)(2,1)S(1)} %get-tuple-element.5.own, bf16[192,768]{1,0:T(8,128)(2,1)S(1)} %collective-permute-done.3.following, bf16[3,384,768]{2,1,0:T(8,128)(2,1)S(1)} %copy-done), custom_call_target="tpu_custom_call" | custom-call | tf_op jit(solution)/shard_map/video_grad/pallas_call | solution.py:126
  104.5 7.1 %all-to-all-done.3 = bf16[16,24,128]{2,1,0:T(8,128)(2,1)S(1)} async-done(((bf16[16,24,128]{2,1,0:T(8,128)(2,1)}), bf16[16,24,128]{2,1,0:T(8,128)(2,1)S(1)}, u32[]{:S(2)}, u32[]{:S(2)}) %all-to-all-start.3) | async-done | bytes 98336 | tf_op jit(solution)/shard_map/all_to_all | solution.py:173
  111.6 0.1 fusion
  111.8 0.6 copy.19
  112.4 0.7 copy.17
  (8 shorter events, 0.1 us)
Async XLA Ops:
  0.6 7.5 %copy-start.3 = (bf16[1,2,2,48,384]{4,3,2,1,0:T(8,128)(2,1)S(1)}, bf16[1,2,2,48,384]{4,3,2,1,0:T(8,128)(2,1)}, u32[]{:S(2)}) copy-start(bf16[1,2,2,48,384]{4,3,2,1,0:T(8,128)(2,1)} %param.4) | copy-start | bytes 442372
  0.6 13.3 %copy-start = (bf16[3,384,768]{2,1,0:T(8,128)(2,1)S(1)}, bf16[3,384,768]{2,1,0:T(8,128)(2,1)}, u32[]{:S(2)}) copy-start(bf16[3,384,768]{2,1,0:T(8,128)(2,1)} %w_time.3) | copy-start | bytes 5308420
  2.0 9.4 %collective-permute-start = (bf16[4,96,192]{2,1,0:T(8,128)(2,1)S(1)}, bf16[4,96,192]{2,1,0:T(8,128)(2,1)S(1)}, u32[]{:S(2)}, u32[]{:S(2)}) collective-permute-start(bf16[4,96,192]{2,1,0:T(8,128)(2,1)S(1)} %get-tuple-element.14), channel_id=1, source_target_pairs={{0,2},{2,4},{4,6},{6,8},{8,10},{10,12},{12,14},{14,16},{16,18},{18... | collective-permute-start | bytes 442376 | tf_op jit(solution)/shard_map/ppermute | solution.py:152
  6.9 7.0 %collective-permute-start.1 = (bf16[4,96,192]{2,1,0:T(8,128)(2,1)S(1)}, bf16[4,96,192]{2,1,0:T(8,128)(2,1)S(1)}, u32[]{:S(2)}, u32[]{:S(2)}) collective-permute-start(bf16[4,96,192]{2,1,0:T(8,128)(2,1)S(1)} %get-tuple-element.13), channel_id=1, source_target_pairs={{2,0},{4,2},{6,4},{8,6},{10,8},{12,10},{14,12},{16,14},{18,16},{20... | collective-permute-start | bytes 442376 | tf_op jit(solution)/shard_map/ppermute | solution.py:153
  8.2 5.7 %collective-permute-start.2 = (bf16[192,384]{1,0:T(8,128)(2,1)S(1)}, bf16[192,384]{1,0:T(8,128)(2,1)S(1)}, u32[]{:S(2)}, u32[]{:S(2)}) collective-permute-start(bf16[192,384]{1,0:T(8,128)(2,1)S(1)} %bitcast.24), channel_id=1, source_target_pairs={{0,64},{64,128},{128,192},{192,256},{256,320},{320,384},{384,448},... | collective-permute-start | bytes 442376 | tf_op jit(solution)/shard_map/ppermute | solution.py:154
  13.9 1.1 %copy-start.1 = (bf16[1,4,4,96,192]{4,3,2,1,0:T(8,128)(2,1)S(1)}, bf16[1,4,4,96,192]{4,3,2,1,0:T(8,128)(2,1)}, u32[]{:S(2)}) copy-start(bf16[1,4,4,96,192]{4,3,2,1,0:T(8,128)(2,1)} %param.5) | copy-start | bytes 1769476
  15.0 1.3 %copy-start.2 = (bf16[3,3,384,192]{2,3,1,0:T(8,128)(2,1)S(1)}, bf16[3,3,384,192]{2,3,1,0:T(8,128)(2,1)}, u32[]{:S(2)}) copy-start(bf16[3,3,384,192]{2,3,1,0:T(8,128)(2,1)} %param.7) | copy-start | bytes 3981316
  66.9 26.8 %all-to-all-start.2 = ((bf16[64,24,128]{2,1,0:T(8,128)(2,1)}), bf16[64,24,128]{2,1,0:T(8,128)(2,1)S(1)}, u32[]{:S(2)}, u32[]{:S(2)}) async-start(bf16[64,24,128]{2,1,0:T(8,128)(2,1)} %bitcast.10), calls=%async_computation.2 | async-start | bytes 786432 | tf_op jit(solution)/shard_map/all_to_all | solution.py:167
  79.9 23.3 %collective-permute-start.3 = (bf16[192,768]{1,0:T(8,128)(2,1)S(1)}, bf16[192,768]{1,0:T(8,128)(2,1)S(1)}, u32[]{:S(2)}, u32[]{:S(2)}) collective-permute-start(bf16[192,768]{1,0:T(8,128)(2,1)S(1)} %get-tuple-element.5.own), channel_id=1, source_target_pairs={{64,0},{128,64},{192,128},{256,192},{320,256},{384,320},{448,384},... | collective-permute-start | bytes 884744 | tf_op jit(solution)/shard_map/ppermute | solution.py:158
  94.5 17.1 %all-to-all-start.3 = ((bf16[16,24,128]{2,1,0:T(8,128)(2,1)}), bf16[16,24,128]{2,1,0:T(8,128)(2,1)S(1)}, u32[]{:S(2)}, u32[]{:S(2)}) async-start(bf16[16,24,128]{2,1,0:T(8,128)(2,1)} %broadcast_in_dim.2), calls=%async_computation.3 | async-start | bytes 196608 | tf_op jit(solution)/shard_map/all_to_all | solution.py:173

commit v2 on v1

v2 whole, which is shorter than its diff:
```python
import math

import jax
import jax.numpy as jnp
from jax import lax
from jax.experimental import pallas as pl
from jax.experimental.pallas import tpu as pltpu
from jax.sharding import PartitionSpec as P

FRAMES, BAND, COLS, CH_IN, CH_OUT = 2, 2, 48, 384, 192
CELLS = BAND * COLS
N_X, N_Z = 4, 8
F32, BF16 = jnp.float32, jnp.bfloat16
LANES = 128
PIECE, LINES = 48, 384
TIME_ROWS, SPACE_ROWS = 36, 108


def dot(a, b):
    return jnp.dot(a, b, preferred_element_type=F32)


def dot_t(a, b):
    return lax.dot_general(a, b, (((0,), (0,)), ((), ())), preferred_element_type=F32)


VMEM = pl.BlockSpec(memory_space=pltpu.VMEM)


def params(mib):
    return pltpu.CompilerParams(vmem_limit_bytes=mib * 1024 * 1024)


def picker():
    row = lax.broadcasted_iota(jnp.int32, (3 * COLS, 2 * COLS), 0)
    col = lax.broadcasted_iota(jnp.int32, (3 * COLS, 2 * COLS), 1)
    first = 2 * (row % COLS) + 1 - row // COLS
    return jnp.where((col == first) | (col == first + 1), 1.0, 0.0).astype(BF16)


def put(z, a, p, s, both):
    start = (p * 2 * FRAMES + s) * COLS
    for c in range(3):
        z[3 * a + c, start : start + COLS] = both[c * COLS : (c + 1) * COLS]


HALF = 2 * FRAMES * COLS


def edges_kernel(cot, top, bottom, sems):
    copies = [
        pltpu.make_async_copy(cot.at[:, 2 * BAND - 1], bottom, sems.at[0]),
        pltpu.make_async_copy(cot.at[:, 0], top, sems.at[1]),
    ]
    for copy in copies:
        copy.start()
    for copy in copies:
        copy.wait()


def edges(cot):
    edge = jax.ShapeDtypeStruct((2 * FRAMES, 2 * COLS, CH_OUT), BF16)
    return pl.pallas_call(
        edges_kernel,
        name="edges",
        out_shape=(edge, edge),
        in_specs=[pl.BlockSpec(memory_space=pl.ANY)],
        out_specs=(VMEM, VMEM),
        scratch_shapes=[pltpu.SemaphoreType.DMA((2,))],
    )(cot)


def inner_kernel(cot, video, w_time, w_space, z, grad, hidden):
    pick = picker()
    for s in range(2 * FRAMES):
        reach = [dot(pick, cot[s, p]) for p in range(2 * BAND)]
        for p in range(BAND):
            put(z, 1, p, s, (reach[2 * p] + reach[2 * p + 1]).astype(BF16))
        both = (reach[1] + reach[2]).astype(BF16)
        put(z, 0, 0, s, both)
        put(z, 2, 1, s, both)
    total = dot(z[3], w_space[3])
    for tap in (4, 5):
        total = total + dot(z[tap], w_space[tap])
    upper, lower = total[:HALF], total[HALF:]
    for c in range(3):
        upper = upper + dot(z[c, :HALF], w_space[c])
        lower = lower + dot(z[6 + c, HALF:], w_space[6 + c])
    grad[:HALF] = upper
    grad[HALF:] = lower
    hidden[:CELLS] = dot(video[:CELLS], w_time[2])
    hidden[CELLS:] = dot(video[:CELLS], w_time[1]) + dot(video[CELLS:], w_time[2])


def inner_terms(cot, video, w_time, w_space):
    cells = FRAMES * CELLS
    return pl.pallas_call(
        inner_kernel,
        name="inner_terms",
        out_shape=(
            jax.ShapeDtypeStruct((9, 2 * cells, CH_OUT), BF16),
            jax.ShapeDtypeStruct((2 * cells, CH_IN), F32),
            jax.ShapeDtypeStruct((cells, 2 * CH_IN), F32),
        ),
        in_specs=[VMEM] * 4,
        out_specs=(VMEM,) * 3,
        compiler_params=params(12),
        cost_estimate=pl.CostEstimate(flops=1_500_000_000, bytes_accessed=6_000_000, transcendentals=0),
    )(cot, video, w_time, w_space)


def block_kernel(
    cot, low, high, video, carried, w_time, w_space, z_in, grad_in, hidden_in,
    keep, send, grad_hidden, z,
    ext, hid, time_acc, space_acc, line,
):
    ext[0 : FRAMES * CELLS] = carried[...]
    ext[FRAMES * CELLS :] = video[...]
    pick = picker()
    for s in range(2 * FRAMES):
        put(z, 2, 0, s, (dot(pick, low[s]) + dot(pick, cot[s, 0])).astype(BF16))
        put(z, 0, 1, s, (dot(pick, cot[s, 2 * BAND - 1]) + dot(pick, high[s])).astype(BF16))
    upper, lower = grad_in[:HALF], grad_in[HALF:]
    for c in range(3):
        upper = upper + dot(z[6 + c, :HALF], w_space[6 + c])
        lower = lower + dot(z[c, HALF:], w_space[c])
    for p, part in enumerate((upper, lower)):
        for t in range(FRAMES):
            for j in range(2):
                s = 2 * t + j
                grad_hidden[(t * BAND + p) * COLS : (t * BAND + p + 1) * COLS, j * CH_IN : (j + 1) * CH_IN] = part[
                    s * COLS : (s + 1) * COLS
                ].astype(BF16)

    first = hidden_in[:CELLS] + dot(carried[:CELLS], w_time[0]) + dot(carried[CELLS:], w_time[1])
    second = hidden_in[CELLS:] + dot(carried[CELLS:], w_time[0])
    for t, hidden in enumerate((first, second)):
        for p in range(BAND):
            for j in range(2):
                start = (p * 2 * FRAMES + 2 * t + j) * COLS
                hid[start : start + COLS] = hidden[
                    p * COLS : (p + 1) * COLS, j * CH_IN : (j + 1) * CH_IN
                ].astype(BF16)

    for k in range(3):
        time_acc[k * CH_IN : (k + 1) * CH_IN] = dot_t(ext[k * CELLS : (k + FRAMES) * CELLS], grad_hidden[...])
    hid_t = hid[...].T
    for tap in range(9):
        space_acc[tap * CH_IN : (tap + 1) * CH_IN] = dot(hid_t, z[tap])

    mine = lax.axis_index("clip")
    line[378:LINES] = jnp.zeros((6, LANES), F32)
    half = SPACE_ROWS // 2
    for r in range(N_X * N_Z):
        x, zh, zl = r // N_Z, r % N_Z // 2, r % 2
        t0, s0 = r * TIME_ROWS, r * SPACE_ROWS
        for j in range(6):
            line[j * TIME_ROWS : (j + 1) * TIME_ROWS] = time_acc[t0 : t0 + TIME_ROWS, j * LANES : (j + 1) * LANES]
        line[216:324] = space_acc[s0 : s0 + SPACE_ROWS, 0:LANES]
        line[324:378] = jnp.concatenate(
            [space_acc[s0 : s0 + half, LANES:CH_OUT], space_acc[s0 + half : s0 + SPACE_ROWS, LANES:CH_OUT]], axis=1
        )
        for c0 in range(2):
            for c1 in range(2):
                piece = (c0 * 2 + c1) * PIECE
                own = pl.multiple_of(mine * (LINES // 2) + piece, 8)
                other = pl.multiple_of((1 - mine) * (LINES // 2) + piece, 8)
                keep[x, c0, zl, c1, zh] = line[pl.ds(own, PIECE)].astype(BF16)
                send[x, c0, zl, c1, zh] = line[pl.ds(other, PIECE)].astype(BF16)


def block_terms(cot, low, high, video, carried, w_time, w_space, z, grad, hidden):
    cells = FRAMES * CELLS
    half = jax.ShapeDtypeStruct((N_X, 2, 2, 2, N_Z // 2, PIECE, LANES), BF16)
    return pl.pallas_call(
        block_kernel,
        name="block_terms",
        out_shape=(
            half,
            half,
            jax.ShapeDtypeStruct((cells, 2 * CH_IN), BF16),
            jax.ShapeDtypeStruct(z.shape, BF16),
        ),
        in_specs=[VMEM] * 10,
        out_specs=(VMEM,) * 4,
        input_output_aliases={7: 3},
        scratch_shapes=[
            pltpu.VMEM((2 * cells, CH_IN), BF16),
            pltpu.VMEM((2 * cells, CH_IN), BF16),
            pltpu.VMEM((3 * CH_IN, 2 * CH_IN), F32),
            pltpu.VMEM((9 * CH_IN, CH_OUT), F32),
            pltpu.VMEM((LINES, LANES), F32),
        ],
        compiler_params=params(24),
        cost_estimate=pl.CostEstimate(flops=2_500_000_000, bytes_accessed=10_000_000, transcendentals=0),
    )(cot, low, high, video, carried, w_time, w_space, z, grad, hidden)


def pair_kernel(a, b, out):
    out[...] = (a[...].astype(F32) + b[...].astype(F32)).astype(BF16)


def pair_sum(a, b):
    return pl.pallas_call(
        pair_kernel,
        name="pair_sum",
        out_shape=jax.ShapeDtypeStruct(a.shape, BF16),
        in_specs=[VMEM] * 2,
        out_specs=VMEM,
        compiler_params=params(8),
    )(a, b)


def group_kernel(copies, parts, out):
    total = parts[0].astype(F32)
    for i in range(1, parts.shape[0]):
        total = total + parts[i].astype(F32)
    total = total.astype(BF16)
    if copies is None:
        out[...] = total
    else:
        for i in range(copies):
            out[i] = total


def group_sum(parts, copies=None):
    lead = () if copies is None else (copies,)
    return pl.pallas_call(
        lambda *refs: group_kernel(copies, *refs),
        name="group_sum",
        out_shape=jax.ShapeDtypeStruct(lead + parts.shape[1:], BF16),
        in_specs=[VMEM],
        out_specs=VMEM,
        compiler_params=params(8),
    )(parts)


def unpack_kernel(scale, pieces, time, space, line):
    for k in range(2):
        for c0 in range(2):
            for c1 in range(2):
                low = (c1 * 2 + c0) * 2 + k
                start = ((k * 2 + c0) * 2 + c1) * PIECE
                total = pieces[low].astype(F32) + pieces[8 + low].astype(F32)
                line[start : start + PIECE] = total * scale
    for j in range(6):
        time[:, j * LANES : (j + 1) * LANES] = line[j * TIME_ROWS : (j + 1) * TIME_ROWS].astype(BF16)
    space[0:LANES] = line[216 : 216 + LANES].T[:, :SPACE_ROWS].astype(BF16)
    half = SPACE_ROWS // 2
    rest = line[324 : 324 + 64].T
    space[LANES:] = jnp.concatenate([rest[0:64, :half], rest[64:, :half]], axis=1).astype(BF16)


def unpack(pieces, scale):
    return pl.pallas_call(
        lambda *refs: unpack_kernel(scale, *refs),
        name="unpack",
        out_shape=(
            jax.ShapeDtypeStruct((TIME_ROWS, 6 * LANES), BF16),
            jax.ShapeDtypeStruct((CH_OUT, SPACE_ROWS), BF16),
        ),
        in_specs=[VMEM],
        out_specs=(VMEM, VMEM),
        scratch_shapes=[pltpu.VMEM((LINES + 8, LANES), F32)],
        compiler_params=params(8),
    )(pieces)


def video_kernel(own, following, w_time, out):
    ahead = jnp.concatenate([own[...], following[...]], axis=0)
    total = None
    for k in range(3):
        term = lax.dot_general(
            ahead[(2 - k) * CELLS : (2 - k + FRAMES) * CELLS],
            w_time[k],
            (((1,), (1,)), ((), ())),
            preferred_element_type=F32,
        )
        total = term if total is None else total + term
    out[...] = total.astype(BF16)


def video_grad(own, following, w_time):
    return pl.pallas_call(
        video_kernel,
        name="video_grad",
        out_shape=jax.ShapeDtypeStruct((FRAMES * CELLS, CH_IN), BF16),
        in_specs=[VMEM] * 3,
        out_specs=VMEM,
        compiler_params=params(8),
        cost_estimate=pl.CostEstimate(flops=350_000_000, bytes_accessed=2_500_000, transcendentals=0),
    )(own, following, w_time)


def along(axis, steps):
    count = lax.axis_size(axis)
    return [(i, i + steps) for i in range(count) if 0 <= i + steps < count]


def exchange(parts, groups):
    return lax.all_to_all(parts, ("chain", "rows"), 0, 0, tiled=True, axis_index_groups=groups)


def local(video, cotangent, w_time, w_space):
    cot = cotangent[0]
    own = video[0].reshape(FRAMES * CELLS, CH_IN)
    rows, chain = lax.axis_size("rows"), lax.axis_size("chain")
    w_space = w_space.transpose(0, 1, 3, 2).reshape(9, CH_OUT, CH_IN)
    top, bottom = edges(cot)
    low = lax.ppermute(bottom, "rows", along("rows", 1))
    high = lax.ppermute(top, "rows", along("rows", -1))
    carried = lax.ppermute(own, "chain", along("chain", 1))
    inner = inner_terms(cot, own, w_time, w_space)
    keep, send, grad_hidden, _ = block_terms(cot, low, high, own, carried, w_time, w_space, *inner)
    received = lax.ppermute(send, "clip", [(0, 1), (1, 0)])
    following = lax.ppermute(grad_hidden, "chain", along("chain", -1))

    def device(c, x, z):
        return c * rows + x * N_Z + z

    near = [
        [device(2 * ch + c, x, 2 * zh + z) for x in range(N_X) for c in range(2) for z in range(2)]
        for ch in range(chain // 2)
        for zh in range(N_Z // 2)
    ]
    far = [
        [device(4 * c2 + 2 * c + c0, x, 2 * zh + zl) for c in range(2) for zh in range(N_Z // 2)]
        for c2 in range(chain // 4)
        for c0 in range(2)
        for x in range(N_X)
        for zl in range(2)
    ]
    share = pair_sum(keep.reshape(-1, LANES), received.reshape(-1, LANES))
    share = group_sum(exchange(share.reshape(4 * N_X, -1, LANES), near))
    share = group_sum(exchange(share.reshape(N_Z, PIECE, LANES), far), 2 * chain)
    pieces = lax.all_to_all(share, ("chain", "clip"), 0, 0, tiled=True)
    voxels = 2 * chain * 2 * FRAMES * rows * 2 * BAND * 2 * COLS
    grad_time, grad_space = unpack(pieces, 1.0 / math.sqrt(voxels))
    grad_video = video_grad(grad_hidden, following, w_time).reshape(video.shape)
    return grad_video, grad_time, grad_space.T


def solution(mesh):
    placed = P("clip", "chain", "rows", None, None)
    return jax.shard_map(
        local,
        mesh=mesh,
        in_specs=(placed, placed, P(), P()),
        out_specs=(placed, P("rows", None), P("rows", None)),
        check_vma=False,
    )
```

time: 114 us -> 102 us (0.89)
  starting transfers between devices: 32.2 us -> 20.8 us
  blocking collectives: 40 us -> 48.2 us
  waiting for transfers between devices: 22.2 us -> 15.2 us
  other arithmetic: 6.7 us -> 0 us
  Pallas kernels: 5.37 us -> 10.8 us
    all_to_all x2 -> x1, waiting for transfers between devices: 19.7 us -> 0.01 us  [local(): pieces = lax.all_to_all(share, ('chain', 'clip'), 0, 0, tiled=True)]
    all_to_all x2 -> x1, starting transfers between devices: 21.5 us -> 6.5 us  [local(): pieces = lax.all_to_all(share, ('chain', 'clip'), 0, 0, tiled=True)]
    ppermute x1, waiting for transfers between devices: 0.01 us -> 11.6 us  [local(): following = lax.ppermute(grad_hidden, 'chain', along('chain', -1))]
    all_to_all x2, blocking collectives: 40 us -> 48.2 us  [exchange(): lax.all_to_all(parts, ('chain', 'rows'), 0, 0, tiled=True, axis_index_gro...]
    reduce_sum x3 -> x0, other arithmetic: 6.67 us -> none  [the longest x2 6.59 us: local(): share = share.astype(F32).sum(0).astype(BF16)]
    pallas_call x1 -> x7, Pallas kernels: 3.97 us -> 9.42 us  [the longest x1 4.11 us: block_terms(): pl.pallas_call(block_kernel, name='block_terms', out_shape=(half, half, j...]
    ppermute x2 -> x3, starting transfers between devices: 6.13 us -> 9.02 us  [the longest x1 4.01 us: local(): low = lax.ppermute(bottom, 'rows', along('rows', 1))]
    ppermute x2 -> x3, waiting for transfers between devices: 2.51 us -> 3.58 us  [the longest x1 3.01 us: local(): received = lax.ppermute(send, 'clip', [(0, 1), (1, 0)])]
  transfers between devices with their start and end apart: 6 -> 6, of which waited for: 3 -> 3; matrix products, arithmetic and copies ran while one was open for 1% -> 0% of each run, Pallas kernels for 1% -> 5%
where the time goes in v2:
time: 102 us; the launch traced here: 101 us
  blocking collectives  48.2 us (47%)
  starting transfers between devices  20.8 us (20%)
  waiting for transfers between devices  15.2 us (15%)
  Pallas kernels  10.8 us (11%)
  local copies, waits for them, and re-layouts  4.89 us (5%)
    all_to_all x2, blocking collectives, exchange(): lax.all_to_all(parts, ('chain', 'rows'), 0, 0, tiled=True, axis_index_gro...  48.2 us
    ppermute x1, waiting for transfers between devices, local(): following = lax.ppermute(grad_hidden, 'chain', along('chain', -1))  11.6 us
    all_to_all x1, starting transfers between devices, local(): pieces = lax.all_to_all(share, ('chain', 'clip'), 0, 0, tiled=True)  6.5 us
    unnamed x16, local copies, waits for them, and re-layouts  4.89 us
    pallas_call x1, Pallas kernels, block_terms(): pl.pallas_call(block_kernel, name='block_terms', out_shape=(half, half, j...  4.11 us
    ppermute x1, starting transfers between devices, local(): carried = lax.ppermute(own, 'chain', along('chain', 1))  4.04 us
    ppermute x1, starting transfers between devices, local(): low = lax.ppermute(bottom, 'rows', along('rows', 1))  4.01 us
    ppermute x1, starting transfers between devices, local(): received = lax.ppermute(send, 'clip', [(0, 1), (1, 0)])  3.72 us
  transfers between devices with their start and end apart: 6, of which 3 were waited for; matrix products, arithmetic and copies ran while one was open for 0% of the time, Pallas kernels for 5%

profile of v2, /device:TPU:1, one launch (start us, length us, event | category | flops | bytes accessed | tf_op | source)
XLA Modules:
  0.0 100.7 jit_solution(13563835972994777827)
XLA Ops:
  0.6 4.0 %collective-permute-start.2 = (bf16[192,384]{1,0:T(8,128)(2,1)}, bf16[192,384]{1,0:T(8,128)(2,1)S(1)}, u32[]{:S(2)}, u32[]{:S(2)}) collective-permute-start(bf16[192,384]{1,0:T(8,128)(2,1)} %bitcast.20), channel_id=1, source_target_pairs={{0,64},{64,128},{128,192},{192,256},{256,320},{320,384},{384,448},... | collective-permute-start | bytes 442376 | tf_op jit(solution)/shard_map/ppermute | solution.py:312
  4.7 1.8 %edges.1 = (bf16[4,96,192]{2,1,0:T(8,128)(2,1)}, bf16[4,96,192]{2,1,0:T(8,128)(2,1)}) custom-call(bf16[4,4,96,192]{3,2,1,0:T(8,128)(2,1)} %bitcast.14), custom_call_target="tpu_custom_call" | custom-call | tf_op jit(solution)/shard_map/edges/pallas_call | solution.py:63
  6.5 4.0 %collective-permute-start = (bf16[4,96,192]{2,1,0:T(8,128)(2,1)}, bf16[4,96,192]{2,1,0:T(8,128)(2,1)S(1)}, u32[]{:S(2)}, u32[]{:S(2)}) collective-permute-start(bf16[4,96,192]{2,1,0:T(8,128)(2,1)} %get-tuple-element.13), channel_id=1, source_target_pairs={{0,2},{2,4},{4,6},{6,8},{8,10},{10,12},{12,14},{14,16},{16,18},{18... | collective-permute-start | bytes 442376 | tf_op jit(solution)/shard_map/ppermute | solution.py:310
  10.5 1.3 %collective-permute-start.1 = (bf16[4,96,192]{2,1,0:T(8,128)(2,1)}, bf16[4,96,192]{2,1,0:T(8,128)(2,1)S(1)}, u32[]{:S(2)}, u32[]{:S(2)}) collective-permute-start(bf16[4,96,192]{2,1,0:T(8,128)(2,1)} %get-tuple-element.14), channel_id=1, source_target_pairs={{2,0},{4,2},{6,4},{8,6},{10,8},{12,10},{14,12},{16,14},{18,16},{20... | collective-permute-start | bytes 442376 | tf_op jit(solution)/shard_map/ppermute | solution.py:311
  11.8 0.0 copy-start
  11.8 1.5 %copy-done = bf16[3,384,768]{2,1,0:T(8,128)(2,1)S(1)} copy-done((bf16[3,384,768]{2,1,0:T(8,128)(2,1)S(1)}, bf16[3,384,768]{2,1,0:T(8,128)(2,1)}, u32[]{:S(2)}) %copy-start) | copy-done | bytes 1769496
  13.3 0.0 copy-start.2
  13.3 1.1 %copy-done.2 = bf16[1,4,4,96,192]{4,3,2,1,0:T(8,128)(2,1)S(1)} copy-done((bf16[1,4,4,96,192]{4,3,2,1,0:T(8,128)(2,1)S(1)}, bf16[1,4,4,96,192]{4,3,2,1,0:T(8,128)(2,1)}, u32[]{:S(2)}) %copy-start.2) | copy-done | bytes 589848
  14.4 0.0 copy-start.4
  14.4 1.3 %copy-done.4 = bf16[3,3,384,192]{2,3,1,0:T(8,128)(2,1)S(1)} copy-done((bf16[3,3,384,192]{2,3,1,0:T(8,128)(2,1)S(1)}, bf16[3,3,384,192]{2,3,1,0:T(8,128)(2,1)}, u32[]{:S(2)}) %copy-start.4) | copy-done | bytes 1327128
  15.7 0.0 copy-start.6
  15.7 0.9 copy-done.6
  16.6 0.0 copy-start.1
  16.6 0.0 copy-start.3
  16.6 0.0 copy-start.5
  16.6 0.0 copy-start.7
  16.7 1.4 %inner_terms.1 = (bf16[9,384,192]{2,1,0:T(8,128)(2,1)S(1)}, f32[384,384]{1,0:T(8,128)S(1)}, f32[192,768]{1,0:T(8,128)S(1)}) custom-call(bf16[4,4,96,192]{3,2,1,0:T(8,128)(2,1)S(1)} %bitcast.15, bf16[192,384]{1,0:T(8,128)(2,1)S(1)} %bitcast.21, bf16[3,384,768]{2,1,0:T(8,128)(2,1)S(1)} %copy-done, bf16[9,192,384]{2,1,0:T(8,128)(2,1)S(1)} %bitcast.18), custom_call_target="tpu_custom_call" | custom-call | flops 1500000000 | bytes 6000000 | tf_op jit(solution)/shard_map/inner_terms/pallas_call | solution.py:97
  18.1 0.0 collective-permute-done.2.carried
  18.1 0.0 collective-permute-done.low
  18.1 0.6 collective-permute-done.1.high
  18.7 0.0 copy-done.1
  18.7 0.0 copy-done.3
  18.7 0.0 copy-done.5
  18.7 0.0 copy-done.7
  18.7 4.1 %block_terms.1 = (bf16[4,2,2,2,4,48,128]{6,5,4,3,2,1,0:T(8,128)(2,1)S(1)}, bf16[4,2,2,2,4,48,128]{6,5,4,3,2,1,0:T(8,128)(2,1)S(1)}, bf16[192,768]{1,0:T(8,128)(2,1)S(1)}, bf16[9,384,192]{2,1,0:T(8,128)(2,1)S(1)}) custom-call(bf16[4,4,96,192]{3,2,1,0:T(8,128)(2,1)S(1)} %bitcast.16, ...), custom_call_target="tpu_custom_call", output_to_operand_aliasing={{3}: (7, {})} | custom-call | flops 2500000000 | bytes 10000000 | tf_op jit(solution)/shard_map/block_terms/pallas_call | solution.py:175
  22.8 3.7 %collective-permute-start.4 = (bf16[4,2,2,2,4,48,128]{6,5,4,3,2,1,0:T(8,128)(2,1)S(1)}, bf16[4,2,2,2,4,48,128]{6,5,4,3,2,1,0:T(8,128)(2,1)S(1)}, u32[]{:S(2)}, u32[]{:S(2)}) collective-permute-start(bf16[4,2,2,2,4,48,128]{6,5,4,3,2,1,0:T(8,128)(2,1)S(1)} %get-tuple-element.20), channel_id=1, source_target_pairs={{0,1},{1,0},{2,3},{3,2},{4,5},{5,4},{6,7},{7,6},{8,9},{9,8},{10,11... | collective-permute-start | bytes 4718600 | tf_op jit(solution)/shard_map/ppermute | solution.py:315
  26.6 3.0 %collective-permute-done.4 = bf16[4,2,2,2,4,48,128]{6,5,4,3,2,1,0:T(8,128)(2,1)S(1)} collective-permute-done((bf16[4,2,2,2,4,48,128]{6,5,4,3,2,1,0:T(8,128)(2,1)S(1)}, bf16[4,2,2,2,4,48,128]{6,5,4,3,2,1,0:T(8,128)(2,1)S(1)}, u32[]{:S(2)}, u32[]{:S(2)}) %collective-permute-start.4) | collective-permute-done | bytes 1572896 | tf_op jit(solution)/shard_map/ppermute | solution.py:315
  29.6 0.4 pair_sum.1
  29.9 32.3 %all_to_all.15.refs_0_ = bf16[16,384,128]{2,1,0:T(8,128)(2,1)S(1)} all-to-all(bf16[16,384,128]{2,1,0:T(8,128)(2,1)S(1)} %bitcast.11), channel_id=1, replica_groups={{0,2,64,66,16,18,80,82,32,34,96,98,48,50,112,114},{4,6,68,70,20,22,84,8..., dimensions={0} | all-to-all | bytes 3145728 | tf_op jit(solution)/shard_map/all_to_all | solution.py:301
  62.2 0.2 group_sum.2
  62.4 16.0 %all_to_all.16.refs_0_ = bf16[8,48,128]{2,1,0:T(8,128)(2,1)S(1)} all-to-all(bf16[8,48,128]{2,1,0:T(8,128)(2,1)S(1)} %bitcast.17), channel_id=1, replica_groups={{0,4,8,12,128,132,136,140},{2,6,10,14,130,134,138,142},{16,20,24,28,144..., dimensions={0} | all-to-all | bytes 196608 | tf_op jit(solution)/shard_map/all_to_all | solution.py:301
  78.4 0.7 group_sum.3
  79.1 6.5 %all-to-all-start.2 = ((bf16[16,48,128]{2,1,0:T(8,128)(2,1)}), bf16[16,48,128]{2,1,0:T(8,128)(2,1)S(1)}, u32[]{:S(2)}, u32[]{:S(2)}) async-start(bf16[16,48,128]{2,1,0:T(8,128)(2,1)} %group_sum.3), calls=%async_computation.2 | async-start | bytes 393216 | tf_op jit(solution)/shard_map/all_to_all | solution.py:336
  85.6 1.3 %collective-permute-start.3 = (bf16[192,768]{1,0:T(8,128)(2,1)S(1)}, bf16[192,768]{1,0:T(8,128)(2,1)S(1)}, u32[]{:S(2)}, u32[]{:S(2)}) collective-permute-start(bf16[192,768]{1,0:T(8,128)(2,1)S(1)} %get-tuple-element.18.own), channel_id=1, source_target_pairs={{64,0},{128,64},{192,128},{256,192},{320,256},{384,320},{448,384},... | collective-permute-start | bytes 884744 | tf_op jit(solution)/shard_map/ppermute | solution.py:316
  86.9 11.6 %collective-permute-done.3.following = bf16[192,768]{1,0:T(8,128)(2,1)S(1)} collective-permute-done((bf16[192,768]{1,0:T(8,128)(2,1)S(1)}, bf16[192,768]{1,0:T(8,128)(2,1)S(1)}, u32[]{:S(2)}, u32[]{:S(2)}) %collective-permute-start.3) | collective-permute-done | bytes 294944 | tf_op jit(solution)/shard_map/ppermute | solution.py:316
  98.5 1.4 %video_grad.1 = bf16[192,384]{1,0:T(8,128)(2,1)} custom-call(bf16[192,768]{1,0:T(8,128)(2,1)S(1)} %get-tuple-element.18.own, bf16[192,768]{1,0:T(8,128)(2,1)S(1)} %collective-permute-done.3.following, bf16[3,384,768]{2,1,0:T(8,128)(2,1)S(1)} %copy-done.1), custom_call_target="tpu_custom_call" | custom-call | flops 350000000 | bytes 2500000 | tf_op jit(solution)/shard_map/video_grad/pallas_call | solution.py:284
  99.9 0.0 all-to-all-done.2.refs_0_
  99.9 0.8 unpack.1
Async XLA Ops:
  0.6 17.5 %collective-permute-start.2 = (bf16[192,384]{1,0:T(8,128)(2,1)}, bf16[192,384]{1,0:T(8,128)(2,1)S(1)}, u32[]{:S(2)}, u32[]{:S(2)}) collective-permute-start(bf16[192,384]{1,0:T(8,128)(2,1)} %bitcast.20), channel_id=1, source_target_pairs={{0,64},{64,128},{128,192},{192,256},{256,320},{320,384},{384,448},... | collective-permute-start | bytes 442376 | tf_op jit(solution)/shard_map/ppermute | solution.py:312
  6.5 11.6 %collective-permute-start = (bf16[4,96,192]{2,1,0:T(8,128)(2,1)}, bf16[4,96,192]{2,1,0:T(8,128)(2,1)S(1)}, u32[]{:S(2)}, u32[]{:S(2)}) collective-permute-start(bf16[4,96,192]{2,1,0:T(8,128)(2,1)} %get-tuple-element.13), channel_id=1, source_target_pairs={{0,2},{2,4},{4,6},{6,8},{8,10},{10,12},{12,14},{14,16},{16,18},{18... | collective-permute-start | bytes 442376 | tf_op jit(solution)/shard_map/ppermute | solution.py:310
  10.5 8.2 %collective-permute-start.1 = (bf16[4,96,192]{2,1,0:T(8,128)(2,1)}, bf16[4,96,192]{2,1,0:T(8,128)(2,1)S(1)}, u32[]{:S(2)}, u32[]{:S(2)}) collective-permute-start(bf16[4,96,192]{2,1,0:T(8,128)(2,1)} %get-tuple-element.14), channel_id=1, source_target_pairs={{2,0},{4,2},{6,4},{8,6},{10,8},{12,10},{14,12},{16,14},{18,16},{20... | collective-permute-start | bytes 442376 | tf_op jit(solution)/shard_map/ppermute | solution.py:311
  11.8 1.5 %copy-start = (bf16[3,384,768]{2,1,0:T(8,128)(2,1)S(1)}, bf16[3,384,768]{2,1,0:T(8,128)(2,1)}, u32[]{:S(2)}) copy-start(bf16[3,384,768]{2,1,0:T(8,128)(2,1)} %w_time.5) | copy-start | bytes 5308420
  13.3 1.1 %copy-start.2 = (bf16[1,4,4,96,192]{4,3,2,1,0:T(8,128)(2,1)S(1)}, bf16[1,4,4,96,192]{4,3,2,1,0:T(8,128)(2,1)}, u32[]{:S(2)}) copy-start(bf16[1,4,4,96,192]{4,3,2,1,0:T(8,128)(2,1)} %param.5) | copy-start | bytes 1769476
  14.4 1.3 %copy-start.4 = (bf16[3,3,384,192]{2,3,1,0:T(8,128)(2,1)S(1)}, bf16[3,3,384,192]{2,3,1,0:T(8,128)(2,1)}, u32[]{:S(2)}) copy-start(bf16[3,3,384,192]{2,3,1,0:T(8,128)(2,1)} %param.7) | copy-start | bytes 3981316
  15.7 0.9 copy-start.6
  16.6 2.0 %copy-start.1 = (bf16[3,384,768]{2,1,0:T(8,128)(2,1)S(1)}, bf16[3,384,768]{2,1,0:T(8,128)(2,1)}, u32[]{:S(2)}) copy-start(bf16[3,384,768]{2,1,0:T(8,128)(2,1)} %w_time.5) | copy-start | bytes 5308420
  16.6 2.0 %copy-start.3 = (bf16[1,4,4,96,192]{4,3,2,1,0:T(8,128)(2,1)S(1)}, bf16[1,4,4,96,192]{4,3,2,1,0:T(8,128)(2,1)}, u32[]{:S(2)}) copy-start(bf16[1,4,4,96,192]{4,3,2,1,0:T(8,128)(2,1)} %param.5) | copy-start | bytes 1769476
  16.6 2.1 %copy-start.5 = (bf16[3,3,384,192]{2,3,1,0:T(8,128)(2,1)S(1)}, bf16[3,3,384,192]{2,3,1,0:T(8,128)(2,1)}, u32[]{:S(2)}) copy-start(bf16[3,3,384,192]{2,3,1,0:T(8,128)(2,1)} %param.7) | copy-start | bytes 3981316
  16.6 2.1 %copy-start.7 = (bf16[1,2,2,48,384]{4,3,2,1,0:T(8,128)(2,1)S(1)}, bf16[1,2,2,48,384]{4,3,2,1,0:T(8,128)(2,1)}, u32[]{:S(2)}) copy-start(bf16[1,2,2,48,384]{4,3,2,1,0:T(8,128)(2,1)} %param.4) | copy-start | bytes 442372
  22.8 6.7 %collective-permute-start.4 = (bf16[4,2,2,2,4,48,128]{6,5,4,3,2,1,0:T(8,128)(2,1)S(1)}, bf16[4,2,2,2,4,48,128]{6,5,4,3,2,1,0:T(8,128)(2,1)S(1)}, u32[]{:S(2)}, u32[]{:S(2)}) collective-permute-start(bf16[4,2,2,2,4,48,128]{6,5,4,3,2,1,0:T(8,128)(2,1)S(1)} %get-tuple-element.20), channel_id=1, source_target_pairs={{0,1},{1,0},{2,3},{3,2},{4,5},{5,4},{6,7},{7,6},{8,9},{9,8},{10,11... | collective-permute-start | bytes 4718600 | tf_op jit(solution)/shard_map/ppermute | solution.py:315
  79.1 20.8 %all-to-all-start.2 = ((bf16[16,48,128]{2,1,0:T(8,128)(2,1)}), bf16[16,48,128]{2,1,0:T(8,128)(2,1)S(1)}, u32[]{:S(2)}, u32[]{:S(2)}) async-start(bf16[16,48,128]{2,1,0:T(8,128)(2,1)} %group_sum.3), calls=%async_computation.2 | async-start | bytes 393216 | tf_op jit(solution)/shard_map/all_to_all | solution.py:336
  85.6 12.9 %collective-permute-start.3 = (bf16[192,768]{1,0:T(8,128)(2,1)S(1)}, bf16[192,768]{1,0:T(8,128)(2,1)S(1)}, u32[]{:S(2)}, u32[]{:S(2)}) collective-permute-start(bf16[192,768]{1,0:T(8,128)(2,1)S(1)} %get-tuple-element.18.own), channel_id=1, source_target_pairs={{64,0},{128,64},{192,128},{256,192},{320,256},{384,320},{448,384},... | collective-permute-start | bytes 884744 | tf_op jit(solution)/shard_map/ppermute | solution.py:316

commit v3 on v2

--- a/solution.py
+++ b/solution.py
@@ -38,56 +38,44 @@
     return jnp.where((col == first) | (col == first + 1), 1.0, 0.0).astype(BF16)
 
 
-def put(z, a, p, s, both):
-    start = (p * 2 * FRAMES + s) * COLS
+HALF = 2 * FRAMES * COLS
+
+
+def put(z, row, s, both):
     for c in range(3):
-        z[3 * a + c, start : start + COLS] = both[c * COLS : (c + 1) * COLS]
-
-
-HALF = 2 * FRAMES * COLS
-
-
-def edges_kernel(cot, top, bottom, sems):
+        z[row + c, s * COLS : (s + 1) * COLS] = both[c * COLS : (c + 1) * COLS]
+
+
+INNER, OUTER = ((0, 1), (1, 1), (0, 0), (1, 2)), ((0, 2), (1, 0))
+
+
+def taps(z, which, w_space):
+    sums = [0.0, 0.0]
+    for i, (p, a) in enumerate(which):
+        for c in range(3):
+            sums[p] = sums[p] + dot(z[3 * i + c], w_space[3 * a + c])
+    return sums
+
+
+def inner_kernel(cot_in, video_in, w_time_in, w_space_in, cot, video, w_time, w_space, inner, grad, hidden, sems):
     copies = [
-        pltpu.make_async_copy(cot.at[:, 2 * BAND - 1], bottom, sems.at[0]),
-        pltpu.make_async_copy(cot.at[:, 0], top, sems.at[1]),
+        pltpu.make_async_copy(source, target, sems.at[i])
+        for i, (source, target) in enumerate(
+            ((cot_in, cot), (w_space_in, w_space), (video_in, video), (w_time_in, w_time))
+        )
     ]
     for copy in copies:
         copy.start()
-    for copy in copies:
-        copy.wait()
-
-
-def edges(cot):
-    edge = jax.ShapeDtypeStruct((2 * FRAMES, 2 * COLS, CH_OUT), BF16)
-    return pl.pallas_call(
-        edges_kernel,
-        name="edges",
-        out_shape=(edge, edge),
-        in_specs=[pl.BlockSpec(memory_space=pl.ANY)],
-        out_specs=(VMEM, VMEM),
-        scratch_shapes=[pltpu.SemaphoreType.DMA((2,))],
-    )(cot)
-
-
-def inner_kernel(cot, video, w_time, w_space, z, grad, hidden):
     pick = picker()
+    copies[0].wait()
     for s in range(2 * FRAMES):
         reach = [dot(pick, cot[s, p]) for p in range(2 * BAND)]
-        for p in range(BAND):
-            put(z, 1, p, s, (reach[2 * p] + reach[2 * p + 1]).astype(BF16))
-        both = (reach[1] + reach[2]).astype(BF16)
-        put(z, 0, 0, s, both)
-        put(z, 2, 1, s, both)
-    total = dot(z[3], w_space[3])
-    for tap in (4, 5):
-        total = total + dot(z[tap], w_space[tap])
-    upper, lower = total[:HALF], total[HALF:]
-    for c in range(3):
-        upper = upper + dot(z[c, :HALF], w_space[c])
-        lower = lower + dot(z[6 + c, HALF:], w_space[6 + c])
-    grad[:HALF] = upper
-    grad[HALF:] = lower
+        for i, (p, a) in enumerate(INNER):
+            put(inner, 3 * i, s, (reach[2 * p + 1 - a] + reach[2 * p + 2 - a]).astype(BF16))
+    copies[1].wait()
+    grad[...] = jnp.concatenate(taps(inner, INNER, w_space))
+    copies[2].wait()
+    copies[3].wait()
     hidden[:CELLS] = dot(video[:CELLS], w_time[2])
     hidden[CELLS:] = dot(video[:CELLS], w_time[1]) + dot(video[CELLS:], w_time[2])
 
@@ -98,33 +86,26 @@
         inner_kernel,
         name="inner_terms",
         out_shape=(
-            jax.ShapeDtypeStruct((9, 2 * cells, CH_OUT), BF16),
+            *(jax.ShapeDtypeStruct(array.shape, BF16) for array in (cot, video, w_time, w_space)),
+            jax.ShapeDtypeStruct((3 * len(INNER), HALF, CH_OUT), BF16),
             jax.ShapeDtypeStruct((2 * cells, CH_IN), F32),
             jax.ShapeDtypeStruct((cells, 2 * CH_IN), F32),
         ),
-        in_specs=[VMEM] * 4,
-        out_specs=(VMEM,) * 3,
-        compiler_params=params(12),
+        in_specs=[pl.BlockSpec(memory_space=pltpu.HBM)] * 4,
+        out_specs=(VMEM,) * 7,
+        scratch_shapes=[pltpu.SemaphoreType.DMA((4,))],
+        compiler_params=params(16),
         cost_estimate=pl.CostEstimate(flops=1_500_000_000, bytes_accessed=6_000_000, transcendentals=0),
     )(cot, video, w_time, w_space)
 
 
-def block_kernel(
-    cot, low, high, video, carried, w_time, w_space, z_in, grad_in, hidden_in,
-    keep, send, grad_hidden, z,
-    ext, hid, time_acc, space_acc, line,
-):
-    ext[0 : FRAMES * CELLS] = carried[...]
-    ext[FRAMES * CELLS :] = video[...]
+def grad_kernel(cot, low, high, w_space, grad_in, grad_hidden, outer):
     pick = picker()
     for s in range(2 * FRAMES):
-        put(z, 2, 0, s, (dot(pick, low[s]) + dot(pick, cot[s, 0])).astype(BF16))
-        put(z, 0, 1, s, (dot(pick, cot[s, 2 * BAND - 1]) + dot(pick, high[s])).astype(BF16))
-    upper, lower = grad_in[:HALF], grad_in[HALF:]
-    for c in range(3):
-        upper = upper + dot(z[6 + c, :HALF], w_space[6 + c])
-        lower = lower + dot(z[c, HALF:], w_space[c])
-    for p, part in enumerate((upper, lower)):
+        put(outer, 0, s, (dot(pick, low[s, 0]) + dot(pick, cot[s, 0])).astype(BF16))
+        put(outer, 3, s, (dot(pick, cot[s, 2 * BAND - 1]) + dot(pick, high[s, 0])).astype(BF16))
+    for p, part in enumerate(taps(outer, OUTER, w_space)):
+        part = part + grad_in[p * HALF : (p + 1) * HALF]
         for t in range(FRAMES):
             for j in range(2):
                 s = 2 * t + j
@@ -132,6 +113,29 @@
                     s * COLS : (s + 1) * COLS
                 ].astype(BF16)
 
+
+def grad_terms(cot, low, high, w_space, grad):
+    return pl.pallas_call(
+        grad_kernel,
+        name="grad_terms",
+        out_shape=(
+            jax.ShapeDtypeStruct((FRAMES * CELLS, 2 * CH_IN), BF16),
+            jax.ShapeDtypeStruct((3 * len(OUTER), HALF, CH_OUT), BF16),
+        ),
+        in_specs=[VMEM] * 5,
+        out_specs=(VMEM,) * 2,
+        compiler_params=params(8),
+        cost_estimate=pl.CostEstimate(flops=800_000_000, bytes_accessed=4_000_000, transcendentals=0),
+    )(cot, low, high, w_space, grad)
+
+
+def block_kernel(
+    video, carried, w_time, inner, outer, grad_hidden, hidden_in,
+    keep, send,
+    ext, hid, time_acc, space_acc, line,
+):
+    ext[0 : FRAMES * CELLS] = carried[...]
+    ext[FRAMES * CELLS :] = video[...]
     first = hidden_in[:CELLS] + dot(carried[:CELLS], w_time[0]) + dot(carried[CELLS:], w_time[1])
     second = hidden_in[CELLS:] + dot(carried[CELLS:], w_time[0])
     for t, hidden in enumerate((first, second)):
@@ -144,9 +148,16 @@
 
     for k in range(3):
         time_acc[k * CH_IN : (k + 1) * CH_IN] = dot_t(ext[k * CELLS : (k + FRAMES) * CELLS], grad_hidden[...])
-    hid_t = hid[...].T
-    for tap in range(9):
-        space_acc[tap * CH_IN : (tap + 1) * CH_IN] = dot(hid_t, z[tap])
+    hid_t = [hid[p * HALF : (p + 1) * HALF].T for p in range(BAND)]
+    where = {key: (z, 3 * i) for z, order in ((inner, INNER), (outer, OUTER)) for i, key in enumerate(order)}
+    for a in range(3):
+        for c in range(3):
+            total = 0.0
+            for p in range(BAND):
+                z, row = where[p, a]
+                total = total + dot(hid_t[p], z[row + c])
+            tap = 3 * a + c
+            space_acc[tap * CH_IN : (tap + 1) * CH_IN] = total
 
     mine = lax.axis_index("clip")
     line[378:LINES] = jnp.zeros((6, LANES), F32)
@@ -169,21 +180,15 @@
                 send[x, c0, zl, c1, zh] = line[pl.ds(other, PIECE)].astype(BF16)
 
 
-def block_terms(cot, low, high, video, carried, w_time, w_space, z, grad, hidden):
+def block_terms(video, carried, w_time, inner, outer, grad_hidden, hidden):
     cells = FRAMES * CELLS
     half = jax.ShapeDtypeStruct((N_X, 2, 2, 2, N_Z // 2, PIECE, LANES), BF16)
     return pl.pallas_call(
         block_kernel,
         name="block_terms",
-        out_shape=(
-            half,
-            half,
-            jax.ShapeDtypeStruct((cells, 2 * CH_IN), BF16),
-            jax.ShapeDtypeStruct(z.shape, BF16),
-        ),
-        in_specs=[VMEM] * 10,
-        out_specs=(VMEM,) * 4,
-        input_output_aliases={7: 3},
+        out_shape=(half, half),
+        in_specs=[VMEM] * 7,
+        out_specs=(VMEM,) * 2,
         scratch_shapes=[
             pltpu.VMEM((2 * cells, CH_IN), BF16),
             pltpu.VMEM((2 * cells, CH_IN), BF16),
@@ -191,9 +196,9 @@
             pltpu.VMEM((9 * CH_IN, CH_OUT), F32),
             pltpu.VMEM((LINES, LANES), F32),
         ],
-        compiler_params=params(24),
-        cost_estimate=pl.CostEstimate(flops=2_500_000_000, bytes_accessed=10_000_000, transcendentals=0),
-    )(cot, low, high, video, carried, w_time, w_space, z, grad, hidden)
+        compiler_params=params(20),
+        cost_estimate=pl.CostEstimate(flops=3_000_000_000, bytes_accessed=12_000_000, transcendentals=0),
+    )(video, carried, w_time, inner, outer, grad_hidden, hidden)
 
 
 def pair_kernel(a, b, out):
@@ -306,14 +311,16 @@
     own = video[0].reshape(FRAMES * CELLS, CH_IN)
     rows, chain = lax.axis_size("rows"), lax.axis_size("chain")
     w_space = w_space.transpose(0, 1, 3, 2).reshape(9, CH_OUT, CH_IN)
-    top, bottom = edges(cot)
-    low = lax.ppermute(bottom, "rows", along("rows", 1))
-    high = lax.ppermute(top, "rows", along("rows", -1))
+    low = lax.ppermute(cot[:, 2 * BAND - 1 :], "rows", along("rows", 1))
+    high = lax.ppermute(cot[:, :1], "rows", along("rows", -1))
     carried = lax.ppermute(own, "chain", along("chain", 1))
-    inner = inner_terms(cot, own, w_time, w_space)
-    keep, send, grad_hidden, _ = block_terms(cot, low, high, own, carried, w_time, w_space, *inner)
+    operands = [pltpu.with_memory_space_constraint(value, pltpu.HBM) for value in (cot, own, w_time, w_space)]
+    cot, own, w_time, w_space, inner, grad, hidden = inner_terms(*operands)
+    grad_hidden, outer = grad_terms(cot, low, high, w_space, grad)
+    following = lax.ppermute(grad_hidden, "chain", along("chain", -1))
+    keep, send = block_terms(own, carried, w_time, inner, outer, grad_hidden, hidden)
     received = lax.ppermute(send, "clip", [(0, 1), (1, 0)])
-    following = lax.ppermute(grad_hidden, "chain", along("chain", -1))
+    received, following = lax.optimization_barrier((received, following))
 
     def device(c, x, z):
         return c * rows + x * N_Z + z

time: 102 us -> 101 us (level); the launches traced: 101 us -> 101 us
  local copies, waits for them, and re-layouts: 4.89 us -> 1.05 us
  waiting for transfers between devices: 15.2 us -> 18.2 us
  starting transfers between devices: 20.8 us -> 23.4 us
  blocking collectives: 48.2 us -> 47 us
    all_to_all x1, waiting for transfers between devices: 0.01 us -> 8.98 us  [local(): pieces = lax.all_to_all(share, ('chain', 'clip'), 0, 0, tiled=True)]
    unnamed x16 -> x0, local copies, waits for them, and re-layouts: 4.89 us -> none
    ppermute x1, waiting for transfers between devices: 3.01 us -> 0.01 us  [local(): received = lax.ppermute(send, 'clip', [(0, 1), (1, 0)])]
    ppermute x1, waiting for transfers between devices: 11.6 us -> 9.22 us  [local(): following = lax.ppermute(grad_hidden, 'chain', along('chain', -1))]
    ppermute x1, starting transfers between devices: 3.72 us -> 5.35 us  [local(): received = lax.ppermute(send, 'clip', [(0, 1), (1, 0)])]
    all_to_all x2, blocking collectives: 48.2 us -> 47 us  [exchange(): lax.all_to_all(parts, ('chain', 'rows'), 0, 0, tiled=True, axis_index_gro...]
    slice x0 -> x1, local copies, waits for them, and re-layouts: none -> 1.05 us  [local(): high = lax.ppermute(cot[:, :1], 'rows', along('rows', -1))]
  transfers between devices with their start and end apart: 6 -> 6, of which waited for: 3 -> 2; matrix products, arithmetic and copies ran while one was open for 0% -> 0% of each run, Pallas kernels for 5% -> 5%
where the time goes in v3:
time: 101 us
  blocking collectives  47 us (47%)
  starting transfers between devices  23.4 us (23%)
  waiting for transfers between devices  18.2 us (18%)
  Pallas kernels  10.6 us (10%)
  local copies, waits for them, and re-layouts  1.05 us (1%)
    all_to_all x2, blocking collectives, exchange(): lax.all_to_all(parts, ('chain', 'rows'), 0, 0, tiled=True, axis_index_gro...  47 us
    ppermute x1, waiting for transfers between devices, local(): following = lax.ppermute(grad_hidden, 'chain', along('chain', -1))  9.22 us
    all_to_all x1, waiting for transfers between devices, local(): pieces = lax.all_to_all(share, ('chain', 'clip'), 0, 0, tiled=True)  8.98 us
    all_to_all x1, starting transfers between devices, local(): pieces = lax.all_to_all(share, ('chain', 'clip'), 0, 0, tiled=True)  7.39 us
    ppermute x1, starting transfers between devices, local(): received = lax.ppermute(send, 'clip', [(0, 1), (1, 0)])  5.35 us
    ppermute x1, starting transfers between devices, local(): low = lax.ppermute(cot[:, 2 * BAND - 1:], 'rows', along('rows', 1))  4.84 us
    pallas_call x1, Pallas kernels, block_terms(): pl.pallas_call(block_kernel, name='block_terms', out_shape=(half, half),...  3.35 us
    ppermute x1, starting transfers between devices, local(): carried = lax.ppermute(own, 'chain', along('chain', 1))  3.21 us
  transfers between devices with their start and end apart: 6, of which 2 were waited for; matrix products, arithmetic and copies ran while one was open for 0% of the time, Pallas kernels for 5%

profile of v3, /device:TPU:1, one launch (start us, length us, event | category | flops | bytes accessed | tf_op | source)
XLA Modules:
  0.0 100.9 jit_solution(12540853798769945411)
XLA Ops:
  0.6 1.1 %fusion = (bf16[4,1,96,192]{3,2,1,0:T(8,128)(2,1)S(1)}, bf16[4,1,96,192]{3,2,1,0:T(8,128)(2,1)S(1)}) fusion(bf16[4,4,96,192]{3,2,1,0:T(8,128)(2,1)} %bitcast.15), kind=kLoop, calls=%fused_computation | loop fusion | bytes 589824 | tf_op jit(solution)/shard_map/slice | solution.py:315
  1.7 4.8 %collective-permute-start = (bf16[4,1,96,192]{3,2,1,0:T(8,128)(2,1)S(1)}, bf16[4,1,96,192]{3,2,1,0:T(8,128)(2,1)S(1)}, u32[]{:S(2)}, u32[]{:S(2)}) collective-permute-start(bf16[4,1,96,192]{3,2,1,0:T(8,128)(2,1)S(1)} %get-tuple-element.34), channel_id=1, source_target_pairs={{0,2},{2,4},{4,6},{6,8},{8,10},{10,12},{12,14},{14,16},{16,18},{18... | collective-permute-start | bytes 442376 | tf_op jit(solution)/shard_map/ppermute | solution.py:314
  6.5 1.3 %collective-permute-start.1 = (bf16[4,1,96,192]{3,2,1,0:T(8,128)(2,1)S(1)}, bf16[4,1,96,192]{3,2,1,0:T(8,128)(2,1)S(1)}, u32[]{:S(2)}, u32[]{:S(2)}) collective-permute-start(bf16[4,1,96,192]{3,2,1,0:T(8,128)(2,1)S(1)} %get-tuple-element.33), channel_id=1, source_target_pairs={{2,0},{4,2},{6,4},{8,6},{10,8},{12,10},{14,12},{16,14},{18,16},{20... | collective-permute-start | bytes 442376 | tf_op jit(solution)/shard_map/ppermute | solution.py:315
  7.8 3.2 %collective-permute-start.2 = (bf16[192,384]{1,0:T(8,128)(2,1)}, bf16[192,384]{1,0:T(8,128)(2,1)S(1)}, u32[]{:S(2)}, u32[]{:S(2)}) collective-permute-start(bf16[192,384]{1,0:T(8,128)(2,1)} %bitcast.19), channel_id=1, source_target_pairs={{0,64},{64,128},{128,192},{192,256},{256,320},{320,384},{384,448},... | collective-permute-start | bytes 442376 | tf_op jit(solution)/shard_map/ppermute | solution.py:316
  11.1 2.9 %inner_terms.1 = (bf16[4,4,96,192]{3,2,1,0:T(8,128)(2,1)S(1)}, bf16[192,384]{1,0:T(8,128)(2,1)S(1)}, bf16[3,384,768]{2,1,0:T(8,128)(2,1)S(1)}, bf16[9,192,384]{2...) custom-call(bf16[4,4,96,192]{3,2,1,0:T(8,128)(2,1)} %bitcast.16, ...), custom_call_target="tpu_custom_call" | custom-call | flops 1500000000 | bytes 6000000 | tf_op jit(solution)/shard_map/inner_terms/pallas_call | solution.py:85
  14.0 0.0 collective-permute-done.low
  14.0 0.0 collective-permute-done.1.high
  14.0 0.8 grad_terms.1
  14.8 0.0 collective-permute-done.2.carried
  14.8 3.3 %block_terms.1 = (bf16[4,2,2,2,4,48,128]{6,5,4,3,2,1,0:T(8,128)(2,1)S(1)}, bf16[4,2,2,2,4,48,128]{6,5,4,3,2,1,0:T(8,128)(2,1)S(1)}) custom-call(bf16[192,384]{1,0:T(8,128)(2,1)S(1)} %get-tuple-element.22.video, bf16[192,384]{1,0:T(8,128)(2,1)S(1)} %collective-permute-done.2.carried, bf16[3,384,768]{2,1,0:T(8,128)(2,1)S(1)} %get-tuple-element.23.w_time, ...), custom_call_target="tpu_custom_call" | custom-call | flops 3000000000 | bytes 12000000 | tf_op jit(solution)/shard_map/block_terms/pallas_call | solution.py:186
  18.2 5.4 %collective-permute-start.3 = (bf16[4,2,2,2,4,48,128]{6,5,4,3,2,1,0:T(8,128)(2,1)S(1)}, bf16[4,2,2,2,4,48,128]{6,5,4,3,2,1,0:T(8,128)(2,1)S(1)}, u32[]{:S(2)}, u32[]{:S(2)}) collective-permute-start(bf16[4,2,2,2,4,48,128]{6,5,4,3,2,1,0:T(8,128)(2,1)S(1)} %get-tuple-element.27), channel_id=1, source_target_pairs={{0,1},{1,0},{2,3},{3,2},{4,5},{5,4},{6,7},{7,6},{8,9},{9,8},{10,11... | collective-permute-start | bytes 4718600 | tf_op jit(solution)/shard_map/ppermute | solution.py:322
  23.6 1.3 %collective-permute-start.4 = (bf16[192,768]{1,0:T(8,128)(2,1)S(1)}, bf16[192,768]{1,0:T(8,128)(2,1)S(1)}, u32[]{:S(2)}, u32[]{:S(2)}) collective-permute-start(bf16[192,768]{1,0:T(8,128)(2,1)S(1)} %get-tuple-element.21.grad_hidden.own), channel_id=1, source_target_pairs={{64,0},{128,64},{192,128},{256,192},{320,256},{384,320},{448,384},... | collective-permute-start | bytes 884744 | tf_op jit(solution)/shard_map/ppermute | solution.py:320
  24.9 9.2 %collective-permute-done.4.following = bf16[192,768]{1,0:T(8,128)(2,1)S(1)} collective-permute-done((bf16[192,768]{1,0:T(8,128)(2,1)S(1)}, bf16[192,768]{1,0:T(8,128)(2,1)S(1)}, u32[]{:S(2)}, u32[]{:S(2)}) %collective-permute-start.4) | collective-permute-done | bytes 294944 | tf_op jit(solution)/shard_map/ppermute | solution.py:320
  34.1 0.0 collective-permute-done.3
  34.1 0.4 pair_sum.1
  34.4 30.0 %all_to_all.15.refs_0_ = bf16[16,384,128]{2,1,0:T(8,128)(2,1)S(1)} all-to-all(bf16[16,384,128]{2,1,0:T(8,128)(2,1)S(1)} %bitcast.11), channel_id=1, replica_groups={{0,2,64,66,16,18,80,82,32,34,96,98,48,50,112,114},{4,6,68,70,20,22,84,8..., dimensions={0} | all-to-all | bytes 3145728 | tf_op jit(solution)/shard_map/all_to_all | solution.py:306
  64.4 0.2 group_sum.2
  64.7 17.0 %all_to_all.16.refs_0_ = bf16[8,48,128]{2,1,0:T(8,128)(2,1)S(1)} all-to-all(bf16[8,48,128]{2,1,0:T(8,128)(2,1)S(1)} %bitcast.14), channel_id=1, replica_groups={{0,4,8,12,128,132,136,140},{2,6,10,14,130,134,138,142},{16,20,24,28,144..., dimensions={0} | all-to-all | bytes 196608 | tf_op jit(solution)/shard_map/all_to_all | solution.py:306
  81.6 0.7 group_sum.3
  82.3 7.4 %all-to-all-start.2 = ((bf16[16,48,128]{2,1,0:T(8,128)(2,1)}), bf16[16,48,128]{2,1,0:T(8,128)(2,1)S(1)}, u32[]{:S(2)}, u32[]{:S(2)}) async-start(bf16[16,48,128]{2,1,0:T(8,128)(2,1)} %group_sum.3), calls=%async_computation.2 | async-start | bytes 393216 | tf_op jit(solution)/shard_map/all_to_all | solution.py:343
  89.7 1.4 %video_grad.1 = bf16[192,384]{1,0:T(8,128)(2,1)} custom-call(bf16[192,768]{1,0:T(8,128)(2,1)S(1)} %get-tuple-element.21.grad_hidden.own, bf16[192,768]{1,0:T(8,128)(2,1)S(1)} %collective-permute-done.4.following, bf16[3,384,768]{2,1,0:T(8,128)(2,1)S(1)} %get-tuple-element.23.w_time), custom_call_target="tpu_custom_call" | custom-call | flops 350000000 | bytes 2500000 | tf_op jit(solution)/shard_map/video_grad/pallas_call | solution.py:289
  91.1 9.0 %all-to-all-done.2.refs_0_ = bf16[16,48,128]{2,1,0:T(8,128)(2,1)S(1)} async-done(((bf16[16,48,128]{2,1,0:T(8,128)(2,1)}), bf16[16,48,128]{2,1,0:T(8,128)(2,1)S(1)}, u32[]{:S(2)}, u32[]{:S(2)}) %all-to-all-start.2) | async-done | bytes 196640 | tf_op jit(solution)/shard_map/all_to_all | solution.py:343
  100.1 0.8 unpack.1
Async XLA Ops:
  1.7 12.3 %collective-permute-start = (bf16[4,1,96,192]{3,2,1,0:T(8,128)(2,1)S(1)}, bf16[4,1,96,192]{3,2,1,0:T(8,128)(2,1)S(1)}, u32[]{:S(2)}, u32[]{:S(2)}) collective-permute-start(bf16[4,1,96,192]{3,2,1,0:T(8,128)(2,1)S(1)} %get-tuple-element.34), channel_id=1, source_target_pairs={{0,2},{2,4},{4,6},{6,8},{8,10},{10,12},{12,14},{14,16},{16,18},{18... | collective-permute-start | bytes 442376 | tf_op jit(solution)/shard_map/ppermute | solution.py:314
  6.5 7.4 %collective-permute-start.1 = (bf16[4,1,96,192]{3,2,1,0:T(8,128)(2,1)S(1)}, bf16[4,1,96,192]{3,2,1,0:T(8,128)(2,1)S(1)}, u32[]{:S(2)}, u32[]{:S(2)}) collective-permute-start(bf16[4,1,96,192]{3,2,1,0:T(8,128)(2,1)S(1)} %get-tuple-element.33), channel_id=1, source_target_pairs={{2,0},{4,2},{6,4},{8,6},{10,8},{12,10},{14,12},{16,14},{18,16},{20... | collective-permute-start | bytes 442376 | tf_op jit(solution)/shard_map/ppermute | solution.py:315
  7.8 7.0 %collective-permute-start.2 = (bf16[192,384]{1,0:T(8,128)(2,1)}, bf16[192,384]{1,0:T(8,128)(2,1)S(1)}, u32[]{:S(2)}, u32[]{:S(2)}) collective-permute-start(bf16[192,384]{1,0:T(8,128)(2,1)} %bitcast.19), channel_id=1, source_target_pairs={{0,64},{64,128},{128,192},{192,256},{256,320},{320,384},{384,448},... | collective-permute-start | bytes 442376 | tf_op jit(solution)/shard_map/ppermute | solution.py:316
  18.2 15.9 %collective-permute-start.3 = (bf16[4,2,2,2,4,48,128]{6,5,4,3,2,1,0:T(8,128)(2,1)S(1)}, bf16[4,2,2,2,4,48,128]{6,5,4,3,2,1,0:T(8,128)(2,1)S(1)}, u32[]{:S(2)}, u32[]{:S(2)}) collective-permute-start(bf16[4,2,2,2,4,48,128]{6,5,4,3,2,1,0:T(8,128)(2,1)S(1)} %get-tuple-element.27), channel_id=1, source_target_pairs={{0,1},{1,0},{2,3},{3,2},{4,5},{5,4},{6,7},{7,6},{8,9},{9,8},{10,11... | collective-permute-start | bytes 4718600 | tf_op jit(solution)/shard_map/ppermute | solution.py:322
  23.6 10.5 %collective-permute-start.4 = (bf16[192,768]{1,0:T(8,128)(2,1)S(1)}, bf16[192,768]{1,0:T(8,128)(2,1)S(1)}, u32[]{:S(2)}, u32[]{:S(2)}) collective-permute-start(bf16[192,768]{1,0:T(8,128)(2,1)S(1)} %get-tuple-element.21.grad_hidden.own), channel_id=1, source_target_pairs={{64,0},{128,64},{192,128},{256,192},{320,256},{384,320},{448,384},... | collective-permute-start | bytes 884744 | tf_op jit(solution)/shard_map/ppermute | solution.py:320
  82.3 17.8 %all-to-all-start.2 = ((bf16[16,48,128]{2,1,0:T(8,128)(2,1)}), bf16[16,48,128]{2,1,0:T(8,128)(2,1)S(1)}, u32[]{:S(2)}, u32[]{:S(2)}) async-start(bf16[16,48,128]{2,1,0:T(8,128)(2,1)} %group_sum.3), calls=%async_computation.2 | async-start | bytes 393216 | tf_op jit(solution)/shard_map/all_to_all | solution.py:343

commit v4 on v3

--- a/solution.py
+++ b/solution.py
@@ -320,7 +320,6 @@
     following = lax.ppermute(grad_hidden, "chain", along("chain", -1))
     keep, send = block_terms(own, carried, w_time, inner, outer, grad_hidden, hidden)
     received = lax.ppermute(send, "clip", [(0, 1), (1, 0)])
-    received, following = lax.optimization_barrier((received, following))
 
     def device(c, x, z):
         return c * rows + x * N_Z + z
@@ -338,7 +337,8 @@
         for zl in range(2)
     ]
     share = pair_sum(keep.reshape(-1, LANES), received.reshape(-1, LANES))
-    share = group_sum(exchange(share.reshape(4 * N_X, -1, LANES), near))
+    share, following = lax.optimization_barrier((exchange(share.reshape(4 * N_X, -1, LANES), near), following))
+    share = group_sum(share)
     share = group_sum(exchange(share.reshape(N_Z, PIECE, LANES), far), 2 * chain)
     pieces = lax.all_to_all(share, ("chain", "clip"), 0, 0, tiled=True)
     voxels = 2 * chain * 2 * FRAMES * rows * 2 * BAND * 2 * COLS

time: 101 us -> 99.6 us (0.986)
  blocking collectives: 47 us -> 15.9 us
  waiting for transfers between devices: 18.2 us -> 33.9 us
  starting transfers between devices: 23.4 us -> 33.2 us
  local copies, waits for them, and re-layouts: 1.05 us -> 3.7 us
  Pallas kernels: 10.6 us -> 11.7 us
    all_to_all x2 -> x1, blocking collectives: 47 us -> 15.9 us  [exchange(): lax.all_to_all(parts, ('chain', 'rows'), 0, 0, tiled=True, axis_index_gro...]
    ppermute x1, waiting for transfers between devices: 9.22 us -> 23.9 us  [local(): following = lax.ppermute(grad_hidden, 'chain', along('chain', -1))]
    all_to_all x0 -> x1, starting transfers between devices: none -> 10.3 us  [exchange(): lax.all_to_all(parts, ('chain', 'rows'), 0, 0, tiled=True, axis_index_gro...]
    ppermute x1, waiting for transfers between devices: 0.01 us -> 3.01 us  [local(): received = lax.ppermute(send, 'clip', [(0, 1), (1, 0)])]
    unnamed x0 -> x8, local copies, waits for them, and re-layouts: none -> 2.64 us
    all_to_all x1, waiting for transfers between devices: 8.98 us -> 7 us  [local(): pieces = lax.all_to_all(share, ('chain', 'clip'), 0, 0, tiled=True)]
    pallas_call x1, Pallas kernels: 0.36 us -> 1.53 us  [pair_sum(): pl.pallas_call(pair_kernel, name='pair_sum', out_shape=jax.ShapeDtypeStru...]
  transfers between devices with their start and end apart: 6 -> 7, of which waited for: 2 -> 3; matrix products, arithmetic and copies ran while one was open for 0% -> 0% of each run, Pallas kernels for 5% -> 5%
where the time goes in v4:
time: 99.6 us; the launch traced here: 99.2 us
  waiting for transfers between devices  33.9 us (34%)
  starting transfers between devices  33.2 us (33%)
  blocking collectives  15.9 us (16%)
  Pallas kernels  11.7 us (12%)
  local copies, waits for them, and re-layouts  3.7 us (4%)
    ppermute x1, waiting for transfers between devices, local(): following = lax.ppermute(grad_hidden, 'chain', along('chain', -1))  23.9 us
    all_to_all x1, blocking collectives, exchange(): lax.all_to_all(parts, ('chain', 'rows'), 0, 0, tiled=True, axis_index_gro...  15.9 us
    all_to_all x1, starting transfers between devices, exchange(): lax.all_to_all(parts, ('chain', 'rows'), 0, 0, tiled=True, axis_index_gro...  10.3 us
    all_to_all x1, waiting for transfers between devices, local(): pieces = lax.all_to_all(share, ('chain', 'clip'), 0, 0, tiled=True)  7 us
    all_to_all x1, starting transfers between devices, local(): pieces = lax.all_to_all(share, ('chain', 'clip'), 0, 0, tiled=True)  6.91 us
    ppermute x1, starting transfers between devices, local(): received = lax.ppermute(send, 'clip', [(0, 1), (1, 0)])  5.35 us
    ppermute x1, starting transfers between devices, local(): low = lax.ppermute(cot[:, 2 * BAND - 1:], 'rows', along('rows', 1))  4.84 us
    pallas_call x1, Pallas kernels, block_terms(): pl.pallas_call(block_kernel, name='block_terms', out_shape=(half, half),...  3.34 us
  transfers between devices with their start and end apart: 7, of which 3 were waited for; matrix products, arithmetic and copies ran while one was open for 0% of the time, Pallas kernels for 5%

profile of v4, /device:TPU:1, one launch (start us, length us, event | category | flops | bytes accessed | tf_op | source)
XLA Modules:
  0.0 99.2 jit_solution(1326382818128891912)
XLA Ops:
  0.6 1.1 %fusion = (bf16[4,1,96,192]{3,2,1,0:T(8,128)(2,1)S(1)}, bf16[4,1,96,192]{3,2,1,0:T(8,128)(2,1)S(1)}) fusion(bf16[4,4,96,192]{3,2,1,0:T(8,128)(2,1)} %bitcast.14), kind=kLoop, calls=%fused_computation | loop fusion | bytes 589824 | tf_op jit(solution)/shard_map/slice | solution.py:315
  1.7 4.8 %collective-permute-start = (bf16[4,1,96,192]{3,2,1,0:T(8,128)(2,1)S(1)}, bf16[4,1,96,192]{3,2,1,0:T(8,128)(2,1)S(1)}, u32[]{:S(2)}, u32[]{:S(2)}) collective-permute-start(bf16[4,1,96,192]{3,2,1,0:T(8,128)(2,1)S(1)} %get-tuple-element.34), channel_id=1, source_target_pairs={{0,2},{2,4},{4,6},{6,8},{8,10},{10,12},{12,14},{14,16},{16,18},{18... | collective-permute-start | bytes 442376 | tf_op jit(solution)/shard_map/ppermute | solution.py:314
  6.5 1.3 %collective-permute-start.1 = (bf16[4,1,96,192]{3,2,1,0:T(8,128)(2,1)S(1)}, bf16[4,1,96,192]{3,2,1,0:T(8,128)(2,1)S(1)}, u32[]{:S(2)}, u32[]{:S(2)}) collective-permute-start(bf16[4,1,96,192]{3,2,1,0:T(8,128)(2,1)S(1)} %get-tuple-element.33), channel_id=1, source_target_pairs={{2,0},{4,2},{6,4},{8,6},{10,8},{12,10},{14,12},{16,14},{18,16},{20... | collective-permute-start | bytes 442376 | tf_op jit(solution)/shard_map/ppermute | solution.py:315
  7.8 3.2 %collective-permute-start.2 = (bf16[192,384]{1,0:T(8,128)(2,1)}, bf16[192,384]{1,0:T(8,128)(2,1)S(1)}, u32[]{:S(2)}, u32[]{:S(2)}) collective-permute-start(bf16[192,384]{1,0:T(8,128)(2,1)} %bitcast.18), channel_id=1, source_target_pairs={{0,64},{64,128},{128,192},{192,256},{256,320},{320,384},{384,448},... | collective-permute-start | bytes 442376 | tf_op jit(solution)/shard_map/ppermute | solution.py:316
  11.1 2.9 %inner_terms.1 = (bf16[4,4,96,192]{3,2,1,0:T(8,128)(2,1)S(1)}, bf16[192,384]{1,0:T(8,128)(2,1)S(1)}, bf16[3,384,768]{2,1,0:T(8,128)(2,1)S(1)}, bf16[9,192,384]{2...) custom-call(bf16[4,4,96,192]{3,2,1,0:T(8,128)(2,1)} %bitcast.15, ...), custom_call_target="tpu_custom_call" | custom-call | flops 1500000000 | bytes 6000000 | tf_op jit(solution)/shard_map/inner_terms/pallas_call | solution.py:85
  14.0 0.0 collective-permute-done.low
  14.0 0.0 collective-permute-done.1.high
  14.0 0.8 grad_terms.1
  14.8 0.0 copy-start
  14.8 0.0 collective-permute-done.2.carried
  14.9 3.3 %block_terms.1 = (bf16[4,2,2,2,4,48,128]{6,5,4,3,2,1,0:T(8,128)(2,1)S(1)}, bf16[4,2,2,2,4,48,128]{6,5,4,3,2,1,0:T(8,128)(2,1)S(1)}) custom-call(bf16[192,384]{1,0:T(8,128)(2,1)S(1)} %get-tuple-element.22.video, bf16[192,384]{1,0:T(8,128)(2,1)S(1)} %collective-permute-done.2.carried, bf16[3,384,768]{2,1,0:T(8,128)(2,1)S(1)} %get-tuple-element.23.w_time, ...), custom_call_target="tpu_custom_call" | custom-call | flops 3000000000 | bytes 12000000 | tf_op jit(solution)/shard_map/block_terms/pallas_call | solution.py:186
  18.2 0.0 copy-done
  18.2 5.4 %collective-permute-start.3 = (bf16[4,2,2,2,4,48,128]{6,5,4,3,2,1,0:T(8,128)(2,1)S(1)}, bf16[4,2,2,2,4,48,128]{6,5,4,3,2,1,0:T(8,128)(2,1)S(1)}, u32[]{:S(2)}, u32[]{:S(2)}) collective-permute-start(bf16[4,2,2,2,4,48,128]{6,5,4,3,2,1,0:T(8,128)(2,1)S(1)} %get-tuple-element.28), channel_id=1, source_target_pairs={{0,1},{1,0},{2,3},{3,2},{4,5},{5,4},{6,7},{7,6},{8,9},{9,8},{10,11... | collective-permute-start | bytes 4718600 | tf_op jit(solution)/shard_map/ppermute | solution.py:322
  23.6 3.0 %collective-permute-done.3 = bf16[4,2,2,2,4,48,128]{6,5,4,3,2,1,0:T(8,128)(2,1)S(1)} collective-permute-done((bf16[4,2,2,2,4,48,128]{6,5,4,3,2,1,0:T(8,128)(2,1)S(1)}, bf16[4,2,2,2,4,48,128]{6,5,4,3,2,1,0:T(8,128)(2,1)S(1)}, u32[]{:S(2)}, u32[]{:S(2)}) %collective-permute-start.3) | collective-permute-done | bytes 1572896 | tf_op jit(solution)/shard_map/ppermute | solution.py:322
  26.6 1.5 %pair_sum.1 = bf16[6144,128]{1,0:T(8,128)(2,1)} custom-call(bf16[6144,128]{1,0:T(8,128)(2,1)S(1)} %bitcast.11, bf16[6144,128]{1,0:T(8,128)(2,1)S(1)} %bitcast.12), custom_call_target="tpu_custom_call" | custom-call | tf_op jit(solution)/shard_map/pair_sum/pallas_call | solution.py:209
  28.1 10.3 %all-to-all-start = ((bf16[16,384,128]{2,1,0:T(8,128)(2,1)}), bf16[16,384,128]{2,1,0:T(8,128)(2,1)S(1)}, u32[]{:S(2)}, u32[]{:S(2)}) async-start(bf16[16,384,128]{2,1,0:T(8,128)(2,1)} %bitcast.6), calls=%async_computation | async-start | bytes 3145728 | tf_op jit(solution)/shard_map/all_to_all | solution.py:306
  38.4 1.3 %collective-permute-start.4 = (bf16[192,768]{1,0:T(8,128)(2,1)}, bf16[192,768]{1,0:T(8,128)(2,1)S(1)}, u32[]{:S(2)}, u32[]{:S(2)}) collective-permute-start(bf16[192,768]{1,0:T(8,128)(2,1)} %copy-done), channel_id=1, source_target_pairs={{64,0},{128,64},{192,128},{256,192},{320,256},{384,320},{448,384},... | collective-permute-start | bytes 884744 | tf_op jit(solution)/shard_map/ppermute | solution.py:320
  39.7 23.9 %collective-permute-done.4.following = bf16[192,768]{1,0:T(8,128)(2,1)S(1)} collective-permute-done((bf16[192,768]{1,0:T(8,128)(2,1)}, bf16[192,768]{1,0:T(8,128)(2,1)S(1)}, u32[]{:S(2)}, u32[]{:S(2)}) %collective-permute-start.4) | collective-permute-done | bytes 294944 | tf_op jit(solution)/shard_map/ppermute | solution.py:320
  63.6 0.0 copy-start.2
  63.6 0.7 copy-done.2
  64.3 0.0 all-to-all-done.refs_0_
  64.3 0.2 group_sum.2
  64.6 15.9 %all_to_all.15.refs_0_ = bf16[8,48,128]{2,1,0:T(8,128)(2,1)S(1)} all-to-all(bf16[8,48,128]{2,1,0:T(8,128)(2,1)S(1)} %bitcast.13), channel_id=1, replica_groups={{0,4,8,12,128,132,136,140},{2,6,10,14,130,134,138,142},{16,20,24,28,144..., dimensions={0} | all-to-all | bytes 196608 | tf_op jit(solution)/shard_map/all_to_all | solution.py:306
  80.4 0.7 group_sum.3
  81.1 6.9 %all-to-all-start.2 = ((bf16[16,48,128]{2,1,0:T(8,128)(2,1)}), bf16[16,48,128]{2,1,0:T(8,128)(2,1)S(1)}, u32[]{:S(2)}, u32[]{:S(2)}) async-start(bf16[16,48,128]{2,1,0:T(8,128)(2,1)} %group_sum.3), calls=%async_computation.2 | async-start | bytes 393216 | tf_op jit(solution)/shard_map/all_to_all | solution.py:343
  88.0 0.0 copy-start.1
  88.0 1.0 copy-done.1
  89.0 0.0 copy-start.3
  89.0 1.0 copy-done.3
  89.9 1.4 %video_grad.1 = bf16[192,384]{1,0:T(8,128)(2,1)} custom-call(bf16[192,768]{1,0:T(8,128)(2,1)S(1)} %copy-done.1, bf16[192,768]{1,0:T(8,128)(2,1)S(1)} %copy-done.3, bf16[3,384,768]{2,1,0:T(8,128)(2,1)S(1)} %get-tuple-element.23.w_time), custom_call_target="tpu_custom_call" | custom-call | flops 350000000 | bytes 2500000 | tf_op jit(solution)/shard_map/video_grad/pallas_call | solution.py:289
  91.3 7.0 %all-to-all-done.2.refs_0_ = bf16[16,48,128]{2,1,0:T(8,128)(2,1)S(1)} async-done(((bf16[16,48,128]{2,1,0:T(8,128)(2,1)}), bf16[16,48,128]{2,1,0:T(8,128)(2,1)S(1)}, u32[]{:S(2)}, u32[]{:S(2)}) %all-to-all-start.2) | async-done | bytes 196640 | tf_op jit(solution)/shard_map/all_to_all | solution.py:343
  98.3 0.8 unpack.1
Async XLA Ops:
  1.7 12.3 %collective-permute-start = (bf16[4,1,96,192]{3,2,1,0:T(8,128)(2,1)S(1)}, bf16[4,1,96,192]{3,2,1,0:T(8,128)(2,1)S(1)}, u32[]{:S(2)}, u32[]{:S(2)}) collective-permute-start(bf16[4,1,96,192]{3,2,1,0:T(8,128)(2,1)S(1)} %get-tuple-element.34), channel_id=1, source_target_pairs={{0,2},{2,4},{4,6},{6,8},{8,10},{10,12},{12,14},{14,16},{16,18},{18... | collective-permute-start | bytes 442376 | tf_op jit(solution)/shard_map/ppermute | solution.py:314
  6.5 7.4 %collective-permute-start.1 = (bf16[4,1,96,192]{3,2,1,0:T(8,128)(2,1)S(1)}, bf16[4,1,96,192]{3,2,1,0:T(8,128)(2,1)S(1)}, u32[]{:S(2)}, u32[]{:S(2)}) collective-permute-start(bf16[4,1,96,192]{3,2,1,0:T(8,128)(2,1)S(1)} %get-tuple-element.33), channel_id=1, source_target_pairs={{2,0},{4,2},{6,4},{8,6},{10,8},{12,10},{14,12},{16,14},{18,16},{20... | collective-permute-start | bytes 442376 | tf_op jit(solution)/shard_map/ppermute | solution.py:315
  7.8 7.0 %collective-permute-start.2 = (bf16[192,384]{1,0:T(8,128)(2,1)}, bf16[192,384]{1,0:T(8,128)(2,1)S(1)}, u32[]{:S(2)}, u32[]{:S(2)}) collective-permute-start(bf16[192,384]{1,0:T(8,128)(2,1)} %bitcast.18), channel_id=1, source_target_pairs={{0,64},{64,128},{128,192},{192,256},{256,320},{320,384},{384,448},... | collective-permute-start | bytes 442376 | tf_op jit(solution)/shard_map/ppermute | solution.py:316
  14.8 3.4 %copy-start = (bf16[192,768]{1,0:T(8,128)(2,1)}, bf16[192,768]{1,0:T(8,128)(2,1)S(1)}, u32[]{:S(2)}) copy-start(bf16[192,768]{1,0:T(8,128)(2,1)S(1)} %get-tuple-element.21.grad_hidden.own) | copy-start | bytes 884740
  18.2 8.4 %collective-permute-start.3 = (bf16[4,2,2,2,4,48,128]{6,5,4,3,2,1,0:T(8,128)(2,1)S(1)}, bf16[4,2,2,2,4,48,128]{6,5,4,3,2,1,0:T(8,128)(2,1)S(1)}, u32[]{:S(2)}, u32[]{:S(2)}) collective-permute-start(bf16[4,2,2,2,4,48,128]{6,5,4,3,2,1,0:T(8,128)(2,1)S(1)} %get-tuple-element.28), channel_id=1, source_target_pairs={{0,1},{1,0},{2,3},{3,2},{4,5},{5,4},{6,7},{7,6},{8,9},{9,8},{10,11... | collective-permute-start | bytes 4718600 | tf_op jit(solution)/shard_map/ppermute | solution.py:322
  28.1 36.2 %all-to-all-start = ((bf16[16,384,128]{2,1,0:T(8,128)(2,1)}), bf16[16,384,128]{2,1,0:T(8,128)(2,1)S(1)}, u32[]{:S(2)}, u32[]{:S(2)}) async-start(bf16[16,384,128]{2,1,0:T(8,128)(2,1)} %bitcast.6), calls=%async_computation | async-start | bytes 3145728 | tf_op jit(solution)/shard_map/all_to_all | solution.py:306
  38.4 25.2 %collective-permute-start.4 = (bf16[192,768]{1,0:T(8,128)(2,1)}, bf16[192,768]{1,0:T(8,128)(2,1)S(1)}, u32[]{:S(2)}, u32[]{:S(2)}) collective-permute-start(bf16[192,768]{1,0:T(8,128)(2,1)} %copy-done), channel_id=1, source_target_pairs={{64,0},{128,64},{192,128},{256,192},{320,256},{384,320},{448,384},... | collective-permute-start | bytes 884744 | tf_op jit(solution)/shard_map/ppermute | solution.py:320
  63.6 0.7 copy-start.2
  81.1 17.2 %all-to-all-start.2 = ((bf16[16,48,128]{2,1,0:T(8,128)(2,1)}), bf16[16,48,128]{2,1,0:T(8,128)(2,1)S(1)}, u32[]{:S(2)}, u32[]{:S(2)}) async-start(bf16[16,48,128]{2,1,0:T(8,128)(2,1)} %group_sum.3), calls=%async_computation.2 | async-start | bytes 393216 | tf_op jit(solution)/shard_map/all_to_all | solution.py:343
  88.0 1.0 copy-start.1
  89.0 1.0 copy-start.3

commit v5 on v3

--- a/solution.py
+++ b/solution.py
@@ -317,10 +317,8 @@
     operands = [pltpu.with_memory_space_constraint(value, pltpu.HBM) for value in (cot, own, w_time, w_space)]
     cot, own, w_time, w_space, inner, grad, hidden = inner_terms(*operands)
     grad_hidden, outer = grad_terms(cot, low, high, w_space, grad)
-    following = lax.ppermute(grad_hidden, "chain", along("chain", -1))
     keep, send = block_terms(own, carried, w_time, inner, outer, grad_hidden, hidden)
     received = lax.ppermute(send, "clip", [(0, 1), (1, 0)])
-    received, following = lax.optimization_barrier((received, following))
 
     def device(c, x, z):
         return c * rows + x * N_Z + z
@@ -339,7 +337,10 @@
     ]
     share = pair_sum(keep.reshape(-1, LANES), received.reshape(-1, LANES))
     share = group_sum(exchange(share.reshape(4 * N_X, -1, LANES), near))
-    share = group_sum(exchange(share.reshape(N_Z, PIECE, LANES), far), 2 * chain)
+    share, grad_hidden = lax.optimization_barrier((share, grad_hidden))
+    following = lax.ppermute(grad_hidden, "chain", along("chain", -1))
+    share, following = lax.optimization_barrier((exchange(share.reshape(N_Z, PIECE, LANES), far), following))
+    share = group_sum(share, 2 * chain)
     pieces = lax.all_to_all(share, ("chain", "clip"), 0, 0, tiled=True)
     voxels = 2 * chain * 2 * FRAMES * rows * 2 * BAND * 2 * COLS
     grad_time, grad_space = unpack(pieces, 1.0 / math.sqrt(voxels))

time: 101 us -> 98.9 us (0.979)
  waiting for transfers between devices: 18.2 us -> 12 us
  starting transfers between devices: 23.4 us -> 26.4 us
    ppermute x1, waiting for transfers between devices: 9.22 us -> 0.01 us  [local(): following = lax.ppermute(grad_hidden, 'chain', along('chain', -1))]
    ppermute x1, waiting for transfers between devices: 0.01 us -> 3.01 us  [local(): received = lax.ppermute(send, 'clip', [(0, 1), (1, 0)])]
    all_to_all x1, starting transfers between devices: 7.39 us -> 9.2 us  [local(): pieces = lax.all_to_all(share, ('chain', 'clip'), 0, 0, tiled=True)]
where the time goes in v5:
time: 98.9 us; the launch traced here: 98.5 us
  blocking collectives  47.8 us (48%)
  starting transfers between devices  26.4 us (27%)
  waiting for transfers between devices  12 us (12%)
  Pallas kernels  10.6 us (11%)
  local copies, waits for them, and re-layouts  1.05 us (1%)
    all_to_all x2, blocking collectives, exchange(): lax.all_to_all(parts, ('chain', 'rows'), 0, 0, tiled=True, axis_index_gro...  47.8 us
    all_to_all x1, starting transfers between devices, local(): pieces = lax.all_to_all(share, ('chain', 'clip'), 0, 0, tiled=True)  9.2 us
    all_to_all x1, waiting for transfers between devices, local(): pieces = lax.all_to_all(share, ('chain', 'clip'), 0, 0, tiled=True)  8.93 us
    ppermute x1, starting transfers between devices, local(): received = lax.ppermute(send, 'clip', [(0, 1), (1, 0)])  5.95 us
    ppermute x1, starting transfers between devices, local(): low = lax.ppermute(cot[:, 2 * BAND - 1:], 'rows', along('rows', 1))  5.47 us
    pallas_call x1, Pallas kernels, block_terms(): pl.pallas_call(block_kernel, name='block_terms', out_shape=(half, half),...  3.35 us
    ppermute x1, starting transfers between devices, local(): carried = lax.ppermute(own, 'chain', along('chain', 1))  3.21 us
    ppermute x1, waiting for transfers between devices, local(): received = lax.ppermute(send, 'clip', [(0, 1), (1, 0)])  3.01 us
  transfers between devices with their start and end apart: 6, of which 2 were waited for; matrix products, arithmetic and copies ran while one was open for 0% of the time, Pallas kernels for 5%

profile of v5, /device:TPU:1, one launch (start us, length us, event | category | flops | bytes accessed | tf_op | source)
XLA Modules:
  0.0 98.5 jit_solution(7347912916415206091)
XLA Ops:
  0.6 1.1 %fusion = (bf16[4,1,96,192]{3,2,1,0:T(8,128)(2,1)S(1)}, bf16[4,1,96,192]{3,2,1,0:T(8,128)(2,1)S(1)}) fusion(bf16[4,4,96,192]{3,2,1,0:T(8,128)(2,1)} %bitcast.15), kind=kLoop, calls=%fused_computation | loop fusion | bytes 589824 | tf_op jit(solution)/shard_map/slice | solution.py:315
  1.7 1.3 %collective-permute-start.2 = (bf16[4,1,96,192]{3,2,1,0:T(8,128)(2,1)S(1)}, bf16[4,1,96,192]{3,2,1,0:T(8,128)(2,1)S(1)}, u32[]{:S(2)}, u32[]{:S(2)}) collective-permute-start(bf16[4,1,96,192]{3,2,1,0:T(8,128)(2,1)S(1)} %get-tuple-element.37), channel_id=1, source_target_pairs={{2,0},{4,2},{6,4},{8,6},{10,8},{12,10},{14,12},{16,14},{18,16},{20... | collective-permute-start | bytes 442376 | tf_op jit(solution)/shard_map/ppermute | solution.py:315
  3.0 5.5 %collective-permute-start.1 = (bf16[4,1,96,192]{3,2,1,0:T(8,128)(2,1)S(1)}, bf16[4,1,96,192]{3,2,1,0:T(8,128)(2,1)S(1)}, u32[]{:S(2)}, u32[]{:S(2)}) collective-permute-start(bf16[4,1,96,192]{3,2,1,0:T(8,128)(2,1)S(1)} %get-tuple-element.38), channel_id=1, source_target_pairs={{0,2},{2,4},{4,6},{6,8},{8,10},{10,12},{12,14},{14,16},{16,18},{18... | collective-permute-start | bytes 442376 | tf_op jit(solution)/shard_map/ppermute | solution.py:314
  8.5 3.2 %collective-permute-start = (bf16[192,384]{1,0:T(8,128)(2,1)}, bf16[192,384]{1,0:T(8,128)(2,1)S(1)}, u32[]{:S(2)}, u32[]{:S(2)}) collective-permute-start(bf16[192,384]{1,0:T(8,128)(2,1)} %bitcast.19), channel_id=1, source_target_pairs={{0,64},{64,128},{128,192},{192,256},{256,320},{320,384},{384,448},... | collective-permute-start | bytes 442376 | tf_op jit(solution)/shard_map/ppermute | solution.py:316
  11.7 2.9 %inner_terms.1 = (bf16[4,4,96,192]{3,2,1,0:T(8,128)(2,1)S(1)}, bf16[192,384]{1,0:T(8,128)(2,1)S(1)}, bf16[3,384,768]{2,1,0:T(8,128)(2,1)S(1)}, bf16[9,192,384]{2...) custom-call(bf16[4,4,96,192]{3,2,1,0:T(8,128)(2,1)} %bitcast.16, ...), custom_call_target="tpu_custom_call" | custom-call | flops 1500000000 | bytes 6000000 | tf_op jit(solution)/shard_map/inner_terms/pallas_call | solution.py:85
  14.6 0.0 collective-permute-done.2.high
  14.6 0.0 collective-permute-done.1.low
  14.6 0.8 grad_terms.1
  15.5 0.0 collective-permute-done.carried
  15.5 3.3 %block_terms.1 = (bf16[4,2,2,2,4,48,128]{6,5,4,3,2,1,0:T(8,128)(2,1)S(1)}, bf16[4,2,2,2,4,48,128]{6,5,4,3,2,1,0:T(8,128)(2,1)S(1)}) custom-call(bf16[192,384]{1,0:T(8,128)(2,1)S(1)} %get-tuple-element.20.video, bf16[192,384]{1,0:T(8,128)(2,1)S(1)} %collective-permute-done.carried, bf16[3,384,768]{2,1,0:T(8,128)(2,1)S(1)} %get-tuple-element.21.w_time, ...), custom_call_target="tpu_custom_call" | custom-call | flops 3000000000 | bytes 12000000 | tf_op jit(solution)/shard_map/block_terms/pallas_call | solution.py:186
  18.8 5.9 %collective-permute-start.3 = (bf16[4,2,2,2,4,48,128]{6,5,4,3,2,1,0:T(8,128)(2,1)S(1)}, bf16[4,2,2,2,4,48,128]{6,5,4,3,2,1,0:T(8,128)(2,1)S(1)}, u32[]{:S(2)}, u32[]{:S(2)}) collective-permute-start(bf16[4,2,2,2,4,48,128]{6,5,4,3,2,1,0:T(8,128)(2,1)S(1)} %get-tuple-element.30), channel_id=1, source_target_pairs={{0,1},{1,0},{2,3},{3,2},{4,5},{5,4},{6,7},{7,6},{8,9},{9,8},{10,11... | collective-permute-start | bytes 4718600 | tf_op jit(solution)/shard_map/ppermute | solution.py:321
  24.8 3.0 %collective-permute-done.3 = bf16[4,2,2,2,4,48,128]{6,5,4,3,2,1,0:T(8,128)(2,1)S(1)} collective-permute-done((bf16[4,2,2,2,4,48,128]{6,5,4,3,2,1,0:T(8,128)(2,1)S(1)}, bf16[4,2,2,2,4,48,128]{6,5,4,3,2,1,0:T(8,128)(2,1)S(1)}, u32[]{:S(2)}, u32[]{:S(2)}) %collective-permute-start.3) | collective-permute-done | bytes 1572896 | tf_op jit(solution)/shard_map/ppermute | solution.py:321
  27.8 0.4 pair_sum.1
  28.2 31.4 %all_to_all.15.refs_0_ = bf16[16,384,128]{2,1,0:T(8,128)(2,1)S(1)} all-to-all(bf16[16,384,128]{2,1,0:T(8,128)(2,1)S(1)} %bitcast.11), channel_id=1, replica_groups={{0,2,64,66,16,18,80,82,32,34,96,98,48,50,112,114},{4,6,68,70,20,22,84,8..., dimensions={0} | all-to-all | bytes 3145728 | tf_op jit(solution)/shard_map/all_to_all | solution.py:306
  59.6 0.2 group_sum.2
  59.8 1.3 %collective-permute-start.4 = (bf16[192,768]{1,0:T(8,128)(2,1)S(1)}, bf16[192,768]{1,0:T(8,128)(2,1)S(1)}, u32[]{:S(2)}, u32[]{:S(2)}) collective-permute-start(bf16[192,768]{1,0:T(8,128)(2,1)S(1)} %get-tuple-element.31.grad_hidden.own), channel_id=1, source_target_pairs={{64,0},{128,64},{192,128},{256,192},{320,256},{384,320},{448,384},... | collective-permute-start | bytes 884744 | tf_op jit(solution)/shard_map/ppermute | solution.py:341
  61.1 16.4 %all_to_all.16.refs_0_ = bf16[8,48,128]{2,1,0:T(8,128)(2,1)S(1)} all-to-all(bf16[8,48,128]{2,1,0:T(8,128)(2,1)S(1)} %bitcast.14), channel_id=1, replica_groups={{0,4,8,12,128,132,136,140},{2,6,10,14,130,134,138,142},{16,20,24,28,144..., dimensions={0} | all-to-all | bytes 196608 | tf_op jit(solution)/shard_map/all_to_all | solution.py:306
  77.5 0.0 collective-permute-done.4.following
  77.5 0.7 group_sum.3
  78.2 9.2 %all-to-all-start.2 = ((bf16[16,48,128]{2,1,0:T(8,128)(2,1)}), bf16[16,48,128]{2,1,0:T(8,128)(2,1)S(1)}, u32[]{:S(2)}, u32[]{:S(2)}) async-start(bf16[16,48,128]{2,1,0:T(8,128)(2,1)} %group_sum.3), calls=%async_computation.2 | async-start | bytes 393216 | tf_op jit(solution)/shard_map/all_to_all | solution.py:344
  87.4 1.4 %video_grad.1 = bf16[192,384]{1,0:T(8,128)(2,1)} custom-call(bf16[192,768]{1,0:T(8,128)(2,1)S(1)} %get-tuple-element.31.grad_hidden.own, bf16[192,768]{1,0:T(8,128)(2,1)S(1)} %collective-permute-done.4.following, bf16[3,384,768]{2,1,0:T(8,128)(2,1)S(1)} %get-tuple-element.21.w_time), custom_call_target="tpu_custom_call" | custom-call | flops 350000000 | bytes 2500000 | tf_op jit(solution)/shard_map/video_grad/pallas_call | solution.py:289
  88.8 8.9 %all-to-all-done.2.refs_0_ = bf16[16,48,128]{2,1,0:T(8,128)(2,1)S(1)} async-done(((bf16[16,48,128]{2,1,0:T(8,128)(2,1)}), bf16[16,48,128]{2,1,0:T(8,128)(2,1)S(1)}, u32[]{:S(2)}, u32[]{:S(2)}) %all-to-all-start.2) | async-done | bytes 196640 | tf_op jit(solution)/shard_map/all_to_all | solution.py:344
  97.7 0.8 unpack.1
Async XLA Ops:
  1.7 12.9 %collective-permute-start.2 = (bf16[4,1,96,192]{3,2,1,0:T(8,128)(2,1)S(1)}, bf16[4,1,96,192]{3,2,1,0:T(8,128)(2,1)S(1)}, u32[]{:S(2)}, u32[]{:S(2)}) collective-permute-start(bf16[4,1,96,192]{3,2,1,0:T(8,128)(2,1)S(1)} %get-tuple-element.37), channel_id=1, source_target_pairs={{2,0},{4,2},{6,4},{8,6},{10,8},{12,10},{14,12},{16,14},{18,16},{20... | collective-permute-start | bytes 442376 | tf_op jit(solution)/shard_map/ppermute | solution.py:315
  3.0 11.6 %collective-permute-start.1 = (bf16[4,1,96,192]{3,2,1,0:T(8,128)(2,1)S(1)}, bf16[4,1,96,192]{3,2,1,0:T(8,128)(2,1)S(1)}, u32[]{:S(2)}, u32[]{:S(2)}) collective-permute-start(bf16[4,1,96,192]{3,2,1,0:T(8,128)(2,1)S(1)} %get-tuple-element.38), channel_id=1, source_target_pairs={{0,2},{2,4},{4,6},{6,8},{8,10},{10,12},{12,14},{14,16},{16,18},{18... | collective-permute-start | bytes 442376 | tf_op jit(solution)/shard_map/ppermute | solution.py:314
  8.5 7.0 %collective-permute-start = (bf16[192,384]{1,0:T(8,128)(2,1)}, bf16[192,384]{1,0:T(8,128)(2,1)S(1)}, u32[]{:S(2)}, u32[]{:S(2)}) collective-permute-start(bf16[192,384]{1,0:T(8,128)(2,1)} %bitcast.19), channel_id=1, source_target_pairs={{0,64},{64,128},{128,192},{192,256},{256,320},{320,384},{384,448},... | collective-permute-start | bytes 442376 | tf_op jit(solution)/shard_map/ppermute | solution.py:316
  18.8 9.0 %collective-permute-start.3 = (bf16[4,2,2,2,4,48,128]{6,5,4,3,2,1,0:T(8,128)(2,1)S(1)}, bf16[4,2,2,2,4,48,128]{6,5,4,3,2,1,0:T(8,128)(2,1)S(1)}, u32[]{:S(2)}, u32[]{:S(2)}) collective-permute-start(bf16[4,2,2,2,4,48,128]{6,5,4,3,2,1,0:T(8,128)(2,1)S(1)} %get-tuple-element.30), channel_id=1, source_target_pairs={{0,1},{1,0},{2,3},{3,2},{4,5},{5,4},{6,7},{7,6},{8,9},{9,8},{10,11... | collective-permute-start | bytes 4718600 | tf_op jit(solution)/shard_map/ppermute | solution.py:321
  59.8 17.7 %collective-permute-start.4 = (bf16[192,768]{1,0:T(8,128)(2,1)S(1)}, bf16[192,768]{1,0:T(8,128)(2,1)S(1)}, u32[]{:S(2)}, u32[]{:S(2)}) collective-permute-start(bf16[192,768]{1,0:T(8,128)(2,1)S(1)} %get-tuple-element.31.grad_hidden.own), channel_id=1, source_target_pairs={{64,0},{128,64},{192,128},{256,192},{320,256},{384,320},{448,384},... | collective-permute-start | bytes 884744 | tf_op jit(solution)/shard_map/ppermute | solution.py:341
  78.2 19.5 %all-to-all-start.2 = ((bf16[16,48,128]{2,1,0:T(8,128)(2,1)}), bf16[16,48,128]{2,1,0:T(8,128)(2,1)S(1)}, u32[]{:S(2)}, u32[]{:S(2)}) async-start(bf16[16,48,128]{2,1,0:T(8,128)(2,1)} %group_sum.3), calls=%async_computation.2 | async-start | bytes 393216 | tf_op jit(solution)/shard_map/all_to_all | solution.py:344

commit v6 on v5

--- a/solution.py
+++ b/solution.py
@@ -18,6 +18,10 @@
 
 def dot(a, b):
     return jnp.dot(a, b, preferred_element_type=F32)
+
+
+def dot_rows(a, b):
+    return lax.dot_general(a, b, (((1,), (1,)), ((), ())), preferred_element_type=F32)
 
 
 def dot_t(a, b):
@@ -99,7 +103,7 @@
     )(cot, video, w_time, w_space)
 
 
-def grad_kernel(cot, low, high, w_space, grad_in, grad_hidden, outer):
+def grad_kernel(cot, low, high, w_space, w_time, grad_in, grad_hidden, outer, returned):
     pick = picker()
     for s in range(2 * FRAMES):
         put(outer, 0, s, (dot(pick, low[s, 0]) + dot(pick, cot[s, 0])).astype(BF16))
@@ -112,21 +116,25 @@
                 grad_hidden[(t * BAND + p) * COLS : (t * BAND + p + 1) * COLS, j * CH_IN : (j + 1) * CH_IN] = part[
                     s * COLS : (s + 1) * COLS
                 ].astype(BF16)
-
-
-def grad_terms(cot, low, high, w_space, grad):
+    first, second = grad_hidden[:CELLS], grad_hidden[CELLS:]
+    returned[:CELLS] = dot_rows(first, w_time[0]).astype(BF16)
+    returned[CELLS:] = (dot_rows(first, w_time[1]) + dot_rows(second, w_time[0])).astype(BF16)
+
+
+def grad_terms(cot, low, high, w_space, w_time, grad):
     return pl.pallas_call(
         grad_kernel,
         name="grad_terms",
         out_shape=(
             jax.ShapeDtypeStruct((FRAMES * CELLS, 2 * CH_IN), BF16),
             jax.ShapeDtypeStruct((3 * len(OUTER), HALF, CH_OUT), BF16),
+            jax.ShapeDtypeStruct((FRAMES * CELLS, CH_IN), BF16),
         ),
-        in_specs=[VMEM] * 5,
-        out_specs=(VMEM,) * 2,
+        in_specs=[VMEM] * 6,
+        out_specs=(VMEM,) * 3,
         compiler_params=params(8),
         cost_estimate=pl.CostEstimate(flops=800_000_000, bytes_accessed=4_000_000, transcendentals=0),
-    )(cot, low, high, w_space, grad)
+    )(cot, low, high, w_space, w_time, grad)
 
 
 def block_kernel(
@@ -240,7 +248,8 @@
     )(parts)
 
 
-def unpack_kernel(scale, pieces, time, space, line):
+def unpack_kernel(scale, pieces, own, following, time, space, video, line):
+    video[...] = (own[...] + following[...].astype(F32)).astype(BF16)
     for k in range(2):
         for c0 in range(2):
             for c1 in range(2):
@@ -256,45 +265,38 @@
     space[LANES:] = jnp.concatenate([rest[0:64, :half], rest[64:, :half]], axis=1).astype(BF16)
 
 
-def unpack(pieces, scale):
+def unpack(pieces, own, following, scale):
     return pl.pallas_call(
         lambda *refs: unpack_kernel(scale, *refs),
         name="unpack",
         out_shape=(
             jax.ShapeDtypeStruct((TIME_ROWS, 6 * LANES), BF16),
             jax.ShapeDtypeStruct((CH_OUT, SPACE_ROWS), BF16),
+            jax.ShapeDtypeStruct(own.shape, BF16),
         ),
-        in_specs=[VMEM],
-        out_specs=(VMEM, VMEM),
+        in_specs=[VMEM] * 3,
+        out_specs=(VMEM,) * 3,
         scratch_shapes=[pltpu.VMEM((LINES + 8, LANES), F32)],
         compiler_params=params(8),
-    )(pieces)
-
-
-def video_kernel(own, following, w_time, out):
-    ahead = jnp.concatenate([own[...], following[...]], axis=0)
-    total = None
-    for k in range(3):
-        term = lax.dot_general(
-            ahead[(2 - k) * CELLS : (2 - k + FRAMES) * CELLS],
-            w_time[k],
-            (((1,), (1,)), ((), ())),
-            preferred_element_type=F32,
-        )
-        total = term if total is None else total + term
-    out[...] = total.astype(BF16)
-
-
-def video_grad(own, following, w_time):
+    )(pieces, own, following)
+
+
+def video_kernel(grad_hidden, w_time, out):
+    first, second = grad_hidden[:CELLS], grad_hidden[CELLS:]
+    out[:CELLS] = dot_rows(first, w_time[2]) + dot_rows(second, w_time[1])
+    out[CELLS:] = dot_rows(second, w_time[2])
+
+
+def video_terms(grad_hidden, w_time):
     return pl.pallas_call(
         video_kernel,
-        name="video_grad",
-        out_shape=jax.ShapeDtypeStruct((FRAMES * CELLS, CH_IN), BF16),
-        in_specs=[VMEM] * 3,
+        name="video_terms",
+        out_shape=jax.ShapeDtypeStruct((FRAMES * CELLS, CH_IN), F32),
+        in_specs=[VMEM] * 2,
         out_specs=VMEM,
         compiler_params=params(8),
         cost_estimate=pl.CostEstimate(flops=350_000_000, bytes_accessed=2_500_000, transcendentals=0),
-    )(own, following, w_time)
+    )(grad_hidden, w_time)
 
 
 def along(axis, steps):
@@ -316,9 +318,11 @@
     carried = lax.ppermute(own, "chain", along("chain", 1))
     operands = [pltpu.with_memory_space_constraint(value, pltpu.HBM) for value in (cot, own, w_time, w_space)]
     cot, own, w_time, w_space, inner, grad, hidden = inner_terms(*operands)
-    grad_hidden, outer = grad_terms(cot, low, high, w_space, grad)
+    grad_hidden, outer, returned = grad_terms(cot, low, high, w_space, w_time, grad)
     keep, send = block_terms(own, carried, w_time, inner, outer, grad_hidden, hidden)
     received = lax.ppermute(send, "clip", [(0, 1), (1, 0)])
+    ours = video_terms(grad_hidden, w_time)
+    received, ours = lax.optimization_barrier((received, ours))
 
     def device(c, x, z):
         return c * rows + x * N_Z + z
@@ -337,15 +341,14 @@
     ]
     share = pair_sum(keep.reshape(-1, LANES), received.reshape(-1, LANES))
     share = group_sum(exchange(share.reshape(4 * N_X, -1, LANES), near))
-    share, grad_hidden = lax.optimization_barrier((share, grad_hidden))
-    following = lax.ppermute(grad_hidden, "chain", along("chain", -1))
+    share, returned = lax.optimization_barrier((share, returned))
+    following = lax.ppermute(returned, "chain", along("chain", -1))
     share, following = lax.optimization_barrier((exchange(share.reshape(N_Z, PIECE, LANES), far), following))
     share = group_sum(share, 2 * chain)
     pieces = lax.all_to_all(share, ("chain", "clip"), 0, 0, tiled=True)
     voxels = 2 * chain * 2 * FRAMES * rows * 2 * BAND * 2 * COLS
-    grad_time, grad_space = unpack(pieces, 1.0 / math.sqrt(voxels))
-    grad_video = video_grad(grad_hidden, following, w_time).reshape(video.shape)
-    return grad_video, grad_time, grad_space.T
+    grad_time, grad_space, grad_video = unpack(pieces, ours, following, 1.0 / math.sqrt(voxels))
+    return grad_video.reshape(video.shape), grad_time, grad_space.T
 
 
 def solution(mesh):

time: 98.9 us -> 93.6 us (0.946)
  starting transfers between devices: 26.4 us -> 23.4 us
  waiting for transfers between devices: 12 us -> 9.8 us
    all_to_all x2 -> x1, blocking collectives: 47.8 us -> 30.6 us  [exchange(): lax.all_to_all(parts, ('chain', 'rows'), 0, 0, tiled=True, axis_index_gro...]
    all_to_all x0 -> x1, blocking collectives: none -> 17.2 us  [local(): pieces = lax.all_to_all(share, ('chain', 'clip'), 0, 0, tiled=True)]
    all_to_all x1, waiting for transfers between devices: 8.93 us -> 2.55 us  [exchange(): lax.all_to_all(parts, ('chain', 'rows'), 0, 0, tiled=True, axis_index_gro...]
    ppermute x1, waiting for transfers between devices: 0.01 us -> 4.88 us  [local(): following = lax.ppermute(returned, 'chain', along('chain', -1))]
    all_to_all x1, starting transfers between devices: 9.2 us -> 7.43 us  [exchange(): lax.all_to_all(parts, ('chain', 'rows'), 0, 0, tiled=True, axis_index_gro...]
  transfers between devices with their start and end apart: 6 -> 6, of which waited for: 2 -> 3; matrix products, arithmetic and copies ran while one was open for 0% -> 0% of each run, Pallas kernels for 5% -> 5%
where the time goes in v6:
time: 93.6 us; the launch traced here: 93.2 us
  blocking collectives  47.8 us (51%)
  starting transfers between devices  23.4 us (25%)
  Pallas kernels  10.5 us (11%)
  waiting for transfers between devices  9.8 us (10%)
  local copies, waits for them, and re-layouts  1.05 us (1%)
    all_to_all x1, blocking collectives, exchange(): lax.all_to_all(parts, ('chain', 'rows'), 0, 0, tiled=True, axis_index_gro...  30.6 us
    all_to_all x1, blocking collectives, local(): pieces = lax.all_to_all(share, ('chain', 'clip'), 0, 0, tiled=True)  17.2 us
    all_to_all x1, starting transfers between devices, exchange(): lax.all_to_all(parts, ('chain', 'rows'), 0, 0, tiled=True, axis_index_gro...  7.43 us
    ppermute x1, starting transfers between devices, local(): received = lax.ppermute(send, 'clip', [(0, 1), (1, 0)])  5.35 us
    ppermute x1, waiting for transfers between devices, local(): following = lax.ppermute(returned, 'chain', along('chain', -1))  4.88 us
    ppermute x1, starting transfers between devices, local(): low = lax.ppermute(cot[:, 2 * BAND - 1:], 'rows', along('rows', 1))  4.84 us
    pallas_call x1, Pallas kernels, block_terms(): pl.pallas_call(block_kernel, name='block_terms', out_shape=(half, half),...  3.35 us
    ppermute x1, starting transfers between devices, local(): carried = lax.ppermute(own, 'chain', along('chain', 1))  3.21 us
  transfers between devices with their start and end apart: 6, of which 3 were waited for; matrix products, arithmetic and copies ran while one was open for 0% of the time, Pallas kernels for 5%

profile of v6, /device:TPU:1, one launch (start us, length us, event | category | flops | bytes accessed | tf_op | source)
XLA Modules:
  0.0 93.2 jit_solution(6414743852871834130)
XLA Ops:
  0.6 1.1 %fusion = (bf16[4,1,96,192]{3,2,1,0:T(8,128)(2,1)S(1)}, bf16[4,1,96,192]{3,2,1,0:T(8,128)(2,1)S(1)}) fusion(bf16[4,4,96,192]{3,2,1,0:T(8,128)(2,1)} %bitcast.14), kind=kLoop, calls=%fused_computation | loop fusion | bytes 589824 | tf_op jit(solution)/shard_map/slice | solution.py:317
  1.7 4.8 %collective-permute-start.1 = (bf16[4,1,96,192]{3,2,1,0:T(8,128)(2,1)S(1)}, bf16[4,1,96,192]{3,2,1,0:T(8,128)(2,1)S(1)}, u32[]{:S(2)}, u32[]{:S(2)}) collective-permute-start(bf16[4,1,96,192]{3,2,1,0:T(8,128)(2,1)S(1)} %get-tuple-element.46), channel_id=1, source_target_pairs={{0,2},{2,4},{4,6},{6,8},{8,10},{10,12},{12,14},{14,16},{16,18},{18... | collective-permute-start | bytes 442376 | tf_op jit(solution)/shard_map/ppermute | solution.py:316
  6.5 1.3 %collective-permute-start.2 = (bf16[4,1,96,192]{3,2,1,0:T(8,128)(2,1)S(1)}, bf16[4,1,96,192]{3,2,1,0:T(8,128)(2,1)S(1)}, u32[]{:S(2)}, u32[]{:S(2)}) collective-permute-start(bf16[4,1,96,192]{3,2,1,0:T(8,128)(2,1)S(1)} %get-tuple-element.45), channel_id=1, source_target_pairs={{2,0},{4,2},{6,4},{8,6},{10,8},{12,10},{14,12},{16,14},{18,16},{20... | collective-permute-start | bytes 442376 | tf_op jit(solution)/shard_map/ppermute | solution.py:317
  7.8 3.2 %collective-permute-start = (bf16[192,384]{1,0:T(8,128)(2,1)}, bf16[192,384]{1,0:T(8,128)(2,1)S(1)}, u32[]{:S(2)}, u32[]{:S(2)}) collective-permute-start(bf16[192,384]{1,0:T(8,128)(2,1)} %bitcast.17), channel_id=1, source_target_pairs={{0,64},{64,128},{128,192},{192,256},{256,320},{320,384},{384,448},... | collective-permute-start | bytes 442376 | tf_op jit(solution)/shard_map/ppermute | solution.py:318
  11.1 2.9 %inner_terms.1 = (bf16[4,4,96,192]{3,2,1,0:T(8,128)(2,1)S(1)}, bf16[192,384]{1,0:T(8,128)(2,1)S(1)}, bf16[3,384,768]{2,1,0:T(8,128)(2,1)S(1)}, bf16[9,192,384]{2...) custom-call(bf16[4,4,96,192]{3,2,1,0:T(8,128)(2,1)} %bitcast.15, ...), custom_call_target="tpu_custom_call" | custom-call | flops 1500000000 | bytes 6000000 | tf_op jit(solution)/shard_map/inner_terms/pallas_call | solution.py:89
  14.0 0.0 collective-permute-done.1.low
  14.0 0.0 collective-permute-done.2.high
  14.0 1.5 %grad_terms.1 = (bf16[192,768]{1,0:T(8,128)(2,1)S(1)}, bf16[6,192,192]{2,1,0:T(8,128)(2,1)S(1)}, bf16[192,384]{1,0:T(8,128)(2,1)S(1)}) custom-call(bf16[4,4,96,192]{3,2,1,0:T(8,128)(2,1)S(1)} %get-tuple-element.27.cot, bf16[4,1,96,192]{3,2,1,0:T(8,128)(2,1)S(1)} %collective-permute-done.1.low, bf16[4,1,96,192]{3,2,1,0:T(8,128)(2,1)S(1)} %collective-permute-done.2.high, ...), custom_call_target="tpu_custom_call" | custom-call | flops 800000000 | bytes 4000000 | tf_op jit(solution)/shard_map/grad_terms/pallas_call | solution.py:125
  15.5 0.0 collective-permute-done.carried
  15.5 3.3 %block_terms.1 = (bf16[4,2,2,2,4,48,128]{6,5,4,3,2,1,0:T(8,128)(2,1)S(1)}, bf16[4,2,2,2,4,48,128]{6,5,4,3,2,1,0:T(8,128)(2,1)S(1)}) custom-call(bf16[192,384]{1,0:T(8,128)(2,1)S(1)} %get-tuple-element.24.video, bf16[192,384]{1,0:T(8,128)(2,1)S(1)} %collective-permute-done.carried, bf16[3,384,768]{2,1,0:T(8,128)(2,1)S(1)} %get-tuple-element.25.w_time, ...), custom_call_target="tpu_custom_call" | custom-call | flops 3000000000 | bytes 12000000 | tf_op jit(solution)/shard_map/block_terms/pallas_call | solution.py:194
  18.8 5.4 %collective-permute-start.3 = (bf16[4,2,2,2,4,48,128]{6,5,4,3,2,1,0:T(8,128)(2,1)S(1)}, bf16[4,2,2,2,4,48,128]{6,5,4,3,2,1,0:T(8,128)(2,1)S(1)}, u32[]{:S(2)}, u32[]{:S(2)}) collective-permute-start(bf16[4,2,2,2,4,48,128]{6,5,4,3,2,1,0:T(8,128)(2,1)S(1)} %get-tuple-element.34), channel_id=1, source_target_pairs={{0,1},{1,0},{2,3},{3,2},{4,5},{5,4},{6,7},{7,6},{8,9},{9,8},{10,11... | collective-permute-start | bytes 4718600 | tf_op jit(solution)/shard_map/ppermute | solution.py:323
  24.2 0.7 video_terms.1.refs_1_
  24.8 2.4 %collective-permute-done.3 = bf16[4,2,2,2,4,48,128]{6,5,4,3,2,1,0:T(8,128)(2,1)S(1)} collective-permute-done((bf16[4,2,2,2,4,48,128]{6,5,4,3,2,1,0:T(8,128)(2,1)S(1)}, bf16[4,2,2,2,4,48,128]{6,5,4,3,2,1,0:T(8,128)(2,1)S(1)}, u32[]{:S(2)}, u32[]{:S(2)}) %collective-permute-start.3) | collective-permute-done | bytes 1572896 | tf_op jit(solution)/shard_map/ppermute | solution.py:323
  27.2 0.4 pair_sum.1
  27.6 30.6 %all_to_all.15.refs_0_ = bf16[16,384,128]{2,1,0:T(8,128)(2,1)S(1)} all-to-all(bf16[16,384,128]{2,1,0:T(8,128)(2,1)S(1)} %bitcast.11), channel_id=1, replica_groups={{0,2,64,66,16,18,80,82,32,34,96,98,48,50,112,114},{4,6,68,70,20,22,84,8..., dimensions={0} | all-to-all | bytes 3145728 | tf_op jit(solution)/shard_map/all_to_all | solution.py:308
  58.2 0.8 group_sum.2
  59.0 7.4 %all-to-all-start.1 = ((bf16[8,48,128]{2,1,0:T(8,128)(2,1)}), bf16[8,48,128]{2,1,0:T(8,128)(2,1)S(1)}, u32[]{:S(2)}, u32[]{:S(2)}) async-start(bf16[8,48,128]{2,1,0:T(8,128)(2,1)} %bitcast.7), calls=%async_computation.1 | async-start | bytes 196608 | tf_op jit(solution)/shard_map/all_to_all | solution.py:308
  66.5 1.3 %collective-permute-start.4 = (bf16[192,384]{1,0:T(8,128)(2,1)S(1)}, bf16[192,384]{1,0:T(8,128)(2,1)S(1)}, u32[]{:S(2)}, u32[]{:S(2)}) collective-permute-start(bf16[192,384]{1,0:T(8,128)(2,1)S(1)} %get-tuple-element.38), channel_id=1, source_target_pairs={{64,0},{128,64},{192,128},{256,192},{320,256},{384,320},{448,384},... | collective-permute-start | bytes 442376 | tf_op jit(solution)/shard_map/ppermute | solution.py:345
  67.8 4.9 %collective-permute-done.4.refs_2_ = bf16[192,384]{1,0:T(8,128)(2,1)S(1)} collective-permute-done((bf16[192,384]{1,0:T(8,128)(2,1)S(1)}, bf16[192,384]{1,0:T(8,128)(2,1)S(1)}, u32[]{:S(2)}, u32[]{:S(2)}) %collective-permute-start.4) | collective-permute-done | bytes 147488 | tf_op jit(solution)/shard_map/ppermute | solution.py:345
  72.6 2.6 %all-to-all-done.1.refs_0_ = bf16[8,48,128]{2,1,0:T(8,128)(2,1)S(1)} async-done(((bf16[8,48,128]{2,1,0:T(8,128)(2,1)}), bf16[8,48,128]{2,1,0:T(8,128)(2,1)S(1)}, u32[]{:S(2)}, u32[]{:S(2)}) %all-to-all-start.1) | async-done | bytes 98336 | tf_op jit(solution)/shard_map/all_to_all | solution.py:308
  75.2 17.2 %all_to_all.16.refs_0_ = bf16[16,48,128]{2,1,0:T(8,128)(2,1)S(1)} all-to-all(bf16[16,48,128]{2,1,0:T(8,128)(2,1)S(1)} %group_sum.3), channel_id=1, replica_groups=mesh['chain'=8,'rows'=32,'clip'=2] {'chain','clip'}, dimensions={0} | all-to-all | bytes 393216 | tf_op jit(solution)/shard_map/all_to_all | solution.py:348
  92.4 0.9 unpack.1
  (1 shorter events, 0.0 us)
Async XLA Ops:
  1.7 12.3 %collective-permute-start.1 = (bf16[4,1,96,192]{3,2,1,0:T(8,128)(2,1)S(1)}, bf16[4,1,96,192]{3,2,1,0:T(8,128)(2,1)S(1)}, u32[]{:S(2)}, u32[]{:S(2)}) collective-permute-start(bf16[4,1,96,192]{3,2,1,0:T(8,128)(2,1)S(1)} %get-tuple-element.46), channel_id=1, source_target_pairs={{0,2},{2,4},{4,6},{6,8},{8,10},{10,12},{12,14},{14,16},{16,18},{18... | collective-permute-start | bytes 442376 | tf_op jit(solution)/shard_map/ppermute | solution.py:316
  6.5 7.4 %collective-permute-start.2 = (bf16[4,1,96,192]{3,2,1,0:T(8,128)(2,1)S(1)}, bf16[4,1,96,192]{3,2,1,0:T(8,128)(2,1)S(1)}, u32[]{:S(2)}, u32[]{:S(2)}) collective-permute-start(bf16[4,1,96,192]{3,2,1,0:T(8,128)(2,1)S(1)} %get-tuple-element.45), channel_id=1, source_target_pairs={{2,0},{4,2},{6,4},{8,6},{10,8},{12,10},{14,12},{16,14},{18,16},{20... | collective-permute-start | bytes 442376 | tf_op jit(solution)/shard_map/ppermute | solution.py:317
  7.8 7.6 %collective-permute-start = (bf16[192,384]{1,0:T(8,128)(2,1)}, bf16[192,384]{1,0:T(8,128)(2,1)S(1)}, u32[]{:S(2)}, u32[]{:S(2)}) collective-permute-start(bf16[192,384]{1,0:T(8,128)(2,1)} %bitcast.17), channel_id=1, source_target_pairs={{0,64},{64,128},{128,192},{192,256},{256,320},{320,384},{384,448},... | collective-permute-start | bytes 442376 | tf_op jit(solution)/shard_map/ppermute | solution.py:318
  18.8 8.4 %collective-permute-start.3 = (bf16[4,2,2,2,4,48,128]{6,5,4,3,2,1,0:T(8,128)(2,1)S(1)}, bf16[4,2,2,2,4,48,128]{6,5,4,3,2,1,0:T(8,128)(2,1)S(1)}, u32[]{:S(2)}, u32[]{:S(2)}) collective-permute-start(bf16[4,2,2,2,4,48,128]{6,5,4,3,2,1,0:T(8,128)(2,1)S(1)} %get-tuple-element.34), channel_id=1, source_target_pairs={{0,1},{1,0},{2,3},{3,2},{4,5},{5,4},{6,7},{7,6},{8,9},{9,8},{10,11... | collective-permute-start | bytes 4718600 | tf_op jit(solution)/shard_map/ppermute | solution.py:323
  59.0 16.2 %all-to-all-start.1 = ((bf16[8,48,128]{2,1,0:T(8,128)(2,1)}), bf16[8,48,128]{2,1,0:T(8,128)(2,1)S(1)}, u32[]{:S(2)}, u32[]{:S(2)}) async-start(bf16[8,48,128]{2,1,0:T(8,128)(2,1)} %bitcast.7), calls=%async_computation.1 | async-start | bytes 196608 | tf_op jit(solution)/shard_map/all_to_all | solution.py:308
  66.5 6.2 %collective-permute-start.4 = (bf16[192,384]{1,0:T(8,128)(2,1)S(1)}, bf16[192,384]{1,0:T(8,128)(2,1)S(1)}, u32[]{:S(2)}, u32[]{:S(2)}) collective-permute-start(bf16[192,384]{1,0:T(8,128)(2,1)S(1)} %get-tuple-element.38), channel_id=1, source_target_pairs={{64,0},{128,64},{192,128},{256,192},{320,256},{384,320},{448,384},... | collective-permute-start | bytes 442376 | tf_op jit(solution)/shard_map/ppermute | solution.py:345

commit v7 on v6

--- a/solution.py
+++ b/solution.py
@@ -103,7 +103,7 @@
     )(cot, video, w_time, w_space)
 
 
-def grad_kernel(cot, low, high, w_space, w_time, grad_in, grad_hidden, outer, returned):
+def grad_kernel(cot, low, high, w_space, grad_in, grad_hidden, outer):
     pick = picker()
     for s in range(2 * FRAMES):
         put(outer, 0, s, (dot(pick, low[s, 0]) + dot(pick, cot[s, 0])).astype(BF16))
@@ -116,31 +116,27 @@
                 grad_hidden[(t * BAND + p) * COLS : (t * BAND + p + 1) * COLS, j * CH_IN : (j + 1) * CH_IN] = part[
                     s * COLS : (s + 1) * COLS
                 ].astype(BF16)
-    first, second = grad_hidden[:CELLS], grad_hidden[CELLS:]
-    returned[:CELLS] = dot_rows(first, w_time[0]).astype(BF16)
-    returned[CELLS:] = (dot_rows(first, w_time[1]) + dot_rows(second, w_time[0])).astype(BF16)
-
-
-def grad_terms(cot, low, high, w_space, w_time, grad):
+
+
+def grad_terms(cot, low, high, w_space, grad):
     return pl.pallas_call(
         grad_kernel,
         name="grad_terms",
         out_shape=(
             jax.ShapeDtypeStruct((FRAMES * CELLS, 2 * CH_IN), BF16),
             jax.ShapeDtypeStruct((3 * len(OUTER), HALF, CH_OUT), BF16),
-            jax.ShapeDtypeStruct((FRAMES * CELLS, CH_IN), BF16),
         ),
-        in_specs=[VMEM] * 6,
-        out_specs=(VMEM,) * 3,
+        in_specs=[VMEM] * 5,
+        out_specs=(VMEM,) * 2,
         compiler_params=params(8),
         cost_estimate=pl.CostEstimate(flops=800_000_000, bytes_accessed=4_000_000, transcendentals=0),
-    )(cot, low, high, w_space, w_time, grad)
+    )(cot, low, high, w_space, grad)
 
 
 def block_kernel(
     video, carried, w_time, inner, outer, grad_hidden, hidden_in,
     keep, send,
-    ext, hid, time_acc, space_acc, line,
+    ext, hid, time_acc, space_acc,
 ):
     ext[0 : FRAMES * CELLS] = carried[...]
     ext[FRAMES * CELLS :] = video[...]
@@ -167,25 +163,24 @@
             tap = 3 * a + c
             space_acc[tap * CH_IN : (tap + 1) * CH_IN] = total
 
-    mine = lax.axis_index("clip")
-    line[378:LINES] = jnp.zeros((6, LANES), F32)
+    mine = lax.axis_index("clip") == 0
     half = SPACE_ROWS // 2
     for r in range(N_X * N_Z):
         x, zh, zl = r // N_Z, r % N_Z // 2, r % 2
         t0, s0 = r * TIME_ROWS, r * SPACE_ROWS
-        for j in range(6):
-            line[j * TIME_ROWS : (j + 1) * TIME_ROWS] = time_acc[t0 : t0 + TIME_ROWS, j * LANES : (j + 1) * LANES]
-        line[216:324] = space_acc[s0 : s0 + SPACE_ROWS, 0:LANES]
-        line[324:378] = jnp.concatenate(
-            [space_acc[s0 : s0 + half, LANES:CH_OUT], space_acc[s0 + half : s0 + SPACE_ROWS, LANES:CH_OUT]], axis=1
-        )
+        lines = [time_acc[t0 : t0 + TIME_ROWS, j * LANES : (j + 1) * LANES] for j in range(6)]
+        lines.append(space_acc[s0 : s0 + SPACE_ROWS, 0:LANES])
+        rest = [space_acc[s0 + i * half : s0 + (i + 1) * half, LANES:CH_OUT] for i in range(2)]
+        lines.append(jnp.concatenate(rest, axis=1))
+        lines.append(jnp.zeros((6, LANES), F32))
+        lines = jnp.concatenate(lines, axis=0).astype(BF16)
+        upper, lower = lines[: LINES // 2], lines[LINES // 2 :]
+        mine_half, other_half = jnp.where(mine, upper, lower), jnp.where(mine, lower, upper)
         for c0 in range(2):
             for c1 in range(2):
                 piece = (c0 * 2 + c1) * PIECE
-                own = pl.multiple_of(mine * (LINES // 2) + piece, 8)
-                other = pl.multiple_of((1 - mine) * (LINES // 2) + piece, 8)
-                keep[x, c0, zl, c1, zh] = line[pl.ds(own, PIECE)].astype(BF16)
-                send[x, c0, zl, c1, zh] = line[pl.ds(other, PIECE)].astype(BF16)
+                keep[x, zl, c0, c1, zh] = mine_half[piece : piece + PIECE]
+                send[x, zl, c0, c1, zh] = other_half[piece : piece + PIECE]
 
 
 def block_terms(video, carried, w_time, inner, outer, grad_hidden, hidden):
@@ -202,7 +197,6 @@
             pltpu.VMEM((2 * cells, CH_IN), BF16),
             pltpu.VMEM((3 * CH_IN, 2 * CH_IN), F32),
             pltpu.VMEM((9 * CH_IN, CH_OUT), F32),
-            pltpu.VMEM((LINES, LANES), F32),
         ],
         compiler_params=params(20),
         cost_estimate=pl.CostEstimate(flops=3_000_000_000, bytes_accessed=12_000_000, transcendentals=0),
@@ -281,21 +275,26 @@
     )(pieces, own, following)
 
 
-def video_kernel(grad_hidden, w_time, out):
+def video_kernel(grad_hidden, w_time, ours, returned):
     first, second = grad_hidden[:CELLS], grad_hidden[CELLS:]
-    out[:CELLS] = dot_rows(first, w_time[2]) + dot_rows(second, w_time[1])
-    out[CELLS:] = dot_rows(second, w_time[2])
+    ours[:CELLS] = dot_rows(first, w_time[2]) + dot_rows(second, w_time[1])
+    ours[CELLS:] = dot_rows(second, w_time[2])
+    returned[:CELLS] = dot_rows(first, w_time[0]).astype(BF16)
+    returned[CELLS:] = (dot_rows(first, w_time[1]) + dot_rows(second, w_time[0])).astype(BF16)
 
 
 def video_terms(grad_hidden, w_time):
     return pl.pallas_call(
         video_kernel,
         name="video_terms",
-        out_shape=jax.ShapeDtypeStruct((FRAMES * CELLS, CH_IN), F32),
+        out_shape=(
+            jax.ShapeDtypeStruct((FRAMES * CELLS, CH_IN), F32),
+            jax.ShapeDtypeStruct((FRAMES * CELLS, CH_IN), BF16),
+        ),
         in_specs=[VMEM] * 2,
-        out_specs=VMEM,
-        compiler_params=params(8),
-        cost_estimate=pl.CostEstimate(flops=350_000_000, bytes_accessed=2_500_000, transcendentals=0),
+        out_specs=(VMEM,) * 2,
+        compiler_params=params(8),
+        cost_estimate=pl.CostEstimate(flops=700_000_000, bytes_accessed=2_500_000, transcendentals=0),
     )(grad_hidden, w_time)
 
 
@@ -318,17 +317,17 @@
     carried = lax.ppermute(own, "chain", along("chain", 1))
     operands = [pltpu.with_memory_space_constraint(value, pltpu.HBM) for value in (cot, own, w_time, w_space)]
     cot, own, w_time, w_space, inner, grad, hidden = inner_terms(*operands)
-    grad_hidden, outer, returned = grad_terms(cot, low, high, w_space, w_time, grad)
+    grad_hidden, outer = grad_terms(cot, low, high, w_space, grad)
     keep, send = block_terms(own, carried, w_time, inner, outer, grad_hidden, hidden)
     received = lax.ppermute(send, "clip", [(0, 1), (1, 0)])
-    ours = video_terms(grad_hidden, w_time)
+    ours, returned = video_terms(grad_hidden, w_time)
     received, ours = lax.optimization_barrier((received, ours))
 
     def device(c, x, z):
         return c * rows + x * N_Z + z
 
     near = [
-        [device(2 * ch + c, x, 2 * zh + z) for x in range(N_X) for c in range(2) for z in range(2)]
+        [device(2 * ch + c, x, 2 * zh + z) for x in range(N_X) for z in range(2) for c in range(2)]
         for ch in range(chain // 2)
         for zh in range(N_Z // 2)
     ]

time: 93.6 us -> 91.7 us (0.980)
  Pallas kernels: 10.5 us -> 9.19 us
    all_to_all x1, blocking collectives: 17.2 us -> 18.4 us  [local(): pieces = lax.all_to_all(share, ('chain', 'clip'), 0, 0, tiled=True)]
    all_to_all x1, blocking collectives: 30.6 us -> 29.4 us  [exchange(): lax.all_to_all(parts, ('chain', 'rows'), 0, 0, tiled=True, axis_index_gro...]
    pallas_call x1, Pallas kernels: 3.35 us -> 2.19 us  [block_terms(): pl.pallas_call(block_kernel, name='block_terms', out_shape=(half, half),...]
where the time goes in v7:
time: 91.7 us; the launch traced here: 91.3 us
  blocking collectives  47.8 us (52%)
  starting transfers between devices  23.3 us (25%)
  waiting for transfers between devices  9.25 us (10%)
  Pallas kernels  9.19 us (10%)
  local copies, waits for them, and re-layouts  1.05 us (1%)
    all_to_all x1, blocking collectives, exchange(): lax.all_to_all(parts, ('chain', 'rows'), 0, 0, tiled=True, axis_index_gro...  29.4 us
    all_to_all x1, blocking collectives, local(): pieces = lax.all_to_all(share, ('chain', 'clip'), 0, 0, tiled=True)  18.4 us
    all_to_all x1, starting transfers between devices, exchange(): lax.all_to_all(parts, ('chain', 'rows'), 0, 0, tiled=True, axis_index_gro...  7.3 us
    ppermute x1, starting transfers between devices, local(): received = lax.ppermute(send, 'clip', [(0, 1), (1, 0)])  5.37 us
    ppermute x1, waiting for transfers between devices, local(): following = lax.ppermute(returned, 'chain', along('chain', -1))  5.24 us
    ppermute x1, starting transfers between devices, local(): low = lax.ppermute(cot[:, 2 * BAND - 1:], 'rows', along('rows', 1))  4.84 us
    ppermute x1, starting transfers between devices, local(): carried = lax.ppermute(own, 'chain', along('chain', 1))  3.21 us
    pallas_call x1, Pallas kernels, inner_terms(): pl.pallas_call(inner_kernel, name='inner_terms', out_shape=(*(jax.ShapeDt...  2.9 us
  transfers between devices with their start and end apart: 6, of which 3 were waited for; matrix products, arithmetic and copies ran while one was open for 0% of the time, Pallas kernels for 5%

profile of v7, /device:TPU:1, one launch (start us, length us, event | category | flops | bytes accessed | tf_op | source)
XLA Modules:
  0.0 91.3 jit_solution(6642938199643248752)
XLA Ops:
  0.6 1.1 %fusion = (bf16[4,1,96,192]{3,2,1,0:T(8,128)(2,1)S(1)}, bf16[4,1,96,192]{3,2,1,0:T(8,128)(2,1)S(1)}) fusion(bf16[4,4,96,192]{3,2,1,0:T(8,128)(2,1)} %bitcast.14), kind=kLoop, calls=%fused_computation | loop fusion | bytes 589824 | tf_op jit(solution)/shard_map/slice | solution.py:316
  1.7 4.8 %collective-permute-start.1 = (bf16[4,1,96,192]{3,2,1,0:T(8,128)(2,1)S(1)}, bf16[4,1,96,192]{3,2,1,0:T(8,128)(2,1)S(1)}, u32[]{:S(2)}, u32[]{:S(2)}) collective-permute-start(bf16[4,1,96,192]{3,2,1,0:T(8,128)(2,1)S(1)} %get-tuple-element.48), channel_id=1, source_target_pairs={{0,2},{2,4},{4,6},{6,8},{8,10},{10,12},{12,14},{14,16},{16,18},{18... | collective-permute-start | bytes 442376 | tf_op jit(solution)/shard_map/ppermute | solution.py:315
  6.5 1.3 %collective-permute-start.2 = (bf16[4,1,96,192]{3,2,1,0:T(8,128)(2,1)S(1)}, bf16[4,1,96,192]{3,2,1,0:T(8,128)(2,1)S(1)}, u32[]{:S(2)}, u32[]{:S(2)}) collective-permute-start(bf16[4,1,96,192]{3,2,1,0:T(8,128)(2,1)S(1)} %get-tuple-element.47), channel_id=1, source_target_pairs={{2,0},{4,2},{6,4},{8,6},{10,8},{12,10},{14,12},{16,14},{18,16},{20... | collective-permute-start | bytes 442376 | tf_op jit(solution)/shard_map/ppermute | solution.py:316
  7.8 3.2 %collective-permute-start = (bf16[192,384]{1,0:T(8,128)(2,1)}, bf16[192,384]{1,0:T(8,128)(2,1)S(1)}, u32[]{:S(2)}, u32[]{:S(2)}) collective-permute-start(bf16[192,384]{1,0:T(8,128)(2,1)} %bitcast.17), channel_id=1, source_target_pairs={{0,64},{64,128},{128,192},{192,256},{256,320},{320,384},{384,448},... | collective-permute-start | bytes 442376 | tf_op jit(solution)/shard_map/ppermute | solution.py:317
  11.1 2.9 %inner_terms.1 = (bf16[4,4,96,192]{3,2,1,0:T(8,128)(2,1)S(1)}, bf16[192,384]{1,0:T(8,128)(2,1)S(1)}, bf16[3,384,768]{2,1,0:T(8,128)(2,1)S(1)}, bf16[9,192,384]{2...) custom-call(bf16[4,4,96,192]{3,2,1,0:T(8,128)(2,1)} %bitcast.15, ...), custom_call_target="tpu_custom_call" | custom-call | flops 1500000000 | bytes 6000000 | tf_op jit(solution)/shard_map/inner_terms/pallas_call | solution.py:89
  14.0 0.0 collective-permute-done.1.low
  14.0 0.0 collective-permute-done.2.high
  14.0 0.8 grad_terms.1
  14.8 0.0 collective-permute-done.carried
  14.8 2.2 %block_terms.1 = (bf16[4,2,2,2,4,48,128]{6,5,4,3,2,1,0:T(8,128)(2,1)S(1)}, bf16[4,2,2,2,4,48,128]{6,5,4,3,2,1,0:T(8,128)(2,1)S(1)}) custom-call(bf16[192,384]{1,0:T(8,128)(2,1)S(1)} %get-tuple-element.25.video, bf16[192,384]{1,0:T(8,128)(2,1)S(1)} %collective-permute-done.carried, bf16[3,384,768]{2,1,0:T(8,128)(2,1)S(1)} %get-tuple-element.26.w_time, ...), custom_call_target="tpu_custom_call" | custom-call | flops 3000000000 | bytes 12000000 | tf_op jit(solution)/shard_map/block_terms/pallas_call | solution.py:189
  17.0 5.4 %collective-permute-start.3 = (bf16[4,2,2,2,4,48,128]{6,5,4,3,2,1,0:T(8,128)(2,1)S(1)}, bf16[4,2,2,2,4,48,128]{6,5,4,3,2,1,0:T(8,128)(2,1)S(1)}, u32[]{:S(2)}, u32[]{:S(2)}) collective-permute-start(bf16[4,2,2,2,4,48,128]{6,5,4,3,2,1,0:T(8,128)(2,1)S(1)} %get-tuple-element.35), channel_id=1, source_target_pairs={{0,1},{1,0},{2,3},{3,2},{4,5},{5,4},{6,7},{7,6},{8,9},{9,8},{10,11... | collective-permute-start | bytes 4718600 | tf_op jit(solution)/shard_map/ppermute | solution.py:322
  22.4 1.2 %video_terms.1 = (f32[192,384]{1,0:T(8,128)S(1)}, bf16[192,384]{1,0:T(8,128)(2,1)S(1)}) custom-call(bf16[192,768]{1,0:T(8,128)(2,1)S(1)} %get-tuple-element.32.grad_hidden, bf16[3,384,768]{2,1,0:T(8,128)(2,1)S(1)} %get-tuple-element.26.w_time), custom_call_target="tpu_custom_call" | custom-call | flops 700000000 | bytes 2500000 | tf_op jit(solution)/shard_map/video_terms/pallas_call | solution.py:287
  23.6 1.9 %collective-permute-done.3 = bf16[4,2,2,2,4,48,128]{6,5,4,3,2,1,0:T(8,128)(2,1)S(1)} collective-permute-done((bf16[4,2,2,2,4,48,128]{6,5,4,3,2,1,0:T(8,128)(2,1)S(1)}, bf16[4,2,2,2,4,48,128]{6,5,4,3,2,1,0:T(8,128)(2,1)S(1)}, u32[]{:S(2)}, u32[]{:S(2)}) %collective-permute-start.3) | collective-permute-done | bytes 1572896 | tf_op jit(solution)/shard_map/ppermute | solution.py:322
  25.4 0.4 pair_sum.1
  25.8 29.4 %all_to_all.15.refs_0_ = bf16[16,384,128]{2,1,0:T(8,128)(2,1)S(1)} all-to-all(bf16[16,384,128]{2,1,0:T(8,128)(2,1)S(1)} %bitcast.11), channel_id=1, replica_groups={{0,64,2,66,16,80,18,82,32,96,34,98,48,112,50,114},{4,68,6,70,20,84,22,8..., dimensions={0} | all-to-all | bytes 3145728 | tf_op jit(solution)/shard_map/all_to_all | solution.py:307
  55.2 0.8 group_sum.2
  56.0 7.3 %all-to-all-start.1 = ((bf16[8,48,128]{2,1,0:T(8,128)(2,1)}), bf16[8,48,128]{2,1,0:T(8,128)(2,1)S(1)}, u32[]{:S(2)}, u32[]{:S(2)}) async-start(bf16[8,48,128]{2,1,0:T(8,128)(2,1)} %bitcast.7), calls=%async_computation.1 | async-start | bytes 196608 | tf_op jit(solution)/shard_map/all_to_all | solution.py:307
  63.3 1.3 %collective-permute-start.4 = (bf16[192,384]{1,0:T(8,128)(2,1)S(1)}, bf16[192,384]{1,0:T(8,128)(2,1)S(1)}, u32[]{:S(2)}, u32[]{:S(2)}) collective-permute-start(bf16[192,384]{1,0:T(8,128)(2,1)S(1)} %get-tuple-element.40), channel_id=1, source_target_pairs={{64,0},{128,64},{192,128},{256,192},{320,256},{384,320},{448,384},... | collective-permute-start | bytes 442376 | tf_op jit(solution)/shard_map/ppermute | solution.py:344
  64.6 5.2 %collective-permute-done.4.refs_2_ = bf16[192,384]{1,0:T(8,128)(2,1)S(1)} collective-permute-done((bf16[192,384]{1,0:T(8,128)(2,1)S(1)}, bf16[192,384]{1,0:T(8,128)(2,1)S(1)}, u32[]{:S(2)}, u32[]{:S(2)}) %collective-permute-start.4) | collective-permute-done | bytes 147488 | tf_op jit(solution)/shard_map/ppermute | solution.py:344
  69.9 2.1 %all-to-all-done.1.refs_0_ = bf16[8,48,128]{2,1,0:T(8,128)(2,1)S(1)} async-done(((bf16[8,48,128]{2,1,0:T(8,128)(2,1)}), bf16[8,48,128]{2,1,0:T(8,128)(2,1)S(1)}, u32[]{:S(2)}, u32[]{:S(2)}) %all-to-all-start.1) | async-done | bytes 98336 | tf_op jit(solution)/shard_map/all_to_all | solution.py:307
  72.0 18.4 %all_to_all.16.refs_0_ = bf16[16,48,128]{2,1,0:T(8,128)(2,1)S(1)} all-to-all(bf16[16,48,128]{2,1,0:T(8,128)(2,1)S(1)} %group_sum.3), channel_id=1, replica_groups=mesh['chain'=8,'rows'=32,'clip'=2] {'chain','clip'}, dimensions={0} | all-to-all | bytes 393216 | tf_op jit(solution)/shard_map/all_to_all | solution.py:347
  90.5 0.9 unpack.1
  (1 shorter events, 0.0 us)
Async XLA Ops:
  1.7 12.3 %collective-permute-start.1 = (bf16[4,1,96,192]{3,2,1,0:T(8,128)(2,1)S(1)}, bf16[4,1,96,192]{3,2,1,0:T(8,128)(2,1)S(1)}, u32[]{:S(2)}, u32[]{:S(2)}) collective-permute-start(bf16[4,1,96,192]{3,2,1,0:T(8,128)(2,1)S(1)} %get-tuple-element.48), channel_id=1, source_target_pairs={{0,2},{2,4},{4,6},{6,8},{8,10},{10,12},{12,14},{14,16},{16,18},{18... | collective-permute-start | bytes 442376 | tf_op jit(solution)/shard_map/ppermute | solution.py:315
  6.5 7.4 %collective-permute-start.2 = (bf16[4,1,96,192]{3,2,1,0:T(8,128)(2,1)S(1)}, bf16[4,1,96,192]{3,2,1,0:T(8,128)(2,1)S(1)}, u32[]{:S(2)}, u32[]{:S(2)}) collective-permute-start(bf16[4,1,96,192]{3,2,1,0:T(8,128)(2,1)S(1)} %get-tuple-element.47), channel_id=1, source_target_pairs={{2,0},{4,2},{6,4},{8,6},{10,8},{12,10},{14,12},{16,14},{18,16},{20... | collective-permute-start | bytes 442376 | tf_op jit(solution)/shard_map/ppermute | solution.py:316
  7.8 7.0 %collective-permute-start = (bf16[192,384]{1,0:T(8,128)(2,1)}, bf16[192,384]{1,0:T(8,128)(2,1)S(1)}, u32[]{:S(2)}, u32[]{:S(2)}) collective-permute-start(bf16[192,384]{1,0:T(8,128)(2,1)} %bitcast.17), channel_id=1, source_target_pairs={{0,64},{64,128},{128,192},{192,256},{256,320},{320,384},{384,448},... | collective-permute-start | bytes 442376 | tf_op jit(solution)/shard_map/ppermute | solution.py:317
  17.0 8.4 %collective-permute-start.3 = (bf16[4,2,2,2,4,48,128]{6,5,4,3,2,1,0:T(8,128)(2,1)S(1)}, bf16[4,2,2,2,4,48,128]{6,5,4,3,2,1,0:T(8,128)(2,1)S(1)}, u32[]{:S(2)}, u32[]{:S(2)}) collective-permute-start(bf16[4,2,2,2,4,48,128]{6,5,4,3,2,1,0:T(8,128)(2,1)S(1)} %get-tuple-element.35), channel_id=1, source_target_pairs={{0,1},{1,0},{2,3},{3,2},{4,5},{5,4},{6,7},{7,6},{8,9},{9,8},{10,11... | collective-permute-start | bytes 4718600 | tf_op jit(solution)/shard_map/ppermute | solution.py:322
  56.0 16.0 %all-to-all-start.1 = ((bf16[8,48,128]{2,1,0:T(8,128)(2,1)}), bf16[8,48,128]{2,1,0:T(8,128)(2,1)S(1)}, u32[]{:S(2)}, u32[]{:S(2)}) async-start(bf16[8,48,128]{2,1,0:T(8,128)(2,1)} %bitcast.7), calls=%async_computation.1 | async-start | bytes 196608 | tf_op jit(solution)/shard_map/all_to_all | solution.py:307
  63.3 6.5 %collective-permute-start.4 = (bf16[192,384]{1,0:T(8,128)(2,1)S(1)}, bf16[192,384]{1,0:T(8,128)(2,1)S(1)}, u32[]{:S(2)}, u32[]{:S(2)}) collective-permute-start(bf16[192,384]{1,0:T(8,128)(2,1)S(1)} %get-tuple-element.40), channel_id=1, source_target_pairs={{64,0},{128,64},{192,128},{256,192},{320,256},{384,320},{448,384},... | collective-permute-start | bytes 442376 | tf_op jit(solution)/shard_map/ppermute | solution.py:344

commit v8 on v7

--- a/solution.py
+++ b/solution.py
@@ -166,7 +166,7 @@
     mine = lax.axis_index("clip") == 0
     half = SPACE_ROWS // 2
     for r in range(N_X * N_Z):
-        x, zh, zl = r // N_Z, r % N_Z // 2, r % 2
+        xh, xl, zh, zl = r // N_Z // 2, r // N_Z % 2, r % N_Z // 2, r % 2
         t0, s0 = r * TIME_ROWS, r * SPACE_ROWS
         lines = [time_acc[t0 : t0 + TIME_ROWS, j * LANES : (j + 1) * LANES] for j in range(6)]
         lines.append(space_acc[s0 : s0 + SPACE_ROWS, 0:LANES])
@@ -179,13 +179,13 @@
         for c0 in range(2):
             for c1 in range(2):
                 piece = (c0 * 2 + c1) * PIECE
-                keep[x, zl, c0, c1, zh] = mine_half[piece : piece + PIECE]
-                send[x, zl, c0, c1, zh] = other_half[piece : piece + PIECE]
+                keep[xl, zl, c0, xh, c1, zh] = mine_half[piece : piece + PIECE]
+                send[xl, zl, c0, xh, c1, zh] = other_half[piece : piece + PIECE]
 
 
 def block_terms(video, carried, w_time, inner, outer, grad_hidden, hidden):
     cells = FRAMES * CELLS
-    half = jax.ShapeDtypeStruct((N_X, 2, 2, 2, N_Z // 2, PIECE, LANES), BF16)
+    half = jax.ShapeDtypeStruct((2, 2, 2, N_X // 2, 2, N_Z // 2, PIECE, LANES), BF16)
     return pl.pallas_call(
         block_kernel,
         name="block_terms",
@@ -303,8 +303,8 @@
     return [(i, i + steps) for i in range(count) if 0 <= i + steps < count]
 
 
-def exchange(parts, groups):
-    return lax.all_to_all(parts, ("chain", "rows"), 0, 0, tiled=True, axis_index_groups=groups)
+def exchange(parts, axes, groups=None):
+    return lax.all_to_all(parts, axes, 0, 0, tiled=True, axis_index_groups=groups)
 
 
 def local(video, cotangent, w_time, w_space):
@@ -326,25 +326,40 @@
     def device(c, x, z):
         return c * rows + x * N_Z + z
 
+    def pair(index, core, count):
+        return sorted(((2 * index + core) % count, (2 * index + core + 1) % count), key=lambda i: i % 2)
+
     near = [
-        [device(2 * ch + c, x, 2 * zh + z) for x in range(N_X) for z in range(2) for c in range(2)]
+        [
+            2 * device(c, x, z) + core
+            for x in pair(xh, core, N_X)
+            for z in pair(zh, core, N_Z)
+            for c in pair(ch, core, chain)
+        ]
+        for core in range(2)
+        for xh in range(N_X // 2)
         for ch in range(chain // 2)
         for zh in range(N_Z // 2)
     ]
     far = [
-        [device(4 * c2 + 2 * c + c0, x, 2 * zh + zl) for c in range(2) for zh in range(N_Z // 2)]
+        [
+            device(4 * c2 + 2 * c + c0, 2 * xh + xl, 2 * zh + zl)
+            for xh in range(N_X // 2)
+            for c in range(2)
+            for zh in range(N_Z // 2)
+        ]
         for c2 in range(chain // 4)
         for c0 in range(2)
-        for x in range(N_X)
+        for xl in range(2)
         for zl in range(2)
     ]
     share = pair_sum(keep.reshape(-1, LANES), received.reshape(-1, LANES))
-    share = group_sum(exchange(share.reshape(4 * N_X, -1, LANES), near))
+    share = group_sum(exchange(share.reshape(8, -1, LANES), ("chain", "rows", "clip"), near))
     share, returned = lax.optimization_barrier((share, returned))
     following = lax.ppermute(returned, "chain", along("chain", -1))
-    share, following = lax.optimization_barrier((exchange(share.reshape(N_Z, PIECE, LANES), far), following))
+    share, following = lax.optimization_barrier((exchange(share.reshape(2 * N_Z, PIECE, LANES), ("chain", "rows"), far), following))
     share = group_sum(share, 2 * chain)
-    pieces = lax.all_to_all(share, ("chain", "clip"), 0, 0, tiled=True)
+    pieces = exchange(share, ("chain", "clip"))
     voxels = 2 * chain * 2 * FRAMES * rows * 2 * BAND * 2 * COLS
     grad_time, grad_space, grad_video = unpack(pieces, ours, following, 1.0 / math.sqrt(voxels))
     return grad_video.reshape(video.shape), grad_time, grad_space.T

time: 91.7 us -> 91.1 us (level)
  waiting for transfers between devices: 9.25 us -> 15 us
  starting transfers between devices: 23.3 us -> 19.5 us
  blocking collectives: 47.8 us -> 45.1 us
    all_to_all x1, starting transfers between devices: 7.3 us -> 3.52 us  [exchange(): lax.all_to_all(parts, axes, 0, 0, tiled=True, axis_index_groups=groups)]
    all_to_all x1, waiting for transfers between devices: 2.14 us -> 5.75 us  [exchange(): lax.all_to_all(parts, axes, 0, 0, tiled=True, axis_index_groups=groups)]
    all_to_all x2, blocking collectives: 47.8 us -> 45.1 us  [exchange(): lax.all_to_all(parts, axes, 0, 0, tiled=True, axis_index_groups=groups)]
    ppermute x1, waiting for transfers between devices: 5.24 us -> 7.43 us  [local(): following = lax.ppermute(returned, 'chain', along('chain', -1))]
where the time goes in v8:
time: 91.1 us; the launch traced here: 90.7 us
  blocking collectives  45.1 us (50%)
  starting transfers between devices  19.5 us (21%)
  waiting for transfers between devices  15 us (16%)
  Pallas kernels  9.23 us (10%)
  local copies, waits for them, and re-layouts  1.05 us (1%)
    all_to_all x2, blocking collectives, exchange(): lax.all_to_all(parts, axes, 0, 0, tiled=True, axis_index_groups=groups)  45.1 us
    ppermute x1, waiting for transfers between devices, local(): following = lax.ppermute(returned, 'chain', along('chain', -1))  7.43 us
    all_to_all x1, waiting for transfers between devices, exchange(): lax.all_to_all(parts, axes, 0, 0, tiled=True, axis_index_groups=groups)  5.75 us
    ppermute x1, starting transfers between devices, local(): received = lax.ppermute(send, 'clip', [(0, 1), (1, 0)])  5.37 us
    ppermute x1, starting transfers between devices, local(): low = lax.ppermute(cot[:, 2 * BAND - 1:], 'rows', along('rows', 1))  4.84 us
    all_to_all x1, starting transfers between devices, exchange(): lax.all_to_all(parts, axes, 0, 0, tiled=True, axis_index_groups=groups)  3.52 us
    ppermute x1, starting transfers between devices, local(): carried = lax.ppermute(own, 'chain', along('chain', 1))  3.21 us
    pallas_call x1, Pallas kernels, inner_terms(): pl.pallas_call(inner_kernel, name='inner_terms', out_shape=(*(jax.ShapeDt...  2.9 us
  transfers between devices with their start and end apart: 6, of which 3 were waited for; matrix products, arithmetic and copies ran while one was open for 0% of the time, Pallas kernels for 5%

profile of v8, /device:TPU:1, one launch (start us, length us, event | category | flops | bytes accessed | tf_op | source)
XLA Modules:
  0.0 90.7 jit_solution(12267005912386679087)
XLA Ops:
  0.6 1.1 %fusion = (bf16[4,1,96,192]{3,2,1,0:T(8,128)(2,1)S(1)}, bf16[4,1,96,192]{3,2,1,0:T(8,128)(2,1)S(1)}) fusion(bf16[4,4,96,192]{3,2,1,0:T(8,128)(2,1)} %bitcast.14), kind=kLoop, calls=%fused_computation | loop fusion | bytes 589824 | tf_op jit(solution)/shard_map/slice | solution.py:316
  1.7 4.8 %collective-permute-start.1 = (bf16[4,1,96,192]{3,2,1,0:T(8,128)(2,1)S(1)}, bf16[4,1,96,192]{3,2,1,0:T(8,128)(2,1)S(1)}, u32[]{:S(2)}, u32[]{:S(2)}) collective-permute-start(bf16[4,1,96,192]{3,2,1,0:T(8,128)(2,1)S(1)} %get-tuple-element.48), channel_id=1, source_target_pairs={{0,2},{2,4},{4,6},{6,8},{8,10},{10,12},{12,14},{14,16},{16,18},{18... | collective-permute-start | bytes 442376 | tf_op jit(solution)/shard_map/ppermute | solution.py:315
  6.5 1.3 %collective-permute-start.2 = (bf16[4,1,96,192]{3,2,1,0:T(8,128)(2,1)S(1)}, bf16[4,1,96,192]{3,2,1,0:T(8,128)(2,1)S(1)}, u32[]{:S(2)}, u32[]{:S(2)}) collective-permute-start(bf16[4,1,96,192]{3,2,1,0:T(8,128)(2,1)S(1)} %get-tuple-element.47), channel_id=1, source_target_pairs={{2,0},{4,2},{6,4},{8,6},{10,8},{12,10},{14,12},{16,14},{18,16},{20... | collective-permute-start | bytes 442376 | tf_op jit(solution)/shard_map/ppermute | solution.py:316
  7.8 3.2 %collective-permute-start = (bf16[192,384]{1,0:T(8,128)(2,1)}, bf16[192,384]{1,0:T(8,128)(2,1)S(1)}, u32[]{:S(2)}, u32[]{:S(2)}) collective-permute-start(bf16[192,384]{1,0:T(8,128)(2,1)} %bitcast.17), channel_id=1, source_target_pairs={{0,64},{64,128},{128,192},{192,256},{256,320},{320,384},{384,448},... | collective-permute-start | bytes 442376 | tf_op jit(solution)/shard_map/ppermute | solution.py:317
  11.1 2.9 %inner_terms.1 = (bf16[4,4,96,192]{3,2,1,0:T(8,128)(2,1)S(1)}, bf16[192,384]{1,0:T(8,128)(2,1)S(1)}, bf16[3,384,768]{2,1,0:T(8,128)(2,1)S(1)}, bf16[9,192,384]{2...) custom-call(bf16[4,4,96,192]{3,2,1,0:T(8,128)(2,1)} %bitcast.15, ...), custom_call_target="tpu_custom_call" | custom-call | flops 1500000000 | bytes 6000000 | tf_op jit(solution)/shard_map/inner_terms/pallas_call | solution.py:89
  14.0 0.0 collective-permute-done.1.low
  14.0 0.0 collective-permute-done.2.high
  14.0 0.8 grad_terms.1
  14.8 0.0 collective-permute-done.carried
  14.8 2.2 %block_terms.1 = (bf16[2,2,2,2,2,4,48,128]{7,6,5,4,3,2,1,0:T(8,128)(2,1)S(1)}, bf16[2,2,2,2,2,4,48,128]{7,6,5,4,3,2,1,0:T(8,128)(2,1)S(1)}) custom-call(bf16[192,384]{1,0:T(8,128)(2,1)S(1)} %get-tuple-element.25.video, bf16[192,384]{1,0:T(8,128)(2,1)S(1)} %collective-permute-done.carried, bf16[3,384,768]{2,1,0:T(8,128)(2,1)S(1)} %get-tuple-element.26.w_time, ...), custom_call_target="tpu_custom_call" | custom-call | flops 3000000000 | bytes 12000000 | tf_op jit(solution)/shard_map/block_terms/pallas_call | solution.py:189
  17.0 5.4 %collective-permute-start.3 = (bf16[2,2,2,2,2,4,48,128]{7,6,5,4,3,2,1,0:T(8,128)(2,1)S(1)}, bf16[2,2,2,2,2,4,48,128]{7,6,5,4,3,2,1,0:T(8,128)(2,1)S(1)}, u32[]{:S(2)}, u32[]{:S(2)}) collective-permute-start(bf16[2,2,2,2,2,4,48,128]{7,6,5,4,3,2,1,0:T(8,128)(2,1)S(1)} %get-tuple-element.35), channel_id=1, source_target_pairs={{0,1},{1,0},{2,3},{3,2},{4,5},{5,4},{6,7},{7,6},{8,9},{9,8},{10,11... | collective-permute-start | bytes 4718600 | tf_op jit(solution)/shard_map/ppermute | solution.py:322
  22.4 1.2 %video_terms.1 = (f32[192,384]{1,0:T(8,128)S(1)}, bf16[192,384]{1,0:T(8,128)(2,1)S(1)}) custom-call(bf16[192,768]{1,0:T(8,128)(2,1)S(1)} %get-tuple-element.32.grad_hidden, bf16[3,384,768]{2,1,0:T(8,128)(2,1)S(1)} %get-tuple-element.26.w_time), custom_call_target="tpu_custom_call" | custom-call | flops 700000000 | bytes 2500000 | tf_op jit(solution)/shard_map/video_terms/pallas_call | solution.py:287
  23.6 1.9 %collective-permute-done.3 = bf16[2,2,2,2,2,4,48,128]{7,6,5,4,3,2,1,0:T(8,128)(2,1)S(1)} collective-permute-done((bf16[2,2,2,2,2,4,48,128]{7,6,5,4,3,2,1,0:T(8,128)(2,1)S(1)}, bf16[2,2,2,2,2,4,48,128]{7,6,5,4,3,2,1,0:T(8,128)(2,1)S(1)}, u32[]{:S(2)}, u32[]{:S(2)}) %collective-permute-start.3) | collective-permute-done | bytes 1572896 | tf_op jit(solution)/shard_map/ppermute | solution.py:322
  25.4 0.4 pair_sum.1
  25.8 29.4 %all_to_all.15.refs_0_ = bf16[8,768,128]{2,1,0:T(8,128)(2,1)S(1)} all-to-all(bf16[8,768,128]{2,1,0:T(8,128)(2,1)S(1)} %bitcast.11), channel_id=1, replica_groups={{0,64,2,66,16,80,18,82},{4,68,6,70,20,84,22,86},{8,72,10,74,24,88,26,90..., dimensions={0} | all-to-all | bytes 3145728 | tf_op jit(solution)/shard_map/all_to_all | solution.py:307
  55.2 0.9 group_sum.2
  56.1 3.5 %all-to-all-start.1 = ((bf16[16,48,128]{2,1,0:T(8,128)(2,1)}), bf16[16,48,128]{2,1,0:T(8,128)(2,1)S(1)}, u32[]{:S(2)}, u32[]{:S(2)}) async-start(bf16[16,48,128]{2,1,0:T(8,128)(2,1)} %bitcast.7), calls=%async_computation.1 | async-start | bytes 393216 | tf_op jit(solution)/shard_map/all_to_all | solution.py:307
  59.6 1.3 %collective-permute-start.4 = (bf16[192,384]{1,0:T(8,128)(2,1)S(1)}, bf16[192,384]{1,0:T(8,128)(2,1)S(1)}, u32[]{:S(2)}, u32[]{:S(2)}) collective-permute-start(bf16[192,384]{1,0:T(8,128)(2,1)S(1)} %get-tuple-element.40), channel_id=1, source_target_pairs={{64,0},{128,64},{192,128},{256,192},{320,256},{384,320},{448,384},... | collective-permute-start | bytes 442376 | tf_op jit(solution)/shard_map/ppermute | solution.py:359
  60.9 7.4 %collective-permute-done.4.refs_2_ = bf16[192,384]{1,0:T(8,128)(2,1)S(1)} collective-permute-done((bf16[192,384]{1,0:T(8,128)(2,1)S(1)}, bf16[192,384]{1,0:T(8,128)(2,1)S(1)}, u32[]{:S(2)}, u32[]{:S(2)}) %collective-permute-start.4) | collective-permute-done | bytes 147488 | tf_op jit(solution)/shard_map/ppermute | solution.py:359
  68.3 5.7 %all-to-all-done.1.refs_0_ = bf16[16,48,128]{2,1,0:T(8,128)(2,1)S(1)} async-done(((bf16[16,48,128]{2,1,0:T(8,128)(2,1)}), bf16[16,48,128]{2,1,0:T(8,128)(2,1)S(1)}, u32[]{:S(2)}, u32[]{:S(2)}) %all-to-all-start.1) | async-done | bytes 196640 | tf_op jit(solution)/shard_map/all_to_all | solution.py:307
  74.1 15.7 %all_to_all.16.refs_0_ = bf16[16,48,128]{2,1,0:T(8,128)(2,1)S(1)} all-to-all(bf16[16,48,128]{2,1,0:T(8,128)(2,1)S(1)} %group_sum.3), channel_id=1, replica_groups=mesh['chain'=8,'rows'=32,'clip'=2] {'chain','clip'}, dimensions={0} | all-to-all | bytes 393216 | tf_op jit(solution)/shard_map/all_to_all | solution.py:307
  89.8 0.9 unpack.1
  (1 shorter events, 0.0 us)
Async XLA Ops:
  1.7 12.3 %collective-permute-start.1 = (bf16[4,1,96,192]{3,2,1,0:T(8,128)(2,1)S(1)}, bf16[4,1,96,192]{3,2,1,0:T(8,128)(2,1)S(1)}, u32[]{:S(2)}, u32[]{:S(2)}) collective-permute-start(bf16[4,1,96,192]{3,2,1,0:T(8,128)(2,1)S(1)} %get-tuple-element.48), channel_id=1, source_target_pairs={{0,2},{2,4},{4,6},{6,8},{8,10},{10,12},{12,14},{14,16},{16,18},{18... | collective-permute-start | bytes 442376 | tf_op jit(solution)/shard_map/ppermute | solution.py:315
  6.5 7.4 %collective-permute-start.2 = (bf16[4,1,96,192]{3,2,1,0:T(8,128)(2,1)S(1)}, bf16[4,1,96,192]{3,2,1,0:T(8,128)(2,1)S(1)}, u32[]{:S(2)}, u32[]{:S(2)}) collective-permute-start(bf16[4,1,96,192]{3,2,1,0:T(8,128)(2,1)S(1)} %get-tuple-element.47), channel_id=1, source_target_pairs={{2,0},{4,2},{6,4},{8,6},{10,8},{12,10},{14,12},{16,14},{18,16},{20... | collective-permute-start | bytes 442376 | tf_op jit(solution)/shard_map/ppermute | solution.py:316
  7.8 7.0 %collective-permute-start = (bf16[192,384]{1,0:T(8,128)(2,1)}, bf16[192,384]{1,0:T(8,128)(2,1)S(1)}, u32[]{:S(2)}, u32[]{:S(2)}) collective-permute-start(bf16[192,384]{1,0:T(8,128)(2,1)} %bitcast.17), channel_id=1, source_target_pairs={{0,64},{64,128},{128,192},{192,256},{256,320},{320,384},{384,448},... | collective-permute-start | bytes 442376 | tf_op jit(solution)/shard_map/ppermute | solution.py:317
  17.0 8.4 %collective-permute-start.3 = (bf16[2,2,2,2,2,4,48,128]{7,6,5,4,3,2,1,0:T(8,128)(2,1)S(1)}, bf16[2,2,2,2,2,4,48,128]{7,6,5,4,3,2,1,0:T(8,128)(2,1)S(1)}, u32[]{:S(2)}, u32[]{:S(2)}) collective-permute-start(bf16[2,2,2,2,2,4,48,128]{7,6,5,4,3,2,1,0:T(8,128)(2,1)S(1)} %get-tuple-element.35), channel_id=1, source_target_pairs={{0,1},{1,0},{2,3},{3,2},{4,5},{5,4},{6,7},{7,6},{8,9},{9,8},{10,11... | collective-permute-start | bytes 4718600 | tf_op jit(solution)/shard_map/ppermute | solution.py:322
  56.1 18.0 %all-to-all-start.1 = ((bf16[16,48,128]{2,1,0:T(8,128)(2,1)}), bf16[16,48,128]{2,1,0:T(8,128)(2,1)S(1)}, u32[]{:S(2)}, u32[]{:S(2)}) async-start(bf16[16,48,128]{2,1,0:T(8,128)(2,1)} %bitcast.7), calls=%async_computation.1 | async-start | bytes 393216 | tf_op jit(solution)/shard_map/all_to_all | solution.py:307
  59.6 8.7 %collective-permute-start.4 = (bf16[192,384]{1,0:T(8,128)(2,1)S(1)}, bf16[192,384]{1,0:T(8,128)(2,1)S(1)}, u32[]{:S(2)}, u32[]{:S(2)}) collective-permute-start(bf16[192,384]{1,0:T(8,128)(2,1)S(1)} %get-tuple-element.40), channel_id=1, source_target_pairs={{64,0},{128,64},{192,128},{256,192},{320,256},{384,320},{448,384},... | collective-permute-start | bytes 442376 | tf_op jit(solution)/shard_map/ppermute | solution.py:359

commit v9 on v8

--- a/solution.py
+++ b/solution.py
@@ -355,10 +355,9 @@
     ]
     share = pair_sum(keep.reshape(-1, LANES), received.reshape(-1, LANES))
     share = group_sum(exchange(share.reshape(8, -1, LANES), ("chain", "rows", "clip"), near))
+    share = group_sum(exchange(share.reshape(2 * N_Z, PIECE, LANES), ("chain", "rows"), far), 2 * chain)
     share, returned = lax.optimization_barrier((share, returned))
     following = lax.ppermute(returned, "chain", along("chain", -1))
-    share, following = lax.optimization_barrier((exchange(share.reshape(2 * N_Z, PIECE, LANES), ("chain", "rows"), far), following))
-    share = group_sum(share, 2 * chain)
     pieces = exchange(share, ("chain", "clip"))
     voxels = 2 * chain * 2 * FRAMES * rows * 2 * BAND * 2 * COLS
     grad_time, grad_space, grad_video = unpack(pieces, ours, following, 1.0 / math.sqrt(voxels))

time: 91.1 us -> 91 us (level)
  waiting for transfers between devices: 15 us -> 10.9 us
  starting transfers between devices: 19.5 us -> 21.8 us
  blocking collectives: 45.1 us -> 47 us
    all_to_all x1, waiting for transfers between devices: 5.75 us -> 0.6 us  [exchange(): lax.all_to_all(parts, axes, 0, 0, tiled=True, axis_index_groups=groups)]
    all_to_all x1, starting transfers between devices: 3.52 us -> 5.77 us  [exchange(): lax.all_to_all(parts, axes, 0, 0, tiled=True, axis_index_groups=groups)]
    all_to_all x2, blocking collectives: 45.1 us -> 47 us  [exchange(): lax.all_to_all(parts, axes, 0, 0, tiled=True, axis_index_groups=groups)]
    ppermute x1, waiting for transfers between devices: 7.43 us -> 8.44 us  [local(): following = lax.ppermute(returned, 'chain', along('chain', -1))]
where the time goes in v9:
time: 91 us; the launch traced here: 90.6 us
  blocking collectives  47 us (52%)
  starting transfers between devices  21.8 us (24%)
  waiting for transfers between devices  10.9 us (12%)
  Pallas kernels  9.23 us (10%)
  local copies, waits for them, and re-layouts  1.05 us (1%)
    all_to_all x2, blocking collectives, exchange(): lax.all_to_all(parts, axes, 0, 0, tiled=True, axis_index_groups=groups)  47 us
    ppermute x1, waiting for transfers between devices, local(): following = lax.ppermute(returned, 'chain', along('chain', -1))  8.44 us
    all_to_all x1, starting transfers between devices, exchange(): lax.all_to_all(parts, axes, 0, 0, tiled=True, axis_index_groups=groups)  5.77 us
    ppermute x1, starting transfers between devices, local(): received = lax.ppermute(send, 'clip', [(0, 1), (1, 0)])  5.37 us
    ppermute x1, starting transfers between devices, local(): low = lax.ppermute(cot[:, 2 * BAND - 1:], 'rows', along('rows', 1))  4.84 us
    ppermute x1, starting transfers between devices, local(): carried = lax.ppermute(own, 'chain', along('chain', 1))  3.21 us
    pallas_call x1, Pallas kernels, inner_terms(): pl.pallas_call(inner_kernel, name='inner_terms', out_shape=(*(jax.ShapeDt...  2.9 us
    pallas_call x1, Pallas kernels, block_terms(): pl.pallas_call(block_kernel, name='block_terms', out_shape=(half, half),...  2.19 us
  transfers between devices with their start and end apart: 6, of which 3 were waited for; matrix products, arithmetic and copies ran while one was open for 0% of the time, Pallas kernels for 5%

profile of v9, /device:TPU:1, one launch (start us, length us, event | category | flops | bytes accessed | tf_op | source)
XLA Modules:
  0.0 90.6 jit_solution(13113956892235813184)
XLA Ops:
  0.6 1.1 %fusion = (bf16[4,1,96,192]{3,2,1,0:T(8,128)(2,1)S(1)}, bf16[4,1,96,192]{3,2,1,0:T(8,128)(2,1)S(1)}) fusion(bf16[4,4,96,192]{3,2,1,0:T(8,128)(2,1)} %bitcast.15), kind=kLoop, calls=%fused_computation | loop fusion | bytes 589824 | tf_op jit(solution)/shard_map/slice | solution.py:316
  1.7 4.8 %collective-permute-start.1 = (bf16[4,1,96,192]{3,2,1,0:T(8,128)(2,1)S(1)}, bf16[4,1,96,192]{3,2,1,0:T(8,128)(2,1)S(1)}, u32[]{:S(2)}, u32[]{:S(2)}) collective-permute-start(bf16[4,1,96,192]{3,2,1,0:T(8,128)(2,1)S(1)} %get-tuple-element.44), channel_id=1, source_target_pairs={{0,2},{2,4},{4,6},{6,8},{8,10},{10,12},{12,14},{14,16},{16,18},{18... | collective-permute-start | bytes 442376 | tf_op jit(solution)/shard_map/ppermute | solution.py:315
  6.5 1.3 %collective-permute-start.2 = (bf16[4,1,96,192]{3,2,1,0:T(8,128)(2,1)S(1)}, bf16[4,1,96,192]{3,2,1,0:T(8,128)(2,1)S(1)}, u32[]{:S(2)}, u32[]{:S(2)}) collective-permute-start(bf16[4,1,96,192]{3,2,1,0:T(8,128)(2,1)S(1)} %get-tuple-element.43), channel_id=1, source_target_pairs={{2,0},{4,2},{6,4},{8,6},{10,8},{12,10},{14,12},{16,14},{18,16},{20... | collective-permute-start | bytes 442376 | tf_op jit(solution)/shard_map/ppermute | solution.py:316
  7.8 3.2 %collective-permute-start = (bf16[192,384]{1,0:T(8,128)(2,1)}, bf16[192,384]{1,0:T(8,128)(2,1)S(1)}, u32[]{:S(2)}, u32[]{:S(2)}) collective-permute-start(bf16[192,384]{1,0:T(8,128)(2,1)} %bitcast.18), channel_id=1, source_target_pairs={{0,64},{64,128},{128,192},{192,256},{256,320},{320,384},{384,448},... | collective-permute-start | bytes 442376 | tf_op jit(solution)/shard_map/ppermute | solution.py:317
  11.1 2.9 %inner_terms.1 = (bf16[4,4,96,192]{3,2,1,0:T(8,128)(2,1)S(1)}, bf16[192,384]{1,0:T(8,128)(2,1)S(1)}, bf16[3,384,768]{2,1,0:T(8,128)(2,1)S(1)}, bf16[9,192,384]{2...) custom-call(bf16[4,4,96,192]{3,2,1,0:T(8,128)(2,1)} %bitcast.16, ...), custom_call_target="tpu_custom_call" | custom-call | flops 1500000000 | bytes 6000000 | tf_op jit(solution)/shard_map/inner_terms/pallas_call | solution.py:89
  14.0 0.0 collective-permute-done.1.low
  14.0 0.0 collective-permute-done.2.high
  14.0 0.8 grad_terms.1
  14.8 0.0 collective-permute-done.carried
  14.8 2.2 %block_terms.1 = (bf16[2,2,2,2,2,4,48,128]{7,6,5,4,3,2,1,0:T(8,128)(2,1)S(1)}, bf16[2,2,2,2,2,4,48,128]{7,6,5,4,3,2,1,0:T(8,128)(2,1)S(1)}) custom-call(bf16[192,384]{1,0:T(8,128)(2,1)S(1)} %get-tuple-element.23.video, bf16[192,384]{1,0:T(8,128)(2,1)S(1)} %collective-permute-done.carried, bf16[3,384,768]{2,1,0:T(8,128)(2,1)S(1)} %get-tuple-element.24.w_time, ...), custom_call_target="tpu_custom_call" | custom-call | flops 3000000000 | bytes 12000000 | tf_op jit(solution)/shard_map/block_terms/pallas_call | solution.py:189
  17.0 5.4 %collective-permute-start.3 = (bf16[2,2,2,2,2,4,48,128]{7,6,5,4,3,2,1,0:T(8,128)(2,1)S(1)}, bf16[2,2,2,2,2,4,48,128]{7,6,5,4,3,2,1,0:T(8,128)(2,1)S(1)}, u32[]{:S(2)}, u32[]{:S(2)}) collective-permute-start(bf16[2,2,2,2,2,4,48,128]{7,6,5,4,3,2,1,0:T(8,128)(2,1)S(1)} %get-tuple-element.33), channel_id=1, source_target_pairs={{0,1},{1,0},{2,3},{3,2},{4,5},{5,4},{6,7},{7,6},{8,9},{9,8},{10,11... | collective-permute-start | bytes 4718600 | tf_op jit(solution)/shard_map/ppermute | solution.py:322
  22.4 1.2 %video_terms.1 = (f32[192,384]{1,0:T(8,128)S(1)}, bf16[192,384]{1,0:T(8,128)(2,1)S(1)}) custom-call(bf16[192,768]{1,0:T(8,128)(2,1)S(1)} %get-tuple-element.30.grad_hidden, bf16[3,384,768]{2,1,0:T(8,128)(2,1)S(1)} %get-tuple-element.24.w_time), custom_call_target="tpu_custom_call" | custom-call | flops 700000000 | bytes 2500000 | tf_op jit(solution)/shard_map/video_terms/pallas_call | solution.py:287
  23.6 1.9 %collective-permute-done.3 = bf16[2,2,2,2,2,4,48,128]{7,6,5,4,3,2,1,0:T(8,128)(2,1)S(1)} collective-permute-done((bf16[2,2,2,2,2,4,48,128]{7,6,5,4,3,2,1,0:T(8,128)(2,1)S(1)}, bf16[2,2,2,2,2,4,48,128]{7,6,5,4,3,2,1,0:T(8,128)(2,1)S(1)}, u32[]{:S(2)}, u32[]{:S(2)}) %collective-permute-start.3) | collective-permute-done | bytes 1572896 | tf_op jit(solution)/shard_map/ppermute | solution.py:322
  25.4 0.4 pair_sum.1
  25.8 29.4 %all_to_all.15.refs_0_ = bf16[8,768,128]{2,1,0:T(8,128)(2,1)S(1)} all-to-all(bf16[8,768,128]{2,1,0:T(8,128)(2,1)S(1)} %bitcast.11), channel_id=1, replica_groups={{0,64,2,66,16,80,18,82},{4,68,6,70,20,84,22,86},{8,72,10,74,24,88,26,90..., dimensions={0} | all-to-all | bytes 3145728 | tf_op jit(solution)/shard_map/all_to_all | solution.py:307
  55.2 0.2 group_sum.2
  55.4 17.5 %all_to_all.16.refs_0_ = bf16[16,48,128]{2,1,0:T(8,128)(2,1)S(1)} all-to-all(bf16[16,48,128]{2,1,0:T(8,128)(2,1)S(1)} %bitcast.14), channel_id=1, replica_groups={{0,4,8,12,128,132,136,140,32,36,40,44,160,164,168,172},{2,6,10,14,130,1..., dimensions={0} | all-to-all | bytes 393216 | tf_op jit(solution)/shard_map/all_to_all | solution.py:307
  73.0 0.7 group_sum.3
  73.7 5.8 %all-to-all-start.2 = ((bf16[16,48,128]{2,1,0:T(8,128)(2,1)}), bf16[16,48,128]{2,1,0:T(8,128)(2,1)S(1)}, u32[]{:S(2)}, u32[]{:S(2)}) async-start(bf16[16,48,128]{2,1,0:T(8,128)(2,1)} %group_sum.3), calls=%async_computation.2 | async-start | bytes 393216 | tf_op jit(solution)/shard_map/all_to_all | solution.py:307
  79.4 1.3 %collective-permute-start.4 = (bf16[192,384]{1,0:T(8,128)(2,1)S(1)}, bf16[192,384]{1,0:T(8,128)(2,1)S(1)}, u32[]{:S(2)}, u32[]{:S(2)}) collective-permute-start(bf16[192,384]{1,0:T(8,128)(2,1)S(1)} %get-tuple-element.39), channel_id=1, source_target_pairs={{64,0},{128,64},{192,128},{256,192},{320,256},{384,320},{448,384},... | collective-permute-start | bytes 442376 | tf_op jit(solution)/shard_map/ppermute | solution.py:360
  80.7 8.4 %collective-permute-done.4.refs_2_ = bf16[192,384]{1,0:T(8,128)(2,1)S(1)} collective-permute-done((bf16[192,384]{1,0:T(8,128)(2,1)S(1)}, bf16[192,384]{1,0:T(8,128)(2,1)S(1)}, u32[]{:S(2)}, u32[]{:S(2)}) %collective-permute-start.4) | collective-permute-done | bytes 147488 | tf_op jit(solution)/shard_map/ppermute | solution.py:360
  89.2 0.6 all-to-all-done.2.refs_0_
  89.8 0.9 unpack.1
Async XLA Ops:
  1.7 12.3 %collective-permute-start.1 = (bf16[4,1,96,192]{3,2,1,0:T(8,128)(2,1)S(1)}, bf16[4,1,96,192]{3,2,1,0:T(8,128)(2,1)S(1)}, u32[]{:S(2)}, u32[]{:S(2)}) collective-permute-start(bf16[4,1,96,192]{3,2,1,0:T(8,128)(2,1)S(1)} %get-tuple-element.44), channel_id=1, source_target_pairs={{0,2},{2,4},{4,6},{6,8},{8,10},{10,12},{12,14},{14,16},{16,18},{18... | collective-permute-start | bytes 442376 | tf_op jit(solution)/shard_map/ppermute | solution.py:315
  6.5 7.4 %collective-permute-start.2 = (bf16[4,1,96,192]{3,2,1,0:T(8,128)(2,1)S(1)}, bf16[4,1,96,192]{3,2,1,0:T(8,128)(2,1)S(1)}, u32[]{:S(2)}, u32[]{:S(2)}) collective-permute-start(bf16[4,1,96,192]{3,2,1,0:T(8,128)(2,1)S(1)} %get-tuple-element.43), channel_id=1, source_target_pairs={{2,0},{4,2},{6,4},{8,6},{10,8},{12,10},{14,12},{16,14},{18,16},{20... | collective-permute-start | bytes 442376 | tf_op jit(solution)/shard_map/ppermute | solution.py:316
  7.8 7.0 %collective-permute-start = (bf16[192,384]{1,0:T(8,128)(2,1)}, bf16[192,384]{1,0:T(8,128)(2,1)S(1)}, u32[]{:S(2)}, u32[]{:S(2)}) collective-permute-start(bf16[192,384]{1,0:T(8,128)(2,1)} %bitcast.18), channel_id=1, source_target_pairs={{0,64},{64,128},{128,192},{192,256},{256,320},{320,384},{384,448},... | collective-permute-start | bytes 442376 | tf_op jit(solution)/shard_map/ppermute | solution.py:317
  17.0 8.4 %collective-permute-start.3 = (bf16[2,2,2,2,2,4,48,128]{7,6,5,4,3,2,1,0:T(8,128)(2,1)S(1)}, bf16[2,2,2,2,2,4,48,128]{7,6,5,4,3,2,1,0:T(8,128)(2,1)S(1)}, u32[]{:S(2)}, u32[]{:S(2)}) collective-permute-start(bf16[2,2,2,2,2,4,48,128]{7,6,5,4,3,2,1,0:T(8,128)(2,1)S(1)} %get-tuple-element.33), channel_id=1, source_target_pairs={{0,1},{1,0},{2,3},{3,2},{4,5},{5,4},{6,7},{7,6},{8,9},{9,8},{10,11... | collective-permute-start | bytes 4718600 | tf_op jit(solution)/shard_map/ppermute | solution.py:322
  73.7 16.1 %all-to-all-start.2 = ((bf16[16,48,128]{2,1,0:T(8,128)(2,1)}), bf16[16,48,128]{2,1,0:T(8,128)(2,1)S(1)}, u32[]{:S(2)}, u32[]{:S(2)}) async-start(bf16[16,48,128]{2,1,0:T(8,128)(2,1)} %group_sum.3), calls=%async_computation.2 | async-start | bytes 393216 | tf_op jit(solution)/shard_map/all_to_all | solution.py:307
  79.4 9.7 %collective-permute-start.4 = (bf16[192,384]{1,0:T(8,128)(2,1)S(1)}, bf16[192,384]{1,0:T(8,128)(2,1)S(1)}, u32[]{:S(2)}, u32[]{:S(2)}) collective-permute-start(bf16[192,384]{1,0:T(8,128)(2,1)S(1)} %get-tuple-element.39), channel_id=1, source_target_pairs={{64,0},{128,64},{192,128},{256,192},{320,256},{384,320},{448,384},... | collective-permute-start | bytes 442376 | tf_op jit(solution)/shard_map/ppermute | solution.py:360

commit v10 on v9

--- a/solution.py
+++ b/solution.py
@@ -354,10 +354,11 @@
         for zl in range(2)
     ]
     share = pair_sum(keep.reshape(-1, LANES), received.reshape(-1, LANES))
-    share = group_sum(exchange(share.reshape(8, -1, LANES), ("chain", "rows", "clip"), near))
-    share = group_sum(exchange(share.reshape(2 * N_Z, PIECE, LANES), ("chain", "rows"), far), 2 * chain)
     share, returned = lax.optimization_barrier((share, returned))
     following = lax.ppermute(returned, "chain", along("chain", -1))
+    share = exchange(share.reshape(8, -1, LANES), ("chain", "rows", "clip"), near)
+    share, following = lax.optimization_barrier((share, following))
+    share = group_sum(exchange(group_sum(share).reshape(2 * N_Z, PIECE, LANES), ("chain", "rows"), far), 2 * chain)
     pieces = exchange(share, ("chain", "clip"))
     voxels = 2 * chain * 2 * FRAMES * rows * 2 * BAND * 2 * COLS
     grad_time, grad_space, grad_video = unpack(pieces, ours, following, 1.0 / math.sqrt(voxels))

time: 91 us -> 91.7 us (level)
  blocking collectives: 47 us -> 33.7 us
  starting transfers between devices: 21.8 us -> 29.1 us
  waiting for transfers between devices: 10.9 us -> 17 us
    all_to_all x2, blocking collectives: 47 us -> 33.7 us  [exchange(): lax.all_to_all(parts, axes, 0, 0, tiled=True, axis_index_groups=groups)]
    all_to_all x1, waiting for transfers between devices: 0.6 us -> 8.6 us  [exchange(): lax.all_to_all(parts, axes, 0, 0, tiled=True, axis_index_groups=groups)]
    all_to_all x1, starting transfers between devices: 5.77 us -> 13.1 us  [exchange(): lax.all_to_all(parts, axes, 0, 0, tiled=True, axis_index_groups=groups)]
    ppermute x1, waiting for transfers between devices: 8.44 us -> 6.59 us  [local(): following = lax.ppermute(returned, 'chain', along('chain', -1))]
    pallas_call x1, Pallas kernels: 0.36 us -> 1.52 us  [pair_sum(): pl.pallas_call(pair_kernel, name='pair_sum', out_shape=jax.ShapeDtypeStru...]
where the time goes in v10:
time: 91.7 us; the launch traced here: 91.4 us
  blocking collectives  33.7 us (37%)
  starting transfers between devices  29.1 us (32%)
  waiting for transfers between devices  17 us (19%)
  Pallas kernels  9.72 us (11%)
  local copies, waits for them, and re-layouts  1.05 us (1%)
    all_to_all x2, blocking collectives, exchange(): lax.all_to_all(parts, axes, 0, 0, tiled=True, axis_index_groups=groups)  33.7 us
    all_to_all x1, starting transfers between devices, exchange(): lax.all_to_all(parts, axes, 0, 0, tiled=True, axis_index_groups=groups)  13.1 us
    all_to_all x1, waiting for transfers between devices, exchange(): lax.all_to_all(parts, axes, 0, 0, tiled=True, axis_index_groups=groups)  8.6 us
    ppermute x1, waiting for transfers between devices, local(): following = lax.ppermute(returned, 'chain', along('chain', -1))  6.59 us
    ppermute x1, starting transfers between devices, local(): received = lax.ppermute(send, 'clip', [(0, 1), (1, 0)])  5.37 us
    ppermute x1, starting transfers between devices, local(): low = lax.ppermute(cot[:, 2 * BAND - 1:], 'rows', along('rows', 1))  4.84 us
    ppermute x1, starting transfers between devices, local(): carried = lax.ppermute(own, 'chain', along('chain', 1))  3.21 us
    pallas_call x1, Pallas kernels, inner_terms(): pl.pallas_call(inner_kernel, name='inner_terms', out_shape=(*(jax.ShapeDt...  2.9 us
  transfers between devices with their start and end apart: 6, of which 3 were waited for; matrix products, arithmetic and copies ran while one was open for 0% of the time, Pallas kernels for 5%

profile of v10, /device:TPU:1, one launch (start us, length us, event | category | flops | bytes accessed | tf_op | source)
XLA Modules:
  0.0 91.4 jit_solution(11619653157721425037)
XLA Ops:
  0.6 1.1 %fusion = (bf16[4,1,96,192]{3,2,1,0:T(8,128)(2,1)S(1)}, bf16[4,1,96,192]{3,2,1,0:T(8,128)(2,1)S(1)}) fusion(bf16[4,4,96,192]{3,2,1,0:T(8,128)(2,1)} %bitcast.14), kind=kLoop, calls=%fused_computation | loop fusion | bytes 589824 | tf_op jit(solution)/shard_map/slice | solution.py:316
  1.7 4.8 %collective-permute-start.1 = (bf16[4,1,96,192]{3,2,1,0:T(8,128)(2,1)S(1)}, bf16[4,1,96,192]{3,2,1,0:T(8,128)(2,1)S(1)}, u32[]{:S(2)}, u32[]{:S(2)}) collective-permute-start(bf16[4,1,96,192]{3,2,1,0:T(8,128)(2,1)S(1)} %get-tuple-element.48), channel_id=1, source_target_pairs={{0,2},{2,4},{4,6},{6,8},{8,10},{10,12},{12,14},{14,16},{16,18},{18... | collective-permute-start | bytes 442376 | tf_op jit(solution)/shard_map/ppermute | solution.py:315
  6.5 1.3 %collective-permute-start.2 = (bf16[4,1,96,192]{3,2,1,0:T(8,128)(2,1)S(1)}, bf16[4,1,96,192]{3,2,1,0:T(8,128)(2,1)S(1)}, u32[]{:S(2)}, u32[]{:S(2)}) collective-permute-start(bf16[4,1,96,192]{3,2,1,0:T(8,128)(2,1)S(1)} %get-tuple-element.47), channel_id=1, source_target_pairs={{2,0},{4,2},{6,4},{8,6},{10,8},{12,10},{14,12},{16,14},{18,16},{20... | collective-permute-start | bytes 442376 | tf_op jit(solution)/shard_map/ppermute | solution.py:316
  7.8 3.2 %collective-permute-start = (bf16[192,384]{1,0:T(8,128)(2,1)}, bf16[192,384]{1,0:T(8,128)(2,1)S(1)}, u32[]{:S(2)}, u32[]{:S(2)}) collective-permute-start(bf16[192,384]{1,0:T(8,128)(2,1)} %bitcast.17), channel_id=1, source_target_pairs={{0,64},{64,128},{128,192},{192,256},{256,320},{320,384},{384,448},... | collective-permute-start | bytes 442376 | tf_op jit(solution)/shard_map/ppermute | solution.py:317
  11.1 2.9 %inner_terms.1 = (bf16[4,4,96,192]{3,2,1,0:T(8,128)(2,1)S(1)}, bf16[192,384]{1,0:T(8,128)(2,1)S(1)}, bf16[3,384,768]{2,1,0:T(8,128)(2,1)S(1)}, bf16[9,192,384]{2...) custom-call(bf16[4,4,96,192]{3,2,1,0:T(8,128)(2,1)} %bitcast.15, ...), custom_call_target="tpu_custom_call" | custom-call | flops 1500000000 | bytes 6000000 | tf_op jit(solution)/shard_map/inner_terms/pallas_call | solution.py:89
  14.0 0.0 collective-permute-done.1.low
  14.0 0.0 collective-permute-done.2.high
  14.0 0.8 grad_terms.1
  14.8 0.0 collective-permute-done.carried
  14.8 2.2 %block_terms.1 = (bf16[2,2,2,2,2,4,48,128]{7,6,5,4,3,2,1,0:T(8,128)(2,1)S(1)}, bf16[2,2,2,2,2,4,48,128]{7,6,5,4,3,2,1,0:T(8,128)(2,1)S(1)}) custom-call(bf16[192,384]{1,0:T(8,128)(2,1)S(1)} %get-tuple-element.25.video, bf16[192,384]{1,0:T(8,128)(2,1)S(1)} %collective-permute-done.carried, bf16[3,384,768]{2,1,0:T(8,128)(2,1)S(1)} %get-tuple-element.26.w_time, ...), custom_call_target="tpu_custom_call" | custom-call | flops 3000000000 | bytes 12000000 | tf_op jit(solution)/shard_map/block_terms/pallas_call | solution.py:189
  17.0 5.4 %collective-permute-start.3 = (bf16[2,2,2,2,2,4,48,128]{7,6,5,4,3,2,1,0:T(8,128)(2,1)S(1)}, bf16[2,2,2,2,2,4,48,128]{7,6,5,4,3,2,1,0:T(8,128)(2,1)S(1)}, u32[]{:S(2)}, u32[]{:S(2)}) collective-permute-start(bf16[2,2,2,2,2,4,48,128]{7,6,5,4,3,2,1,0:T(8,128)(2,1)S(1)} %get-tuple-element.35), channel_id=1, source_target_pairs={{0,1},{1,0},{2,3},{3,2},{4,5},{5,4},{6,7},{7,6},{8,9},{9,8},{10,11... | collective-permute-start | bytes 4718600 | tf_op jit(solution)/shard_map/ppermute | solution.py:322
  22.4 1.2 %video_terms.1 = (f32[192,384]{1,0:T(8,128)S(1)}, bf16[192,384]{1,0:T(8,128)(2,1)S(1)}) custom-call(bf16[192,768]{1,0:T(8,128)(2,1)S(1)} %get-tuple-element.32.grad_hidden, bf16[3,384,768]{2,1,0:T(8,128)(2,1)S(1)} %get-tuple-element.26.w_time), custom_call_target="tpu_custom_call" | custom-call | flops 700000000 | bytes 2500000 | tf_op jit(solution)/shard_map/video_terms/pallas_call | solution.py:287
  23.6 1.9 %collective-permute-done.3 = bf16[2,2,2,2,2,4,48,128]{7,6,5,4,3,2,1,0:T(8,128)(2,1)S(1)} collective-permute-done((bf16[2,2,2,2,2,4,48,128]{7,6,5,4,3,2,1,0:T(8,128)(2,1)S(1)}, bf16[2,2,2,2,2,4,48,128]{7,6,5,4,3,2,1,0:T(8,128)(2,1)S(1)}, u32[]{:S(2)}, u32[]{:S(2)}) %collective-permute-start.3) | collective-permute-done | bytes 1572896 | tf_op jit(solution)/shard_map/ppermute | solution.py:322
  25.4 1.5 %pair_sum.1 = bf16[6144,128]{1,0:T(8,128)(2,1)} custom-call(bf16[6144,128]{1,0:T(8,128)(2,1)S(1)} %bitcast.11, bf16[6144,128]{1,0:T(8,128)(2,1)S(1)} %bitcast.12), custom_call_target="tpu_custom_call" | custom-call | tf_op jit(solution)/shard_map/pair_sum/pallas_call | solution.py:211
  27.0 13.1 %all-to-all-start = ((bf16[8,768,128]{2,1,0:T(8,128)(2,1)}), bf16[8,768,128]{2,1,0:T(8,128)(2,1)S(1)}, u32[]{:S(2)}, u32[]{:S(2)}) async-start(bf16[8,768,128]{2,1,0:T(8,128)(2,1)} %bitcast.6), calls=%async_computation | async-start | bytes 3145728 | tf_op jit(solution)/shard_map/all_to_all | solution.py:307
  40.1 1.3 %collective-permute-start.4 = (bf16[192,384]{1,0:T(8,128)(2,1)S(1)}, bf16[192,384]{1,0:T(8,128)(2,1)S(1)}, u32[]{:S(2)}, u32[]{:S(2)}) collective-permute-start(bf16[192,384]{1,0:T(8,128)(2,1)S(1)} %get-tuple-element.40), channel_id=1, source_target_pairs={{64,0},{128,64},{192,128},{256,192},{320,256},{384,320},{448,384},... | collective-permute-start | bytes 442376 | tf_op jit(solution)/shard_map/ppermute | solution.py:358
  41.4 6.6 %collective-permute-done.4.refs_2_ = bf16[192,384]{1,0:T(8,128)(2,1)S(1)} collective-permute-done((bf16[192,384]{1,0:T(8,128)(2,1)S(1)}, bf16[192,384]{1,0:T(8,128)(2,1)S(1)}, u32[]{:S(2)}, u32[]{:S(2)}) %collective-permute-start.4) | collective-permute-done | bytes 147488 | tf_op jit(solution)/shard_map/ppermute | solution.py:358
  48.0 8.6 %all-to-all-done.refs_0_ = bf16[8,768,128]{2,1,0:T(8,128)(2,1)S(1)} async-done(((bf16[8,768,128]{2,1,0:T(8,128)(2,1)}), bf16[8,768,128]{2,1,0:T(8,128)(2,1)S(1)}, u32[]{:S(2)}, u32[]{:S(2)}) %all-to-all-start) | async-done | bytes 1572896 | tf_op jit(solution)/shard_map/all_to_all | solution.py:307
  56.6 0.2 group_sum.2
  56.8 15.3 %all_to_all.15.refs_0_ = bf16[16,48,128]{2,1,0:T(8,128)(2,1)S(1)} all-to-all(bf16[16,48,128]{2,1,0:T(8,128)(2,1)S(1)} %bitcast.13), channel_id=1, replica_groups={{0,4,8,12,128,132,136,140,32,36,40,44,160,164,168,172},{2,6,10,14,130,1..., dimensions={0} | all-to-all | bytes 393216 | tf_op jit(solution)/shard_map/all_to_all | solution.py:307
  72.1 18.4 %all_to_all.16.refs_0_ = bf16[16,48,128]{2,1,0:T(8,128)(2,1)S(1)} all-to-all(bf16[16,48,128]{2,1,0:T(8,128)(2,1)S(1)} %group_sum.3), channel_id=1, replica_groups=mesh['chain'=8,'rows'=32,'clip'=2] {'chain','clip'}, dimensions={0} | all-to-all | bytes 393216 | tf_op jit(solution)/shard_map/all_to_all | solution.py:307
  90.5 0.9 unpack.1
  (1 shorter events, 0.0 us)
Async XLA Ops:
  1.7 12.3 %collective-permute-start.1 = (bf16[4,1,96,192]{3,2,1,0:T(8,128)(2,1)S(1)}, bf16[4,1,96,192]{3,2,1,0:T(8,128)(2,1)S(1)}, u32[]{:S(2)}, u32[]{:S(2)}) collective-permute-start(bf16[4,1,96,192]{3,2,1,0:T(8,128)(2,1)S(1)} %get-tuple-element.48), channel_id=1, source_target_pairs={{0,2},{2,4},{4,6},{6,8},{8,10},{10,12},{12,14},{14,16},{16,18},{18... | collective-permute-start | bytes 442376 | tf_op jit(solution)/shard_map/ppermute | solution.py:315
  6.5 7.4 %collective-permute-start.2 = (bf16[4,1,96,192]{3,2,1,0:T(8,128)(2,1)S(1)}, bf16[4,1,96,192]{3,2,1,0:T(8,128)(2,1)S(1)}, u32[]{:S(2)}, u32[]{:S(2)}) collective-permute-start(bf16[4,1,96,192]{3,2,1,0:T(8,128)(2,1)S(1)} %get-tuple-element.47), channel_id=1, source_target_pairs={{2,0},{4,2},{6,4},{8,6},{10,8},{12,10},{14,12},{16,14},{18,16},{20... | collective-permute-start | bytes 442376 | tf_op jit(solution)/shard_map/ppermute | solution.py:316
  7.8 7.0 %collective-permute-start = (bf16[192,384]{1,0:T(8,128)(2,1)}, bf16[192,384]{1,0:T(8,128)(2,1)S(1)}, u32[]{:S(2)}, u32[]{:S(2)}) collective-permute-start(bf16[192,384]{1,0:T(8,128)(2,1)} %bitcast.17), channel_id=1, source_target_pairs={{0,64},{64,128},{128,192},{192,256},{256,320},{320,384},{384,448},... | collective-permute-start | bytes 442376 | tf_op jit(solution)/shard_map/ppermute | solution.py:317
  17.0 8.4 %collective-permute-start.3 = (bf16[2,2,2,2,2,4,48,128]{7,6,5,4,3,2,1,0:T(8,128)(2,1)S(1)}, bf16[2,2,2,2,2,4,48,128]{7,6,5,4,3,2,1,0:T(8,128)(2,1)S(1)}, u32[]{:S(2)}, u32[]{:S(2)}) collective-permute-start(bf16[2,2,2,2,2,4,48,128]{7,6,5,4,3,2,1,0:T(8,128)(2,1)S(1)} %get-tuple-element.35), channel_id=1, source_target_pairs={{0,1},{1,0},{2,3},{3,2},{4,5},{5,4},{6,7},{7,6},{8,9},{9,8},{10,11... | collective-permute-start | bytes 4718600 | tf_op jit(solution)/shard_map/ppermute | solution.py:322
  27.0 29.6 %all-to-all-start = ((bf16[8,768,128]{2,1,0:T(8,128)(2,1)}), bf16[8,768,128]{2,1,0:T(8,128)(2,1)S(1)}, u32[]{:S(2)}, u32[]{:S(2)}) async-start(bf16[8,768,128]{2,1,0:T(8,128)(2,1)} %bitcast.6), calls=%async_computation | async-start | bytes 3145728 | tf_op jit(solution)/shard_map/all_to_all | solution.py:307
  40.1 7.9 %collective-permute-start.4 = (bf16[192,384]{1,0:T(8,128)(2,1)S(1)}, bf16[192,384]{1,0:T(8,128)(2,1)S(1)}, u32[]{:S(2)}, u32[]{:S(2)}) collective-permute-start(bf16[192,384]{1,0:T(8,128)(2,1)S(1)} %get-tuple-element.40), channel_id=1, source_target_pairs={{64,0},{128,64},{192,128},{256,192},{320,256},{384,320},{448,384},... | collective-permute-start | bytes 442376 | tf_op jit(solution)/shard_map/ppermute | solution.py:358

commit v11 on v8

--- a/solution.py
+++ b/solution.py
@@ -14,6 +14,7 @@
 LANES = 128
 PIECE, LINES = 48, 384
 TIME_ROWS, SPACE_ROWS = 36, 108
+SPLIT = 12
 
 
 def dot(a, b):
@@ -133,13 +134,17 @@
     )(cot, low, high, w_space, grad)
 
 
-def block_kernel(
-    video, carried, w_time, inner, outer, grad_hidden, hidden_in,
-    keep, send,
-    ext, hid, time_acc, space_acc,
-):
-    ext[0 : FRAMES * CELLS] = carried[...]
-    ext[FRAMES * CELLS :] = video[...]
+def time_half(ext, grad_hidden, out, time_acc):
+    for k in range(3):
+        time_acc[k * CH_IN : (k + 1) * CH_IN] = dot_t(ext[k * CELLS : (k + FRAMES) * CELLS], grad_hidden[...])
+    for r in range(N_X * N_Z):
+        t0 = r * TIME_ROWS
+        lines = [time_acc[t0 : t0 + TIME_ROWS, j * LANES : (j + 1) * LANES] for j in range(5)]
+        lines.append(time_acc[t0 : t0 + SPLIT, 5 * LANES :])
+        put_lines(out, r, lines)
+
+
+def space_half(ext, carried, w_time, inner, outer, grad_hidden, hidden_in, out, hid, time_acc, space_acc):
     first = hidden_in[:CELLS] + dot(carried[:CELLS], w_time[0]) + dot(carried[CELLS:], w_time[1])
     second = hidden_in[CELLS:] + dot(carried[CELLS:], w_time[0])
     for t, hidden in enumerate((first, second)):
@@ -149,9 +154,10 @@
                 hid[start : start + COLS] = hidden[
                     p * COLS : (p + 1) * COLS, j * CH_IN : (j + 1) * CH_IN
                 ].astype(BF16)
-
     for k in range(3):
-        time_acc[k * CH_IN : (k + 1) * CH_IN] = dot_t(ext[k * CELLS : (k + FRAMES) * CELLS], grad_hidden[...])
+        time_acc[k * CH_IN : (k + 1) * CH_IN, 5 * LANES :] = dot_t(
+            ext[k * CELLS : (k + FRAMES) * CELLS], grad_hidden[:, 5 * LANES :]
+        )
     hid_t = [hid[p * HALF : (p + 1) * HALF].T for p in range(BAND)]
     where = {key: (z, 3 * i) for z, order in ((inner, INNER), (outer, OUTER)) for i, key in enumerate(order)}
     for a in range(3):
@@ -162,36 +168,52 @@
                 total = total + dot(hid_t[p], z[row + c])
             tap = 3 * a + c
             space_acc[tap * CH_IN : (tap + 1) * CH_IN] = total
-
-    mine = lax.axis_index("clip") == 0
     half = SPACE_ROWS // 2
     for r in range(N_X * N_Z):
-        xh, xl, zh, zl = r // N_Z // 2, r // N_Z % 2, r % N_Z // 2, r % 2
         t0, s0 = r * TIME_ROWS, r * SPACE_ROWS
-        lines = [time_acc[t0 : t0 + TIME_ROWS, j * LANES : (j + 1) * LANES] for j in range(6)]
-        lines.append(space_acc[s0 : s0 + SPACE_ROWS, 0:LANES])
         rest = [space_acc[s0 + i * half : s0 + (i + 1) * half, LANES:CH_OUT] for i in range(2)]
-        lines.append(jnp.concatenate(rest, axis=1))
-        lines.append(jnp.zeros((6, LANES), F32))
-        lines = jnp.concatenate(lines, axis=0).astype(BF16)
-        upper, lower = lines[: LINES // 2], lines[LINES // 2 :]
-        mine_half, other_half = jnp.where(mine, upper, lower), jnp.where(mine, lower, upper)
-        for c0 in range(2):
-            for c1 in range(2):
-                piece = (c0 * 2 + c1) * PIECE
-                keep[xl, zl, c0, xh, c1, zh] = mine_half[piece : piece + PIECE]
-                send[xl, zl, c0, xh, c1, zh] = other_half[piece : piece + PIECE]
-
-
-def block_terms(video, carried, w_time, inner, outer, grad_hidden, hidden):
+        lines = [
+            time_acc[t0 + SPLIT : t0 + TIME_ROWS, 5 * LANES :],
+            space_acc[s0 : s0 + SPACE_ROWS, 0:LANES],
+            jnp.concatenate(rest, axis=1),
+            jnp.zeros((6, LANES), F32),
+        ]
+        put_lines(out, r, lines)
+
+
+def put_lines(out, r, lines):
+    xh, xl, zh, zl = r // N_Z // 2, r // N_Z % 2, r % N_Z // 2, r % 2
+    lines = jnp.concatenate(lines, axis=0).astype(BF16)
+    for c0 in range(2):
+        for c1 in range(2):
+            piece = (c0 * 2 + c1) * PIECE
+            out[xl, zl, c0, xh, c1, zh] = lines[piece : piece + PIECE]
+
+
+def half_kernel(
+    flip, video, carried, w_time, inner, outer, grad_hidden, hidden_in, out, ext, hid, time_acc, space_acc
+):
+    ext[0 : FRAMES * CELLS] = carried[...]
+    ext[FRAMES * CELLS :] = video[...]
+    first = lax.axis_index("clip") == flip
+
+    @pl.when(first)
+    def _():
+        time_half(ext, grad_hidden, out, time_acc)
+
+    @pl.when(jnp.logical_not(first))
+    def _():
+        space_half(ext, carried, w_time, inner, outer, grad_hidden, hidden_in, out, hid, time_acc, space_acc)
+
+
+def half_terms(flip, video, carried, w_time, inner, outer, grad_hidden, hidden):
     cells = FRAMES * CELLS
-    half = jax.ShapeDtypeStruct((2, 2, 2, N_X // 2, 2, N_Z // 2, PIECE, LANES), BF16)
-    return pl.pallas_call(
-        block_kernel,
-        name="block_terms",
-        out_shape=(half, half),
+    return pl.pallas_call(
+        lambda *refs: half_kernel(flip, *refs),
+        name="send_terms" if flip else "keep_terms",
+        out_shape=jax.ShapeDtypeStruct((2, 2, 2, N_X // 2, 2, N_Z // 2, PIECE, LANES), BF16),
         in_specs=[VMEM] * 7,
-        out_specs=(VMEM,) * 2,
+        out_specs=VMEM,
         scratch_shapes=[
             pltpu.VMEM((2 * cells, CH_IN), BF16),
             pltpu.VMEM((2 * cells, CH_IN), BF16),
@@ -199,7 +221,7 @@
             pltpu.VMEM((9 * CH_IN, CH_OUT), F32),
         ],
         compiler_params=params(20),
-        cost_estimate=pl.CostEstimate(flops=3_000_000_000, bytes_accessed=12_000_000, transcendentals=0),
+        cost_estimate=pl.CostEstimate(flops=1_500_000_000, bytes_accessed=6_000_000, transcendentals=0),
     )(video, carried, w_time, inner, outer, grad_hidden, hidden)
 
 
@@ -318,10 +340,12 @@
     operands = [pltpu.with_memory_space_constraint(value, pltpu.HBM) for value in (cot, own, w_time, w_space)]
     cot, own, w_time, w_space, inner, grad, hidden = inner_terms(*operands)
     grad_hidden, outer = grad_terms(cot, low, high, w_space, grad)
-    keep, send = block_terms(own, carried, w_time, inner, outer, grad_hidden, hidden)
+    terms = (own, carried, w_time, inner, outer, grad_hidden, hidden)
+    send = half_terms(1, *terms)
     received = lax.ppermute(send, "clip", [(0, 1), (1, 0)])
+    keep = half_terms(0, *terms)
     ours, returned = video_terms(grad_hidden, w_time)
-    received, ours = lax.optimization_barrier((received, ours))
+    received, ours, keep = lax.optimization_barrier((received, ours, keep))
 
     def device(c, x, z):
         return c * rows + x * N_Z + z

time: 91.1 us -> 91 us (level)
  waiting for transfers between devices: 15 us -> 13.3 us
  starting transfers between devices: 19.5 us -> 20.7 us
    ppermute x1, waiting for transfers between devices: 1.85 us -> 0.01 us  [local(): received = lax.ppermute(send, 'clip', [(0, 1), (1, 0)])]
    ppermute x1, starting transfers between devices: 5.37 us -> 6.53 us  [local(): received = lax.ppermute(send, 'clip', [(0, 1), (1, 0)])]
    pallas_call x1 -> x2, Pallas kernels: 2.19 us -> 2.74 us  [half_terms(): pl.pallas_call(lambda *refs: half_kernel(flip, *refs), name='send_terms'...]
  transfers between devices with their start and end apart: 6 -> 6, of which waited for: 3 -> 2; matrix products, arithmetic and copies ran while one was open for 0% -> 0% of each run, Pallas kernels for 5% -> 8%
where the time goes in v11:
time: 91 us; the launch traced here: 90.5 us
  blocking collectives  45 us (49%)
  starting transfers between devices  20.7 us (23%)
  waiting for transfers between devices  13.3 us (15%)
  Pallas kernels  9.78 us (11%)
  local copies, waits for them, and re-layouts  1.05 us (1%)
    all_to_all x2, blocking collectives, exchange(): lax.all_to_all(parts, axes, 0, 0, tiled=True, axis_index_groups=groups)  45 us
    ppermute x1, waiting for transfers between devices, local(): following = lax.ppermute(returned, 'chain', along('chain', -1))  7.7 us
    ppermute x1, starting transfers between devices, local(): received = lax.ppermute(send, 'clip', [(0, 1), (1, 0)])  6.53 us
    all_to_all x1, waiting for transfers between devices, exchange(): lax.all_to_all(parts, axes, 0, 0, tiled=True, axis_index_groups=groups)  5.56 us
    ppermute x1, starting transfers between devices, local(): low = lax.ppermute(cot[:, 2 * BAND - 1:], 'rows', along('rows', 1))  4.84 us
    all_to_all x1, starting transfers between devices, exchange(): lax.all_to_all(parts, axes, 0, 0, tiled=True, axis_index_groups=groups)  3.52 us
    ppermute x1, starting transfers between devices, local(): carried = lax.ppermute(own, 'chain', along('chain', 1))  3.21 us
    pallas_call x1, Pallas kernels, inner_terms(): pl.pallas_call(inner_kernel, name='inner_terms', out_shape=(*(jax.ShapeDt...  2.9 us
  transfers between devices with their start and end apart: 6, of which 2 were waited for; matrix products, arithmetic and copies ran while one was open for 0% of the time, Pallas kernels for 8%

profile of v11, /device:TPU:1, one launch (start us, length us, event | category | flops | bytes accessed | tf_op | source)
XLA Modules:
  0.0 90.5 jit_solution(10745063860797524443)
XLA Ops:
  0.6 1.1 %fusion = (bf16[4,1,96,192]{3,2,1,0:T(8,128)(2,1)S(1)}, bf16[4,1,96,192]{3,2,1,0:T(8,128)(2,1)S(1)}) fusion(bf16[4,4,96,192]{3,2,1,0:T(8,128)(2,1)} %bitcast.14), kind=kLoop, calls=%fused_computation | loop fusion | bytes 589824 | tf_op jit(solution)/shard_map/slice | solution.py:338
  1.7 4.8 %collective-permute-start.1 = (bf16[4,1,96,192]{3,2,1,0:T(8,128)(2,1)S(1)}, bf16[4,1,96,192]{3,2,1,0:T(8,128)(2,1)S(1)}, u32[]{:S(2)}, u32[]{:S(2)}) collective-permute-start(bf16[4,1,96,192]{3,2,1,0:T(8,128)(2,1)S(1)} %get-tuple-element.46), channel_id=1, source_target_pairs={{0,2},{2,4},{4,6},{6,8},{8,10},{10,12},{12,14},{14,16},{16,18},{18... | collective-permute-start | bytes 442376 | tf_op jit(solution)/shard_map/ppermute | solution.py:337
  6.5 1.3 %collective-permute-start.2 = (bf16[4,1,96,192]{3,2,1,0:T(8,128)(2,1)S(1)}, bf16[4,1,96,192]{3,2,1,0:T(8,128)(2,1)S(1)}, u32[]{:S(2)}, u32[]{:S(2)}) collective-permute-start(bf16[4,1,96,192]{3,2,1,0:T(8,128)(2,1)S(1)} %get-tuple-element.45), channel_id=1, source_target_pairs={{2,0},{4,2},{6,4},{8,6},{10,8},{12,10},{14,12},{16,14},{18,16},{20... | collective-permute-start | bytes 442376 | tf_op jit(solution)/shard_map/ppermute | solution.py:338
  7.8 3.2 %collective-permute-start = (bf16[192,384]{1,0:T(8,128)(2,1)}, bf16[192,384]{1,0:T(8,128)(2,1)S(1)}, u32[]{:S(2)}, u32[]{:S(2)}) collective-permute-start(bf16[192,384]{1,0:T(8,128)(2,1)} %bitcast.17), channel_id=1, source_target_pairs={{0,64},{64,128},{128,192},{192,256},{256,320},{320,384},{384,448},... | collective-permute-start | bytes 442376 | tf_op jit(solution)/shard_map/ppermute | solution.py:339
  11.1 2.9 %inner_terms.1 = (bf16[4,4,96,192]{3,2,1,0:T(8,128)(2,1)S(1)}, bf16[192,384]{1,0:T(8,128)(2,1)S(1)}, bf16[3,384,768]{2,1,0:T(8,128)(2,1)S(1)}, bf16[9,192,384]{2...) custom-call(bf16[4,4,96,192]{3,2,1,0:T(8,128)(2,1)} %bitcast.15, ...), custom_call_target="tpu_custom_call" | custom-call | flops 1500000000 | bytes 6000000 | tf_op jit(solution)/shard_map/inner_terms/pallas_call | solution.py:90
  14.0 0.0 collective-permute-done.1.low
  14.0 0.0 collective-permute-done.2.high
  14.0 0.8 grad_terms.1
  14.8 0.0 collective-permute-done.refs_1_
  14.8 0.8 send_terms.1
  15.6 6.5 %collective-permute-start.3 = (bf16[2,2,2,2,2,4,48,128]{7,6,5,4,3,2,1,0:T(8,128)(2,1)S(1)}, bf16[2,2,2,2,2,4,48,128]{7,6,5,4,3,2,1,0:T(8,128)(2,1)S(1)}, u32[]{:S(2)}, u32[]{:S(2)}) collective-permute-start(bf16[2,2,2,2,2,4,48,128]{7,6,5,4,3,2,1,0:T(8,128)(2,1)S(1)} %send_terms.1), channel_id=1, source_target_pairs={{0,1},{1,0},{2,3},{3,2},{4,5},{5,4},{6,7},{7,6},{8,9},{9,8},{10,11... | collective-permute-start | bytes 4718600 | tf_op jit(solution)/shard_map/ppermute | solution.py:345
  22.2 1.2 %video_terms.1 = (f32[192,384]{1,0:T(8,128)S(1)}, bf16[192,384]{1,0:T(8,128)(2,1)S(1)}) custom-call(bf16[192,768]{1,0:T(8,128)(2,1)S(1)} %get-tuple-element.31.refs_5_.grad_hidden, bf16[3,384,768]{2,1,0:T(8,128)(2,1)S(1)} %get-tuple-element.25.refs_2_.w_time), custom_call_target="tpu_custom_call" | custom-call | flops 700000000 | bytes 2500000 | tf_op jit(solution)/shard_map/video_terms/pallas_call | solution.py:309
  23.3 2.0 %keep_terms.1 = bf16[2,2,2,2,2,4,48,128]{7,6,5,4,3,2,1,0:T(8,128)(2,1)S(1)} custom-call(bf16[192,384]{1,0:T(8,128)(2,1)S(1)} %get-tuple-element.24.refs_0_, bf16[192,384]{1,0:T(8,128)(2,1)S(1)} %collective-permute-done.refs_1_, bf16[3,384,768]{2,1,0:T(8,128)(2,1)S(1)} %get-tuple-element.25.refs_2_.w_time, ...), custom_call_target="tpu_custom_call" | custom-call | flops 1500000000 | bytes 6000000 | tf_op jit(solution)/shard_map/keep_terms/pallas_call | solution.py:211
  25.3 0.0 collective-permute-done.3
  25.3 0.4 pair_sum.1
  25.7 29.4 %all_to_all.15.refs_0_ = bf16[8,768,128]{2,1,0:T(8,128)(2,1)S(1)} all-to-all(bf16[8,768,128]{2,1,0:T(8,128)(2,1)S(1)} %bitcast.11), channel_id=1, replica_groups={{0,64,2,66,16,80,18,82},{4,68,6,70,20,84,22,86},{8,72,10,74,24,88,26,90..., dimensions={0} | all-to-all | bytes 3145728 | tf_op jit(solution)/shard_map/all_to_all | solution.py:329
  55.1 0.9 group_sum.2
  56.0 3.5 %all-to-all-start.1 = ((bf16[16,48,128]{2,1,0:T(8,128)(2,1)}), bf16[16,48,128]{2,1,0:T(8,128)(2,1)S(1)}, u32[]{:S(2)}, u32[]{:S(2)}) async-start(bf16[16,48,128]{2,1,0:T(8,128)(2,1)} %bitcast.7), calls=%async_computation.1 | async-start | bytes 393216 | tf_op jit(solution)/shard_map/all_to_all | solution.py:329
  59.5 1.3 %collective-permute-start.4 = (bf16[192,384]{1,0:T(8,128)(2,1)S(1)}, bf16[192,384]{1,0:T(8,128)(2,1)S(1)}, u32[]{:S(2)}, u32[]{:S(2)}) collective-permute-start(bf16[192,384]{1,0:T(8,128)(2,1)S(1)} %get-tuple-element.38), channel_id=1, source_target_pairs={{64,0},{128,64},{192,128},{256,192},{320,256},{384,320},{448,384},... | collective-permute-start | bytes 442376 | tf_op jit(solution)/shard_map/ppermute | solution.py:383
  60.8 7.7 %collective-permute-done.4.refs_2_ = bf16[192,384]{1,0:T(8,128)(2,1)S(1)} collective-permute-done((bf16[192,384]{1,0:T(8,128)(2,1)S(1)}, bf16[192,384]{1,0:T(8,128)(2,1)S(1)}, u32[]{:S(2)}, u32[]{:S(2)}) %collective-permute-start.4) | collective-permute-done | bytes 147488 | tf_op jit(solution)/shard_map/ppermute | solution.py:383
  68.5 5.6 %all-to-all-done.1.refs_0_ = bf16[16,48,128]{2,1,0:T(8,128)(2,1)S(1)} async-done(((bf16[16,48,128]{2,1,0:T(8,128)(2,1)}), bf16[16,48,128]{2,1,0:T(8,128)(2,1)S(1)}, u32[]{:S(2)}, u32[]{:S(2)}) %all-to-all-start.1) | async-done | bytes 196640 | tf_op jit(solution)/shard_map/all_to_all | solution.py:329
  74.1 15.6 %all_to_all.16.refs_0_ = bf16[16,48,128]{2,1,0:T(8,128)(2,1)S(1)} all-to-all(bf16[16,48,128]{2,1,0:T(8,128)(2,1)S(1)} %group_sum.3), channel_id=1, replica_groups=mesh['chain'=8,'rows'=32,'clip'=2] {'chain','clip'}, dimensions={0} | all-to-all | bytes 393216 | tf_op jit(solution)/shard_map/all_to_all | solution.py:329
  89.7 0.9 unpack.1
  (1 shorter events, 0.0 us)
Async XLA Ops:
  1.7 12.3 %collective-permute-start.1 = (bf16[4,1,96,192]{3,2,1,0:T(8,128)(2,1)S(1)}, bf16[4,1,96,192]{3,2,1,0:T(8,128)(2,1)S(1)}, u32[]{:S(2)}, u32[]{:S(2)}) collective-permute-start(bf16[4,1,96,192]{3,2,1,0:T(8,128)(2,1)S(1)} %get-tuple-element.46), channel_id=1, source_target_pairs={{0,2},{2,4},{4,6},{6,8},{8,10},{10,12},{12,14},{14,16},{16,18},{18... | collective-permute-start | bytes 442376 | tf_op jit(solution)/shard_map/ppermute | solution.py:337
  6.5 7.4 %collective-permute-start.2 = (bf16[4,1,96,192]{3,2,1,0:T(8,128)(2,1)S(1)}, bf16[4,1,96,192]{3,2,1,0:T(8,128)(2,1)S(1)}, u32[]{:S(2)}, u32[]{:S(2)}) collective-permute-start(bf16[4,1,96,192]{3,2,1,0:T(8,128)(2,1)S(1)} %get-tuple-element.45), channel_id=1, source_target_pairs={{2,0},{4,2},{6,4},{8,6},{10,8},{12,10},{14,12},{16,14},{18,16},{20... | collective-permute-start | bytes 442376 | tf_op jit(solution)/shard_map/ppermute | solution.py:338
  7.8 7.0 %collective-permute-start = (bf16[192,384]{1,0:T(8,128)(2,1)}, bf16[192,384]{1,0:T(8,128)(2,1)S(1)}, u32[]{:S(2)}, u32[]{:S(2)}) collective-permute-start(bf16[192,384]{1,0:T(8,128)(2,1)} %bitcast.17), channel_id=1, source_target_pairs={{0,64},{64,128},{128,192},{192,256},{256,320},{320,384},{384,448},... | collective-permute-start | bytes 442376 | tf_op jit(solution)/shard_map/ppermute | solution.py:339
  15.6 9.7 %collective-permute-start.3 = (bf16[2,2,2,2,2,4,48,128]{7,6,5,4,3,2,1,0:T(8,128)(2,1)S(1)}, bf16[2,2,2,2,2,4,48,128]{7,6,5,4,3,2,1,0:T(8,128)(2,1)S(1)}, u32[]{:S(2)}, u32[]{:S(2)}) collective-permute-start(bf16[2,2,2,2,2,4,48,128]{7,6,5,4,3,2,1,0:T(8,128)(2,1)S(1)} %send_terms.1), channel_id=1, source_target_pairs={{0,1},{1,0},{2,3},{3,2},{4,5},{5,4},{6,7},{7,6},{8,9},{9,8},{10,11... | collective-permute-start | bytes 4718600 | tf_op jit(solution)/shard_map/ppermute | solution.py:345
  56.0 18.1 %all-to-all-start.1 = ((bf16[16,48,128]{2,1,0:T(8,128)(2,1)}), bf16[16,48,128]{2,1,0:T(8,128)(2,1)S(1)}, u32[]{:S(2)}, u32[]{:S(2)}) async-start(bf16[16,48,128]{2,1,0:T(8,128)(2,1)} %bitcast.7), calls=%async_computation.1 | async-start | bytes 393216 | tf_op jit(solution)/shard_map/all_to_all | solution.py:329
  59.5 9.0 %collective-permute-start.4 = (bf16[192,384]{1,0:T(8,128)(2,1)S(1)}, bf16[192,384]{1,0:T(8,128)(2,1)S(1)}, u32[]{:S(2)}, u32[]{:S(2)}) collective-permute-start(bf16[192,384]{1,0:T(8,128)(2,1)S(1)} %get-tuple-element.38), channel_id=1, source_target_pairs={{64,0},{128,64},{192,128},{256,192},{320,256},{384,320},{448,384},... | collective-permute-start | bytes 442376 | tf_op jit(solution)/shard_map/ppermute | solution.py:383

commit v12 on v8

--- a/solution.py
+++ b/solution.py
@@ -62,26 +62,30 @@
 
 
 def inner_kernel(cot_in, video_in, w_time_in, w_space_in, cot, video, w_time, w_space, inner, grad, hidden, sems):
-    copies = [
-        pltpu.make_async_copy(source, target, sems.at[i])
-        for i, (source, target) in enumerate(
-            ((cot_in, cot), (w_space_in, w_space), (video_in, video), (w_time_in, w_time))
-        )
-    ]
+    pieces = [(cot_in.at[s], cot.at[s]) for s in range(2 * FRAMES)]
+    pieces += [(w_space_in.at[pl.ds(3 * a, 3)], w_space.at[pl.ds(3 * a, 3)]) for a in (1, 0, 2)]
+    pieces += [(video_in, video), (w_time_in.at[pl.ds(1, 2)], w_time.at[pl.ds(1, 2)]), (w_time_in.at[0], w_time.at[0])]
+    copies = [pltpu.make_async_copy(source, target, sems.at[i]) for i, (source, target) in enumerate(pieces)]
     for copy in copies:
         copy.start()
     pick = picker()
-    copies[0].wait()
     for s in range(2 * FRAMES):
+        copies[s].wait()
         reach = [dot(pick, cot[s, p]) for p in range(2 * BAND)]
         for i, (p, a) in enumerate(INNER):
             put(inner, 3 * i, s, (reach[2 * p + 1 - a] + reach[2 * p + 2 - a]).astype(BF16))
-    copies[1].wait()
-    grad[...] = jnp.concatenate(taps(inner, INNER, w_space))
-    copies[2].wait()
-    copies[3].wait()
+    sums = [0.0, 0.0]
+    for i, (p, a) in enumerate(INNER):
+        if i != 1:
+            copies[2 * FRAMES + max(i - 1, 0)].wait()
+        for c in range(3):
+            sums[p] = sums[p] + dot(inner[3 * i + c], w_space[3 * a + c])
+    grad[...] = jnp.concatenate(sums)
+    for copy in copies[2 * FRAMES + 3 : -1]:
+        copy.wait()
     hidden[:CELLS] = dot(video[:CELLS], w_time[2])
     hidden[CELLS:] = dot(video[:CELLS], w_time[1]) + dot(video[CELLS:], w_time[2])
+    copies[-1].wait()
 
 
 def inner_terms(cot, video, w_time, w_space):
@@ -97,7 +101,7 @@
         ),
         in_specs=[pl.BlockSpec(memory_space=pltpu.HBM)] * 4,
         out_specs=(VMEM,) * 7,
-        scratch_shapes=[pltpu.SemaphoreType.DMA((4,))],
+        scratch_shapes=[pltpu.SemaphoreType.DMA((2 * FRAMES + 6,))],
         compiler_params=params(16),
         cost_estimate=pl.CostEstimate(flops=1_500_000_000, bytes_accessed=6_000_000, transcendentals=0),
     )(cot, video, w_time, w_space)

time: 91.1 us -> 91.1 us (level)
  waiting for transfers between devices: 15 us -> 12.2 us
  blocking collectives: 45.1 us -> 47.8 us
    all_to_all x2, blocking collectives: 45.1 us -> 47.8 us  [exchange(): lax.all_to_all(parts, axes, 0, 0, tiled=True, axis_index_groups=groups)]
    ppermute x1, waiting for transfers between devices: 7.43 us -> 6.03 us  [local(): following = lax.ppermute(returned, 'chain', along('chain', -1))]
    all_to_all x1, waiting for transfers between devices: 5.75 us -> 4.36 us  [exchange(): lax.all_to_all(parts, axes, 0, 0, tiled=True, axis_index_groups=groups)]
  transfers between devices with their start and end apart: 6 -> 6, of which waited for: 3 -> 3; matrix products, arithmetic and copies ran while one was open for 0% -> 0% of each run, Pallas kernels for 5% -> 6%
where the time goes in v12:
time: 91.1 us; the launch traced here: 90.6 us
  blocking collectives  47.8 us (52%)
  starting transfers between devices  19 us (21%)
  waiting for transfers between devices  12.2 us (13%)
  Pallas kernels  9.72 us (11%)
  local copies, waits for them, and re-layouts  1.05 us (1%)
    all_to_all x2, blocking collectives, exchange(): lax.all_to_all(parts, axes, 0, 0, tiled=True, axis_index_groups=groups)  47.8 us
    ppermute x1, waiting for transfers between devices, local(): following = lax.ppermute(returned, 'chain', along('chain', -1))  6.03 us
    ppermute x1, starting transfers between devices, local(): received = lax.ppermute(send, 'clip', [(0, 1), (1, 0)])  4.88 us
    ppermute x1, starting transfers between devices, local(): low = lax.ppermute(cot[:, 2 * BAND - 1:], 'rows', along('rows', 1))  4.84 us
    all_to_all x1, waiting for transfers between devices, exchange(): lax.all_to_all(parts, axes, 0, 0, tiled=True, axis_index_groups=groups)  4.36 us
    all_to_all x1, starting transfers between devices, exchange(): lax.all_to_all(parts, axes, 0, 0, tiled=True, axis_index_groups=groups)  3.52 us
    pallas_call x1, Pallas kernels, inner_terms(): pl.pallas_call(inner_kernel, name='inner_terms', out_shape=(*(jax.ShapeDt...  3.39 us
    ppermute x1, starting transfers between devices, local(): carried = lax.ppermute(own, 'chain', along('chain', 1))  3.21 us
  transfers between devices with their start and end apart: 6, of which 3 were waited for; matrix products, arithmetic and copies ran while one was open for 0% of the time, Pallas kernels for 6%

profile of v12, /device:TPU:1, one launch (start us, length us, event | category | flops | bytes accessed | tf_op | source)
XLA Modules:
  0.0 90.6 jit_solution(8584833822934020450)
XLA Ops:
  0.6 1.1 %fusion = (bf16[4,1,96,192]{3,2,1,0:T(8,128)(2,1)S(1)}, bf16[4,1,96,192]{3,2,1,0:T(8,128)(2,1)S(1)}) fusion(bf16[4,4,96,192]{3,2,1,0:T(8,128)(2,1)} %bitcast.14), kind=kLoop, calls=%fused_computation | loop fusion | bytes 589824 | tf_op jit(solution)/shard_map/slice | solution.py:320
  1.7 4.8 %collective-permute-start.1 = (bf16[4,1,96,192]{3,2,1,0:T(8,128)(2,1)S(1)}, bf16[4,1,96,192]{3,2,1,0:T(8,128)(2,1)S(1)}, u32[]{:S(2)}, u32[]{:S(2)}) collective-permute-start(bf16[4,1,96,192]{3,2,1,0:T(8,128)(2,1)S(1)} %get-tuple-element.48), channel_id=1, source_target_pairs={{0,2},{2,4},{4,6},{6,8},{8,10},{10,12},{12,14},{14,16},{16,18},{18... | collective-permute-start | bytes 442376 | tf_op jit(solution)/shard_map/ppermute | solution.py:319
  6.5 1.3 %collective-permute-start.2 = (bf16[4,1,96,192]{3,2,1,0:T(8,128)(2,1)S(1)}, bf16[4,1,96,192]{3,2,1,0:T(8,128)(2,1)S(1)}, u32[]{:S(2)}, u32[]{:S(2)}) collective-permute-start(bf16[4,1,96,192]{3,2,1,0:T(8,128)(2,1)S(1)} %get-tuple-element.47), channel_id=1, source_target_pairs={{2,0},{4,2},{6,4},{8,6},{10,8},{12,10},{14,12},{16,14},{18,16},{20... | collective-permute-start | bytes 442376 | tf_op jit(solution)/shard_map/ppermute | solution.py:320
  7.8 3.2 %collective-permute-start = (bf16[192,384]{1,0:T(8,128)(2,1)}, bf16[192,384]{1,0:T(8,128)(2,1)S(1)}, u32[]{:S(2)}, u32[]{:S(2)}) collective-permute-start(bf16[192,384]{1,0:T(8,128)(2,1)} %bitcast.17), channel_id=1, source_target_pairs={{0,64},{64,128},{128,192},{192,256},{256,320},{320,384},{384,448},... | collective-permute-start | bytes 442376 | tf_op jit(solution)/shard_map/ppermute | solution.py:321
  11.1 3.4 %inner_terms.1 = (bf16[4,4,96,192]{3,2,1,0:T(8,128)(2,1)S(1)}, bf16[192,384]{1,0:T(8,128)(2,1)S(1)}, bf16[3,384,768]{2,1,0:T(8,128)(2,1)S(1)}, bf16[9,192,384]{2...) custom-call(bf16[4,4,96,192]{3,2,1,0:T(8,128)(2,1)} %bitcast.15, ...), custom_call_target="tpu_custom_call" | custom-call | flops 1500000000 | bytes 6000000 | tf_op jit(solution)/shard_map/inner_terms/pallas_call | solution.py:93
  14.4 0.0 collective-permute-done.1.low
  14.5 0.0 collective-permute-done.2.high
  14.5 0.8 grad_terms.1
  15.3 0.0 collective-permute-done.carried
  15.3 2.2 %block_terms.1 = (bf16[2,2,2,2,2,4,48,128]{7,6,5,4,3,2,1,0:T(8,128)(2,1)S(1)}, bf16[2,2,2,2,2,4,48,128]{7,6,5,4,3,2,1,0:T(8,128)(2,1)S(1)}) custom-call(bf16[192,384]{1,0:T(8,128)(2,1)S(1)} %get-tuple-element.25.video, bf16[192,384]{1,0:T(8,128)(2,1)S(1)} %collective-permute-done.carried, bf16[3,384,768]{2,1,0:T(8,128)(2,1)S(1)} %get-tuple-element.26.w_time, ...), custom_call_target="tpu_custom_call" | custom-call | flops 3000000000 | bytes 12000000 | tf_op jit(solution)/shard_map/block_terms/pallas_call | solution.py:193
  17.5 4.9 %collective-permute-start.3 = (bf16[2,2,2,2,2,4,48,128]{7,6,5,4,3,2,1,0:T(8,128)(2,1)S(1)}, bf16[2,2,2,2,2,4,48,128]{7,6,5,4,3,2,1,0:T(8,128)(2,1)S(1)}, u32[]{:S(2)}, u32[]{:S(2)}) collective-permute-start(bf16[2,2,2,2,2,4,48,128]{7,6,5,4,3,2,1,0:T(8,128)(2,1)S(1)} %get-tuple-element.35), channel_id=1, source_target_pairs={{0,1},{1,0},{2,3},{3,2},{4,5},{5,4},{6,7},{7,6},{8,9},{9,8},{10,11... | collective-permute-start | bytes 4718600 | tf_op jit(solution)/shard_map/ppermute | solution.py:326
  22.4 1.2 %video_terms.1 = (f32[192,384]{1,0:T(8,128)S(1)}, bf16[192,384]{1,0:T(8,128)(2,1)S(1)}) custom-call(bf16[192,768]{1,0:T(8,128)(2,1)S(1)} %get-tuple-element.32.grad_hidden, bf16[3,384,768]{2,1,0:T(8,128)(2,1)S(1)} %get-tuple-element.26.w_time), custom_call_target="tpu_custom_call" | custom-call | flops 700000000 | bytes 2500000 | tf_op jit(solution)/shard_map/video_terms/pallas_call | solution.py:291
  23.6 1.9 %collective-permute-done.3 = bf16[2,2,2,2,2,4,48,128]{7,6,5,4,3,2,1,0:T(8,128)(2,1)S(1)} collective-permute-done((bf16[2,2,2,2,2,4,48,128]{7,6,5,4,3,2,1,0:T(8,128)(2,1)S(1)}, bf16[2,2,2,2,2,4,48,128]{7,6,5,4,3,2,1,0:T(8,128)(2,1)S(1)}, u32[]{:S(2)}, u32[]{:S(2)}) %collective-permute-start.3) | collective-permute-done | bytes 1572896 | tf_op jit(solution)/shard_map/ppermute | solution.py:326
  25.4 0.4 pair_sum.1
  25.8 29.4 %all_to_all.15.refs_0_ = bf16[8,768,128]{2,1,0:T(8,128)(2,1)S(1)} all-to-all(bf16[8,768,128]{2,1,0:T(8,128)(2,1)S(1)} %bitcast.11), channel_id=1, replica_groups={{0,64,2,66,16,80,18,82},{4,68,6,70,20,84,22,86},{8,72,10,74,24,88,26,90..., dimensions={0} | all-to-all | bytes 3145728 | tf_op jit(solution)/shard_map/all_to_all | solution.py:311
  55.2 0.9 group_sum.2
  56.1 3.5 %all-to-all-start.1 = ((bf16[16,48,128]{2,1,0:T(8,128)(2,1)}), bf16[16,48,128]{2,1,0:T(8,128)(2,1)S(1)}, u32[]{:S(2)}, u32[]{:S(2)}) async-start(bf16[16,48,128]{2,1,0:T(8,128)(2,1)} %bitcast.7), calls=%async_computation.1 | async-start | bytes 393216 | tf_op jit(solution)/shard_map/all_to_all | solution.py:311
  59.6 1.3 %collective-permute-start.4 = (bf16[192,384]{1,0:T(8,128)(2,1)S(1)}, bf16[192,384]{1,0:T(8,128)(2,1)S(1)}, u32[]{:S(2)}, u32[]{:S(2)}) collective-permute-start(bf16[192,384]{1,0:T(8,128)(2,1)S(1)} %get-tuple-element.40), channel_id=1, source_target_pairs={{64,0},{128,64},{192,128},{256,192},{320,256},{384,320},{448,384},... | collective-permute-start | bytes 442376 | tf_op jit(solution)/shard_map/ppermute | solution.py:363
  60.9 6.0 %collective-permute-done.4.refs_2_ = bf16[192,384]{1,0:T(8,128)(2,1)S(1)} collective-permute-done((bf16[192,384]{1,0:T(8,128)(2,1)S(1)}, bf16[192,384]{1,0:T(8,128)(2,1)S(1)}, u32[]{:S(2)}, u32[]{:S(2)}) %collective-permute-start.4) | collective-permute-done | bytes 147488 | tf_op jit(solution)/shard_map/ppermute | solution.py:363
  66.9 4.4 %all-to-all-done.1.refs_0_ = bf16[16,48,128]{2,1,0:T(8,128)(2,1)S(1)} async-done(((bf16[16,48,128]{2,1,0:T(8,128)(2,1)}), bf16[16,48,128]{2,1,0:T(8,128)(2,1)S(1)}, u32[]{:S(2)}, u32[]{:S(2)}) %all-to-all-start.1) | async-done | bytes 196640 | tf_op jit(solution)/shard_map/all_to_all | solution.py:311
  71.3 18.4 %all_to_all.16.refs_0_ = bf16[16,48,128]{2,1,0:T(8,128)(2,1)S(1)} all-to-all(bf16[16,48,128]{2,1,0:T(8,128)(2,1)S(1)} %group_sum.3), channel_id=1, replica_groups=mesh['chain'=8,'rows'=32,'clip'=2] {'chain','clip'}, dimensions={0} | all-to-all | bytes 393216 | tf_op jit(solution)/shard_map/all_to_all | solution.py:311
  89.8 0.9 unpack.1
  (1 shorter events, 0.0 us)
Async XLA Ops:
  1.7 12.8 %collective-permute-start.1 = (bf16[4,1,96,192]{3,2,1,0:T(8,128)(2,1)S(1)}, bf16[4,1,96,192]{3,2,1,0:T(8,128)(2,1)S(1)}, u32[]{:S(2)}, u32[]{:S(2)}) collective-permute-start(bf16[4,1,96,192]{3,2,1,0:T(8,128)(2,1)S(1)} %get-tuple-element.48), channel_id=1, source_target_pairs={{0,2},{2,4},{4,6},{6,8},{8,10},{10,12},{12,14},{14,16},{16,18},{18... | collective-permute-start | bytes 442376 | tf_op jit(solution)/shard_map/ppermute | solution.py:319
  6.5 7.9 %collective-permute-start.2 = (bf16[4,1,96,192]{3,2,1,0:T(8,128)(2,1)S(1)}, bf16[4,1,96,192]{3,2,1,0:T(8,128)(2,1)S(1)}, u32[]{:S(2)}, u32[]{:S(2)}) collective-permute-start(bf16[4,1,96,192]{3,2,1,0:T(8,128)(2,1)S(1)} %get-tuple-element.47), channel_id=1, source_target_pairs={{2,0},{4,2},{6,4},{8,6},{10,8},{12,10},{14,12},{16,14},{18,16},{20... | collective-permute-start | bytes 442376 | tf_op jit(solution)/shard_map/ppermute | solution.py:320
  7.8 7.5 %collective-permute-start = (bf16[192,384]{1,0:T(8,128)(2,1)}, bf16[192,384]{1,0:T(8,128)(2,1)S(1)}, u32[]{:S(2)}, u32[]{:S(2)}) collective-permute-start(bf16[192,384]{1,0:T(8,128)(2,1)} %bitcast.17), channel_id=1, source_target_pairs={{0,64},{64,128},{128,192},{192,256},{256,320},{320,384},{384,448},... | collective-permute-start | bytes 442376 | tf_op jit(solution)/shard_map/ppermute | solution.py:321
  17.5 7.9 %collective-permute-start.3 = (bf16[2,2,2,2,2,4,48,128]{7,6,5,4,3,2,1,0:T(8,128)(2,1)S(1)}, bf16[2,2,2,2,2,4,48,128]{7,6,5,4,3,2,1,0:T(8,128)(2,1)S(1)}, u32[]{:S(2)}, u32[]{:S(2)}) collective-permute-start(bf16[2,2,2,2,2,4,48,128]{7,6,5,4,3,2,1,0:T(8,128)(2,1)S(1)} %get-tuple-element.35), channel_id=1, source_target_pairs={{0,1},{1,0},{2,3},{3,2},{4,5},{5,4},{6,7},{7,6},{8,9},{9,8},{10,11... | collective-permute-start | bytes 4718600 | tf_op jit(solution)/shard_map/ppermute | solution.py:326
  56.1 15.2 %all-to-all-start.1 = ((bf16[16,48,128]{2,1,0:T(8,128)(2,1)}), bf16[16,48,128]{2,1,0:T(8,128)(2,1)S(1)}, u32[]{:S(2)}, u32[]{:S(2)}) async-start(bf16[16,48,128]{2,1,0:T(8,128)(2,1)} %bitcast.7), calls=%async_computation.1 | async-start | bytes 393216 | tf_op jit(solution)/shard_map/all_to_all | solution.py:311
  59.6 7.3 %collective-permute-start.4 = (bf16[192,384]{1,0:T(8,128)(2,1)S(1)}, bf16[192,384]{1,0:T(8,128)(2,1)S(1)}, u32[]{:S(2)}, u32[]{:S(2)}) collective-permute-start(bf16[192,384]{1,0:T(8,128)(2,1)S(1)} %get-tuple-element.40), channel_id=1, source_target_pairs={{64,0},{128,64},{192,128},{256,192},{320,256},{384,320},{448,384},... | collective-permute-start | bytes 442376 | tf_op jit(solution)/shard_map/ppermute | solution.py:363
